TPU v7x, 128 devices: a whole 4x4x4 slice. The times are simulated.
128 devices in a mesh: ctx: 16 (over x, y_hi, core), head: 8 (over y_lo, z).
Axes of the slice: x: 4, y: 4 (y_hi: 2, y_lo: 2; y = y_hi * 2 + y_lo), z: 4, core: 2. Of those that a mesh axis runs over, the one named last changes fastest.
Arguments:
- queries: bfloat16 [6144, 8192], P('ctx', 'head')
- query_scale: bfloat16 [6144, 64], P('ctx', 'head'), may hold values from 0.25 to 4
- keys: bfloat16 [6144, 1024], P('ctx', 'head')
- key_scale: bfloat16 [6144, 8], P('ctx', 'head'), may hold values from 0.4 to 2
- values: bfloat16 [6144, 1024], P('ctx', 'head'), may hold values from -6 to 6
- value_scale: bfloat16 [6144, 8], P('ctx', 'head'), may hold values from 0.5 to 2
- block_mask: int32 [48, 48], replicated, may hold values from 0 to 1, as said below
- out_weight: bfloat16 [8192, 8192], P('head'), may hold values from -0.5 to 0.5
- out_scale: float32 [8192], P('head'), may hold values from 0.5 to 2
Outputs:
- output: bfloat16 [6144, 8192], P('ctx', 'head')
Inputs may be any that keep to these rules, and one draw needn't show every extreme that they name: block_mask[i, j] is 0 for j > i and 1 for j = i.
All inputs are finite; a program needn't handle non-finite values.
Results may differ from a plain program's by a relative error of at most 0.02.
Values may be sent and summed in bfloat16 or wider, within the bound.
No kernel may reach another device: no remote copies, remote signals or barrier semaphores. Data moves between devices by JAX's collectives and lax.ppermute only.
A program may use at most 128 MiB of HBM per device.

v0:
```python
import math

import jax
import jax.numpy as jnp
from jax import lax
from jax.sharding import PartitionSpec as P

HD = 128
GROUP = 8
BLK = 128


NEG_FILL = -1e30


def block_rows(positions, mask_table):
    count = mask_table.shape[0]
    table_hot = (positions[:, None] // BLK == jnp.arange(count, dtype=jnp.int32)[None, :]).astype(
        jnp.float32
    )
    return jnp.dot(table_hot, mask_table.astype(jnp.float32))


def make_set(q_rows, q_scales, positions, mask_table, limit):
    count = q_rows.shape[0]
    kv_local = q_rows.shape[1] // (GROUP * HD)
    shaped = q_rows.reshape(count, kv_local, GROUP, HD)
    factors = jnp.transpose(q_scales.astype(jnp.float32).reshape(count, kv_local, GROUP), (1, 2, 0))
    return (shaped, factors, positions, block_rows(positions, mask_table), limit)


def attend_block(state, query_set, key_rows, key_scales, value_rows, value_scales, first_key):
    q_rows, factors, positions, mask_rows, limit = query_set
    top, total, accum = state
    kv_local = q_rows.shape[1]
    width = key_rows.shape[0]
    keys3 = key_rows.reshape(width, kv_local, HD)
    vals3 = value_rows.reshape(width, kv_local, HD)
    key_pos = first_key + jnp.arange(width, dtype=jnp.int32)
    col_hot = (
        key_pos[:, None] // BLK == jnp.arange(mask_rows.shape[1], dtype=jnp.int32)[None, :]
    ).astype(jnp.float32)
    block_ok = jnp.dot(mask_rows, col_hot.T) > 0.5
    allowed = block_ok & (key_pos[None, :] <= positions[:, None])
    inv_root = 1.0 / jnp.sqrt(jnp.float32(HD))
    raw = jnp.einsum("rkgd,nkd->kgrn", q_rows, keys3, preferred_element_type=jnp.float32)
    scores = (
        raw * factors[..., None] * key_scales.astype(jnp.float32).T[:, None, None, :] * inv_root
    )
    scores = jnp.where(allowed[None, None], scores, NEG_FILL)
    new_top = jnp.maximum(top, jnp.max(scores, axis=3))
    expo = jnp.where(allowed[None, None], jnp.exp(scores - new_top[..., None]), 0.0)
    decay = jnp.exp(top - new_top)
    weights = (expo * value_scales.astype(jnp.float32).T[:, None, None, :]).astype(jnp.bfloat16)
    total = total * decay + jnp.sum(expo, axis=3)
    accum = accum * decay[..., None] + jnp.einsum(
        "kgrn,nkd->kgrd", weights, vals3, preferred_element_type=jnp.float32
    )
    return (new_top, total, accum)


def empty_state(query_set):
    q_rows = query_set[0]
    count, kv_local = (q_rows.shape[0], q_rows.shape[1])
    top = jnp.full((kv_local, GROUP, count), NEG_FILL, jnp.float32)
    total = jnp.zeros((kv_local, GROUP, count), jnp.float32)
    accum = jnp.zeros((kv_local, GROUP, count, HD), jnp.float32)
    return (top, total, accum)


def finish_state(state):
    top, total, accum = state
    kv_local, count = (accum.shape[0], accum.shape[2])
    safe_total = jnp.where(total > 0.0, total, 1.0)
    attended = accum / safe_total[..., None]
    return (
        jnp.transpose(attended, (2, 0, 1, 3))
        .reshape(count, kv_local * GROUP * HD)
        .astype(jnp.bfloat16)
    )


def run_attention(query_sets, keys, key_scale, values, value_scale):

    def fold_piece(states, key_piece, first_key):
        key_rows, key_sc, value_rows, value_sc = key_piece
        width = key_rows.shape[0]
        span = math.gcd(width, 512)

        def one_set(state, query_set):

            def compute(st_begin):

                def inner(i, st_now):
                    offset = i * span
                    return attend_block(
                        st_now,
                        query_set,
                        lax.dynamic_slice_in_dim(key_rows, offset, span, 0),
                        lax.dynamic_slice_in_dim(key_sc, offset, span, 0),
                        lax.dynamic_slice_in_dim(value_rows, offset, span, 0),
                        lax.dynamic_slice_in_dim(value_sc, offset, span, 0),
                        offset,
                    )

                return lax.fori_loop(0, width // span, inner, st_begin)

            def unchanged(st_begin):
                return st_begin

            return lax.cond(first_key <= query_set[4], compute, unchanged, state)

        return tuple((one_set(state, query_set) for state, query_set in zip(states, query_sets)))

    starting = tuple((empty_state(query_set) for query_set in query_sets))
    states = fold_piece(
        starting,
        (
            lax.all_gather(keys, "ctx", axis=0, tiled=True),
            lax.all_gather(key_scale, "ctx", axis=0, tiled=True),
            lax.all_gather(values, "ctx", axis=0, tiled=True),
            lax.all_gather(value_scale, "ctx", axis=0, tiled=True),
        ),
        jnp.int32(0),
    )
    return tuple((finish_state(state) for state in states))


def local(
    queries, query_scale, keys, key_scale, values, value_scale, block_mask, out_weight, out_scale
):
    tok_rows = queries.shape[0]
    ctx_rank = lax.axis_index("ctx")
    first_own = ctx_rank * tok_rows
    own_pos = first_own + jnp.arange(tok_rows, dtype=jnp.int32)
    whole_set = make_set(queries, query_scale, own_pos, block_mask, first_own + tok_rows - 1)
    (attended,) = run_attention((whole_set,), keys, key_scale, values, value_scale)
    projected = jnp.dot(attended, out_weight, preferred_element_type=jnp.float32)
    summed = lax.psum_scatter(
        projected.astype(jnp.bfloat16), "head", scatter_dimension=1, tiled=True
    ).astype(jnp.float32)
    return (summed * out_scale[None, :]).astype(jnp.bfloat16)


def solution(mesh):
    return jax.shard_map(
        local,
        mesh=mesh,
        in_specs=(
            P("ctx", "head"),
            P("ctx", "head"),
            P("ctx", "head"),
            P("ctx", "head"),
            P("ctx", "head"),
            P("ctx", "head"),
            P(),
            P("head", None),
            P("head"),
        ),
        out_specs=P("ctx", "head"),
        check_vma=False,
    )
```

profile of v0, /device:TPU:22, one launch (start us, length us, event | category | flops | bytes accessed | tf_op | source)
XLA Modules:
  0.0 378.3 jit_solution(14403441867050554419)
XLA Ops:
  8.1 18.6 %all_gather.13 = bf16[6144,1]{0,1:T(2,128)(2,1)S(1)} all-gather(bf16[384,1]{0,1:T(2,128)(2,1)} %param.16), channel_id=1, replica_groups=mesh['ctx'=16,'head'=8] {'ctx'}, dimensions={0}, use_global_device_ids=true | all-gather | bytes 13056 | tf_op jit(solution)/shard_map/all_gather | solution.py:120
  26.7 23.3 %all_gather.14 = bf16[6144,1]{0,1:T(2,128)(2,1)S(1)} all-gather(bf16[384,1]{0,1:T(2,128)(2,1)} %param.18), channel_id=1, replica_groups=mesh['ctx'=16,'head'=8] {'ctx'}, dimensions={0}, use_global_device_ids=true | all-gather | bytes 13056 | tf_op jit(solution)/shard_map/all_gather | solution.py:122
  51.7 4.1 %all-gather.3.cloned.1.call-done = bf16[6144,128]{1,0:T(8,128)(2,1)} async-done(((bf16[384,128]{1,0:T(8,128)(2,1)}), bf16[6144,128]{1,0:T(8,128)(2,1)}) %all-gather.3.cloned.1.call-update) | async-done | bytes 1572880 | tf_op jit(solution)/shard_map/all_gather | solution.py:119
  55.8 47.9 %all-gather.5.cloned.1.call-done = bf16[6144,128]{1,0:T(8,128)(2,1)} async-done(((bf16[384,128]{1,0:T(8,128)(2,1)}), bf16[6144,128]{1,0:T(8,128)(2,1)}) %all-gather.5.cloned.1.call-update) | async-done | bytes 1572880 | tf_op jit(solution)/shard_map/all_gather | solution.py:121
  103.7 175.9 %conditional.1 = (f32[1,8,384]{2,1,0:T(8,128)}, f32[1,8,384,128]{2,3,1,0:T(8,128)S(1)}) conditional(s32[]{:T(128)} %convert_element_type.55, () %tuple.35, (s32[]{:T(128)}, s32[384]{0:T(512)S(1)}, bf16[384,1024]{1,0:T(8,128)(2,1)}, bf16[384,48]{0,1:T(8,128)(2,1)S(1)}, bf16[6144,128]{1,0:T(8,128)(2,1)}, /*index=5*/f32[1,8,384]{2,1,0:T(8,128)S(1)}, ...), branch_computations={%region_0.1_spmd, %region_1.6_spmd} | conditional | flops 857460096 | bytes 55683988 | solution.py:111
  103.7 1.5 copy.15
  105.7 173.3 %while.19 = (s32[]{:T(128)}, f32[1,8,384]{2,1,0:T(8,128)S(1)}, f32[1,8,384]{2,1,0:T(8,128)}, f32[1,8,384,128]{3,2,1,0:T(8,128)S(1)}, bf16[384,48]{1,0:T(8,128)(2...) while((s32[]{:T(128)}, f32[1,8,384]{2,1,0:T(8,128)S(1)}, ...), condition=%wide.region_5.5_spmd.clone, body=%wide.region_2.4_spmd.clone.sunk | while | flops 857459712 | bytes 49315576 | solution.py:106
  106.1 5.0 %fusion.49 = (f32[8,384]{1,0:T(8,128)S(1)}, f32[512,384,8]{1,0,2:T(8,128)}) fusion(f32[512]{0:T(512)S(1)} %bitcast.109, f32[8,384]{1,0:T(8,128)S(1)} %bitcast.106, pred[384,512]{0,1:T(8,128)(4,1)S(1)} %fusion.48, bf16[384,1,8,128]{3,0,2,1:T(8,128)(2,1)S(1)} %get-tuple-element.559, bf16[6144,128]{1,0:T(8,128)(2,1)} %get-tuple-element.558, ...), kind=kOutput, calls=%fused_computation.7.clone.1 | convolution fusion | flops 410514432 | bytes 7432196 | tf_op jit(solution)/shard_map/cond/branch_1_fun/while/body/eval_jaxpr/rkgd,nkd->kgrn/dot_general | solution.py:46
  111.2 5.5 %bitcast_add_fusion.5 = f32[1,8,384,128]{3,2,1,0:T(8,128)S(1)} fusion(f32[1,8,384,128]{3,2,1,0:T(8,128)S(1)} %get-tuple-element.539, f32[512,384,8]{1,0,2:T(8,128)} %get-tuple-element.517, f32[512]{0:T(512)S(1)} %bitcast.112, f32[8,384]{1,0:T(8,128)S(1)} %bitcast.102, f32[512]{0:T(512)S(1)} %bitcast.110, f32[8,384]{1,0:T(8,128)S(1)} %bitcast.107, ...), kind=kOutput, calls=%fused_computation.10.clone.1 | convolution fusion | flops 416415744 | bytes 9805829 | tf_op jit(solution)/shard_map/cond/branch_1_fun/while/body/eval_jaxpr/kgrn,nkd->kgrd/dot_general | solution.py:56
  116.8 2.2 fusion.51
  119.9 5.0 %fusion.49 = (f32[8,384]{1,0:T(8,128)S(1)}, f32[512,384,8]{1,0,2:T(8,128)}) fusion(f32[512]{0:T(512)S(1)} %bitcast.109, f32[8,384]{1,0:T(8,128)S(1)} %bitcast.106, pred[384,512]{0,1:T(8,128)(4,1)S(1)} %fusion.48, bf16[384,1,8,128]{3,0,2,1:T(8,128)(2,1)S(1)} %get-tuple-element.559, bf16[6144,128]{1,0:T(8,128)(2,1)} %get-tuple-element.558, ...), kind=kOutput, calls=%fused_computation.7.clone.1 | convolution fusion | flops 410514432 | bytes 7432196 | tf_op jit(solution)/shard_map/cond/branch_1_fun/while/body/eval_jaxpr/rkgd,nkd->kgrn/dot_general | solution.py:46
  125.0 5.5 %bitcast_add_fusion.5 = f32[1,8,384,128]{3,2,1,0:T(8,128)S(1)} fusion(f32[1,8,384,128]{3,2,1,0:T(8,128)S(1)} %get-tuple-element.539, f32[512,384,8]{1,0,2:T(8,128)} %get-tuple-element.517, f32[512]{0:T(512)S(1)} %bitcast.112, f32[8,384]{1,0:T(8,128)S(1)} %bitcast.102, f32[512]{0:T(512)S(1)} %bitcast.110, f32[8,384]{1,0:T(8,128)S(1)} %bitcast.107, ...), kind=kOutput, calls=%fused_computation.10.clone.1 | convolution fusion | flops 416415744 | bytes 9805829 | tf_op jit(solution)/shard_map/cond/branch_1_fun/while/body/eval_jaxpr/kgrn,nkd->kgrd/dot_general | solution.py:56
  130.6 2.2 fusion.51
  132.7 1.3 bitcast_add_fusion.4
  134.4 5.0 %fusion.49 = (f32[8,384]{1,0:T(8,128)S(1)}, f32[512,384,8]{1,0,2:T(8,128)}) fusion(f32[512]{0:T(512)S(1)} %bitcast.109, f32[8,384]{1,0:T(8,128)S(1)} %bitcast.106, pred[384,512]{0,1:T(8,128)(4,1)S(1)} %fusion.48, bf16[384,1,8,128]{3,0,2,1:T(8,128)(2,1)S(1)} %get-tuple-element.559, bf16[6144,128]{1,0:T(8,128)(2,1)} %get-tuple-element.558, ...), kind=kOutput, calls=%fused_computation.7.clone.1 | convolution fusion | flops 410514432 | bytes 7432196 | tf_op jit(solution)/shard_map/cond/branch_1_fun/while/body/eval_jaxpr/rkgd,nkd->kgrn/dot_general | solution.py:46
  139.5 5.5 %bitcast_add_fusion.5 = f32[1,8,384,128]{3,2,1,0:T(8,128)S(1)} fusion(f32[1,8,384,128]{3,2,1,0:T(8,128)S(1)} %get-tuple-element.539, f32[512,384,8]{1,0,2:T(8,128)} %get-tuple-element.517, f32[512]{0:T(512)S(1)} %bitcast.112, f32[8,384]{1,0:T(8,128)S(1)} %bitcast.102, f32[512]{0:T(512)S(1)} %bitcast.110, f32[8,384]{1,0:T(8,128)S(1)} %bitcast.107, ...), kind=kOutput, calls=%fused_computation.10.clone.1 | convolution fusion | flops 416415744 | bytes 9805829 | tf_op jit(solution)/shard_map/cond/branch_1_fun/while/body/eval_jaxpr/kgrn,nkd->kgrd/dot_general | solution.py:56
  145.1 2.2 fusion.51
  147.2 1.3 bitcast_add_fusion.4
  148.9 5.0 %fusion.49 = (f32[8,384]{1,0:T(8,128)S(1)}, f32[512,384,8]{1,0,2:T(8,128)}) fusion(f32[512]{0:T(512)S(1)} %bitcast.109, f32[8,384]{1,0:T(8,128)S(1)} %bitcast.106, pred[384,512]{0,1:T(8,128)(4,1)S(1)} %fusion.48, bf16[384,1,8,128]{3,0,2,1:T(8,128)(2,1)S(1)} %get-tuple-element.559, bf16[6144,128]{1,0:T(8,128)(2,1)} %get-tuple-element.558, ...), kind=kOutput, calls=%fused_computation.7.clone.1 | convolution fusion | flops 410514432 | bytes 7432196 | tf_op jit(solution)/shard_map/cond/branch_1_fun/while/body/eval_jaxpr/rkgd,nkd->kgrn/dot_general | solution.py:46
  154.0 5.5 %bitcast_add_fusion.5 = f32[1,8,384,128]{3,2,1,0:T(8,128)S(1)} fusion(f32[1,8,384,128]{3,2,1,0:T(8,128)S(1)} %get-tuple-element.539, f32[512,384,8]{1,0,2:T(8,128)} %get-tuple-element.517, f32[512]{0:T(512)S(1)} %bitcast.112, f32[8,384]{1,0:T(8,128)S(1)} %bitcast.102, f32[512]{0:T(512)S(1)} %bitcast.110, f32[8,384]{1,0:T(8,128)S(1)} %bitcast.107, ...), kind=kOutput, calls=%fused_computation.10.clone.1 | convolution fusion | flops 416415744 | bytes 9805829 | tf_op jit(solution)/shard_map/cond/branch_1_fun/while/body/eval_jaxpr/kgrn,nkd->kgrd/dot_general | solution.py:56
  159.6 2.2 fusion.51
  163.5 5.0 %fusion.49 = (f32[8,384]{1,0:T(8,128)S(1)}, f32[512,384,8]{1,0,2:T(8,128)}) fusion(f32[512]{0:T(512)S(1)} %bitcast.109, f32[8,384]{1,0:T(8,128)S(1)} %bitcast.106, pred[384,512]{0,1:T(8,128)(4,1)S(1)} %fusion.48, bf16[384,1,8,128]{3,0,2,1:T(8,128)(2,1)S(1)} %get-tuple-element.559, bf16[6144,128]{1,0:T(8,128)(2,1)} %get-tuple-element.558, ...), kind=kOutput, calls=%fused_computation.7.clone.1 | convolution fusion | flops 410514432 | bytes 7432196 | tf_op jit(solution)/shard_map/cond/branch_1_fun/while/body/eval_jaxpr/rkgd,nkd->kgrn/dot_general | solution.py:46
  168.5 5.5 %bitcast_add_fusion.5 = f32[1,8,384,128]{3,2,1,0:T(8,128)S(1)} fusion(f32[1,8,384,128]{3,2,1,0:T(8,128)S(1)} %get-tuple-element.539, f32[512,384,8]{1,0,2:T(8,128)} %get-tuple-element.517, f32[512]{0:T(512)S(1)} %bitcast.112, f32[8,384]{1,0:T(8,128)S(1)} %bitcast.102, f32[512]{0:T(512)S(1)} %bitcast.110, f32[8,384]{1,0:T(8,128)S(1)} %bitcast.107, ...), kind=kOutput, calls=%fused_computation.10.clone.1 | convolution fusion | flops 416415744 | bytes 9805829 | tf_op jit(solution)/shard_map/cond/branch_1_fun/while/body/eval_jaxpr/kgrn,nkd->kgrd/dot_general | solution.py:56
  174.1 2.2 fusion.51
  178.0 5.0 %fusion.49 = (f32[8,384]{1,0:T(8,128)S(1)}, f32[512,384,8]{1,0,2:T(8,128)}) fusion(f32[512]{0:T(512)S(1)} %bitcast.109, f32[8,384]{1,0:T(8,128)S(1)} %bitcast.106, pred[384,512]{0,1:T(8,128)(4,1)S(1)} %fusion.48, bf16[384,1,8,128]{3,0,2,1:T(8,128)(2,1)S(1)} %get-tuple-element.559, bf16[6144,128]{1,0:T(8,128)(2,1)} %get-tuple-element.558, ...), kind=kOutput, calls=%fused_computation.7.clone.1 | convolution fusion | flops 410514432 | bytes 7432196 | tf_op jit(solution)/shard_map/cond/branch_1_fun/while/body/eval_jaxpr/rkgd,nkd->kgrn/dot_general | solution.py:46
  183.0 5.5 %bitcast_add_fusion.5 = f32[1,8,384,128]{3,2,1,0:T(8,128)S(1)} fusion(f32[1,8,384,128]{3,2,1,0:T(8,128)S(1)} %get-tuple-element.539, f32[512,384,8]{1,0,2:T(8,128)} %get-tuple-element.517, f32[512]{0:T(512)S(1)} %bitcast.112, f32[8,384]{1,0:T(8,128)S(1)} %bitcast.102, f32[512]{0:T(512)S(1)} %bitcast.110, f32[8,384]{1,0:T(8,128)S(1)} %bitcast.107, ...), kind=kOutput, calls=%fused_computation.10.clone.1 | convolution fusion | flops 416415744 | bytes 9805829 | tf_op jit(solution)/shard_map/cond/branch_1_fun/while/body/eval_jaxpr/kgrn,nkd->kgrd/dot_general | solution.py:56
  188.6 2.2 fusion.51
  192.5 5.0 %fusion.49 = (f32[8,384]{1,0:T(8,128)S(1)}, f32[512,384,8]{1,0,2:T(8,128)}) fusion(f32[512]{0:T(512)S(1)} %bitcast.109, f32[8,384]{1,0:T(8,128)S(1)} %bitcast.106, pred[384,512]{0,1:T(8,128)(4,1)S(1)} %fusion.48, bf16[384,1,8,128]{3,0,2,1:T(8,128)(2,1)S(1)} %get-tuple-element.559, bf16[6144,128]{1,0:T(8,128)(2,1)} %get-tuple-element.558, ...), kind=kOutput, calls=%fused_computation.7.clone.1 | convolution fusion | flops 410514432 | bytes 7432196 | tf_op jit(solution)/shard_map/cond/branch_1_fun/while/body/eval_jaxpr/rkgd,nkd->kgrn/dot_general | solution.py:46
  197.5 5.5 %bitcast_add_fusion.5 = f32[1,8,384,128]{3,2,1,0:T(8,128)S(1)} fusion(f32[1,8,384,128]{3,2,1,0:T(8,128)S(1)} %get-tuple-element.539, f32[512,384,8]{1,0,2:T(8,128)} %get-tuple-element.517, f32[512]{0:T(512)S(1)} %bitcast.112, f32[8,384]{1,0:T(8,128)S(1)} %bitcast.102, f32[512]{0:T(512)S(1)} %bitcast.110, f32[8,384]{1,0:T(8,128)S(1)} %bitcast.107, ...), kind=kOutput, calls=%fused_computation.10.clone.1 | convolution fusion | flops 416415744 | bytes 9805829 | tf_op jit(solution)/shard_map/cond/branch_1_fun/while/body/eval_jaxpr/kgrn,nkd->kgrd/dot_general | solution.py:56
  203.1 2.2 fusion.51
  207.0 5.0 %fusion.49 = (f32[8,384]{1,0:T(8,128)S(1)}, f32[512,384,8]{1,0,2:T(8,128)}) fusion(f32[512]{0:T(512)S(1)} %bitcast.109, f32[8,384]{1,0:T(8,128)S(1)} %bitcast.106, pred[384,512]{0,1:T(8,128)(4,1)S(1)} %fusion.48, bf16[384,1,8,128]{3,0,2,1:T(8,128)(2,1)S(1)} %get-tuple-element.559, bf16[6144,128]{1,0:T(8,128)(2,1)} %get-tuple-element.558, ...), kind=kOutput, calls=%fused_computation.7.clone.1 | convolution fusion | flops 410514432 | bytes 7432196 | tf_op jit(solution)/shard_map/cond/branch_1_fun/while/body/eval_jaxpr/rkgd,nkd->kgrn/dot_general | solution.py:46
  212.0 5.5 %bitcast_add_fusion.5 = f32[1,8,384,128]{3,2,1,0:T(8,128)S(1)} fusion(f32[1,8,384,128]{3,2,1,0:T(8,128)S(1)} %get-tuple-element.539, f32[512,384,8]{1,0,2:T(8,128)} %get-tuple-element.517, f32[512]{0:T(512)S(1)} %bitcast.112, f32[8,384]{1,0:T(8,128)S(1)} %bitcast.102, f32[512]{0:T(512)S(1)} %bitcast.110, f32[8,384]{1,0:T(8,128)S(1)} %bitcast.107, ...), kind=kOutput, calls=%fused_computation.10.clone.1 | convolution fusion | flops 416415744 | bytes 9805829 | tf_op jit(solution)/shard_map/cond/branch_1_fun/while/body/eval_jaxpr/kgrn,nkd->kgrd/dot_general | solution.py:56
  217.6 2.2 fusion.51
  221.5 5.0 %fusion.49 = (f32[8,384]{1,0:T(8,128)S(1)}, f32[512,384,8]{1,0,2:T(8,128)}) fusion(f32[512]{0:T(512)S(1)} %bitcast.109, f32[8,384]{1,0:T(8,128)S(1)} %bitcast.106, pred[384,512]{0,1:T(8,128)(4,1)S(1)} %fusion.48, bf16[384,1,8,128]{3,0,2,1:T(8,128)(2,1)S(1)} %get-tuple-element.559, bf16[6144,128]{1,0:T(8,128)(2,1)} %get-tuple-element.558, ...), kind=kOutput, calls=%fused_computation.7.clone.1 | convolution fusion | flops 410514432 | bytes 7432196 | tf_op jit(solution)/shard_map/cond/branch_1_fun/while/body/eval_jaxpr/rkgd,nkd->kgrn/dot_general | solution.py:46
  226.5 5.5 %bitcast_add_fusion.5 = f32[1,8,384,128]{3,2,1,0:T(8,128)S(1)} fusion(f32[1,8,384,128]{3,2,1,0:T(8,128)S(1)} %get-tuple-element.539, f32[512,384,8]{1,0,2:T(8,128)} %get-tuple-element.517, f32[512]{0:T(512)S(1)} %bitcast.112, f32[8,384]{1,0:T(8,128)S(1)} %bitcast.102, f32[512]{0:T(512)S(1)} %bitcast.110, f32[8,384]{1,0:T(8,128)S(1)} %bitcast.107, ...), kind=kOutput, calls=%fused_computation.10.clone.1 | convolution fusion | flops 416415744 | bytes 9805829 | tf_op jit(solution)/shard_map/cond/branch_1_fun/while/body/eval_jaxpr/kgrn,nkd->kgrd/dot_general | solution.py:56
  232.1 2.2 fusion.51
  236.0 5.0 %fusion.49 = (f32[8,384]{1,0:T(8,128)S(1)}, f32[512,384,8]{1,0,2:T(8,128)}) fusion(f32[512]{0:T(512)S(1)} %bitcast.109, f32[8,384]{1,0:T(8,128)S(1)} %bitcast.106, pred[384,512]{0,1:T(8,128)(4,1)S(1)} %fusion.48, bf16[384,1,8,128]{3,0,2,1:T(8,128)(2,1)S(1)} %get-tuple-element.559, bf16[6144,128]{1,0:T(8,128)(2,1)} %get-tuple-element.558, ...), kind=kOutput, calls=%fused_computation.7.clone.1 | convolution fusion | flops 410514432 | bytes 7432196 | tf_op jit(solution)/shard_map/cond/branch_1_fun/while/body/eval_jaxpr/rkgd,nkd->kgrn/dot_general | solution.py:46
  241.0 5.5 %bitcast_add_fusion.5 = f32[1,8,384,128]{3,2,1,0:T(8,128)S(1)} fusion(f32[1,8,384,128]{3,2,1,0:T(8,128)S(1)} %get-tuple-element.539, f32[512,384,8]{1,0,2:T(8,128)} %get-tuple-element.517, f32[512]{0:T(512)S(1)} %bitcast.112, f32[8,384]{1,0:T(8,128)S(1)} %bitcast.102, f32[512]{0:T(512)S(1)} %bitcast.110, f32[8,384]{1,0:T(8,128)S(1)} %bitcast.107, ...), kind=kOutput, calls=%fused_computation.10.clone.1 | convolution fusion | flops 416415744 | bytes 9805829 | tf_op jit(solution)/shard_map/cond/branch_1_fun/while/body/eval_jaxpr/kgrn,nkd->kgrd/dot_general | solution.py:56
  246.6 2.2 fusion.51
  250.5 5.0 %fusion.49 = (f32[8,384]{1,0:T(8,128)S(1)}, f32[512,384,8]{1,0,2:T(8,128)}) fusion(f32[512]{0:T(512)S(1)} %bitcast.109, f32[8,384]{1,0:T(8,128)S(1)} %bitcast.106, pred[384,512]{0,1:T(8,128)(4,1)S(1)} %fusion.48, bf16[384,1,8,128]{3,0,2,1:T(8,128)(2,1)S(1)} %get-tuple-element.559, bf16[6144,128]{1,0:T(8,128)(2,1)} %get-tuple-element.558, ...), kind=kOutput, calls=%fused_computation.7.clone.1 | convolution fusion | flops 410514432 | bytes 7432196 | tf_op jit(solution)/shard_map/cond/branch_1_fun/while/body/eval_jaxpr/rkgd,nkd->kgrn/dot_general | solution.py:46
  255.5 5.5 %bitcast_add_fusion.5 = f32[1,8,384,128]{3,2,1,0:T(8,128)S(1)} fusion(f32[1,8,384,128]{3,2,1,0:T(8,128)S(1)} %get-tuple-element.539, f32[512,384,8]{1,0,2:T(8,128)} %get-tuple-element.517, f32[512]{0:T(512)S(1)} %bitcast.112, f32[8,384]{1,0:T(8,128)S(1)} %bitcast.102, f32[512]{0:T(512)S(1)} %bitcast.110, f32[8,384]{1,0:T(8,128)S(1)} %bitcast.107, ...), kind=kOutput, calls=%fused_computation.10.clone.1 | convolution fusion | flops 416415744 | bytes 9805829 | tf_op jit(solution)/shard_map/cond/branch_1_fun/while/body/eval_jaxpr/kgrn,nkd->kgrd/dot_general | solution.py:56
  261.1 2.2 fusion.51
  265.0 5.0 %fusion.49 = (f32[8,384]{1,0:T(8,128)S(1)}, f32[512,384,8]{1,0,2:T(8,128)}) fusion(f32[512]{0:T(512)S(1)} %bitcast.109, f32[8,384]{1,0:T(8,128)S(1)} %bitcast.106, pred[384,512]{0,1:T(8,128)(4,1)S(1)} %fusion.48, bf16[384,1,8,128]{3,0,2,1:T(8,128)(2,1)S(1)} %get-tuple-element.559, bf16[6144,128]{1,0:T(8,128)(2,1)} %get-tuple-element.558, ...), kind=kOutput, calls=%fused_computation.7.clone.1 | convolution fusion | flops 410514432 | bytes 7432196 | tf_op jit(solution)/shard_map/cond/branch_1_fun/while/body/eval_jaxpr/rkgd,nkd->kgrn/dot_general | solution.py:46
  270.0 5.5 %bitcast_add_fusion.5 = f32[1,8,384,128]{3,2,1,0:T(8,128)S(1)} fusion(f32[1,8,384,128]{3,2,1,0:T(8,128)S(1)} %get-tuple-element.539, f32[512,384,8]{1,0,2:T(8,128)} %get-tuple-element.517, f32[512]{0:T(512)S(1)} %bitcast.112, f32[8,384]{1,0:T(8,128)S(1)} %bitcast.102, f32[512]{0:T(512)S(1)} %bitcast.110, f32[8,384]{1,0:T(8,128)S(1)} %bitcast.107, ...), kind=kOutput, calls=%fused_computation.10.clone.1 | convolution fusion | flops 416415744 | bytes 9805829 | tf_op jit(solution)/shard_map/cond/branch_1_fun/while/body/eval_jaxpr/kgrn,nkd->kgrd/dot_general | solution.py:56
  275.6 2.2 fusion.51
  280.4 14.6 %convolution_convert_fusion = bf16[384,8192]{1,0:T(8,128)(2,1)} fusion(bf16[384,1024]{0,1:T(8,128)(2,1)S(1)} %bitcast.104, bf16[1024,8192]{1,0:T(8,128)(2,1)} %param.20), kind=kOutput, calls=%fused_computation.45 | convolution fusion | flops 6445596672 | bytes 23855104 | tf_op jit(solution)/shard_map/dot_general | solution.py:138
  295.0 74.5 %reduce-scatter.2.cloned.1.call-done = bf16[384,1024]{1,0:T(8,128)(2,1)} async-done(((bf16[384,8192]{1,0:T(8,128)(2,1)}), bf16[384,1024]{1,0:T(8,128)(2,1)}) %reduce-scatter.2.cloned.1.call-update) | async-done | bytes 786448 | tf_op jit(solution)/shard_map/reduce_scatter | solution.py:139
  369.6 2.2 multiply_convert_fusion.1
  (115 shorter events, 22.1 us)
Async XLA Ops:
  6.5 49.3 %all-gather.3.cloned.1.call-start = ((), (), s32[]{:S(2)}) async-start(), calls=%async_computation.1 | async-start | bytes 1671168 | tf_op jit(solution)/shard_map/all_gather | solution.py:119
  7.3 96.4 %all-gather.5.cloned.1.call-start = ((), (), s32[]{:S(2)}) async-start(), calls=%async_computation.2 | async-start | bytes 1671168 | tf_op jit(solution)/shard_map/all_gather | solution.py:121
  8.0 361.6 %reduce-scatter.2.cloned.1.call-start = ((), (), s32[]{:S(2)}) async-start(), calls=%async_computation.3 | async-start | bytes 7077888 | tf_op jit(solution)/shard_map/reduce_scatter | solution.py:139
  111.2 5.6 %copy-start = (f32[512,384,8]{1,0,2:T(8,128)S(1)}, f32[512,384,8]{1,0,2:T(8,128)}, u32[]{:S(2)}) copy-start(f32[512,384,8]{1,0,2:T(8,128)} %get-tuple-element.517) | copy-start | bytes 18874372 | tf_op jit(solution)/shard_map/cond/branch_1_fun/while
  125.0 5.6 %copy-start = (f32[512,384,8]{1,0,2:T(8,128)S(1)}, f32[512,384,8]{1,0,2:T(8,128)}, u32[]{:S(2)}) copy-start(f32[512,384,8]{1,0,2:T(8,128)} %get-tuple-element.517) | copy-start | bytes 18874372 | tf_op jit(solution)/shard_map/cond/branch_1_fun/while
  139.5 5.6 %copy-start = (f32[512,384,8]{1,0,2:T(8,128)S(1)}, f32[512,384,8]{1,0,2:T(8,128)}, u32[]{:S(2)}) copy-start(f32[512,384,8]{1,0,2:T(8,128)} %get-tuple-element.517) | copy-start | bytes 18874372 | tf_op jit(solution)/shard_map/cond/branch_1_fun/while
  154.0 5.6 %copy-start = (f32[512,384,8]{1,0,2:T(8,128)S(1)}, f32[512,384,8]{1,0,2:T(8,128)}, u32[]{:S(2)}) copy-start(f32[512,384,8]{1,0,2:T(8,128)} %get-tuple-element.517) | copy-start | bytes 18874372 | tf_op jit(solution)/shard_map/cond/branch_1_fun/while
  168.5 5.6 %copy-start = (f32[512,384,8]{1,0,2:T(8,128)S(1)}, f32[512,384,8]{1,0,2:T(8,128)}, u32[]{:S(2)}) copy-start(f32[512,384,8]{1,0,2:T(8,128)} %get-tuple-element.517) | copy-start | bytes 18874372 | tf_op jit(solution)/shard_map/cond/branch_1_fun/while
  183.0 5.6 %copy-start = (f32[512,384,8]{1,0,2:T(8,128)S(1)}, f32[512,384,8]{1,0,2:T(8,128)}, u32[]{:S(2)}) copy-start(f32[512,384,8]{1,0,2:T(8,128)} %get-tuple-element.517) | copy-start | bytes 18874372 | tf_op jit(solution)/shard_map/cond/branch_1_fun/while
  197.5 5.6 %copy-start = (f32[512,384,8]{1,0,2:T(8,128)S(1)}, f32[512,384,8]{1,0,2:T(8,128)}, u32[]{:S(2)}) copy-start(f32[512,384,8]{1,0,2:T(8,128)} %get-tuple-element.517) | copy-start | bytes 18874372 | tf_op jit(solution)/shard_map/cond/branch_1_fun/while
  212.0 5.6 %copy-start = (f32[512,384,8]{1,0,2:T(8,128)S(1)}, f32[512,384,8]{1,0,2:T(8,128)}, u32[]{:S(2)}) copy-start(f32[512,384,8]{1,0,2:T(8,128)} %get-tuple-element.517) | copy-start | bytes 18874372 | tf_op jit(solution)/shard_map/cond/branch_1_fun/while
  226.5 5.6 %copy-start = (f32[512,384,8]{1,0,2:T(8,128)S(1)}, f32[512,384,8]{1,0,2:T(8,128)}, u32[]{:S(2)}) copy-start(f32[512,384,8]{1,0,2:T(8,128)} %get-tuple-element.517) | copy-start | bytes 18874372 | tf_op jit(solution)/shard_map/cond/branch_1_fun/while
  241.0 5.6 %copy-start = (f32[512,384,8]{1,0,2:T(8,128)S(1)}, f32[512,384,8]{1,0,2:T(8,128)}, u32[]{:S(2)}) copy-start(f32[512,384,8]{1,0,2:T(8,128)} %get-tuple-element.517) | copy-start | bytes 18874372 | tf_op jit(solution)/shard_map/cond/branch_1_fun/while
  255.5 5.6 %copy-start = (f32[512,384,8]{1,0,2:T(8,128)S(1)}, f32[512,384,8]{1,0,2:T(8,128)}, u32[]{:S(2)}) copy-start(f32[512,384,8]{1,0,2:T(8,128)} %get-tuple-element.517) | copy-start | bytes 18874372 | tf_op jit(solution)/shard_map/cond/branch_1_fun/while
  270.0 5.6 %copy-start = (f32[512,384,8]{1,0,2:T(8,128)S(1)}, f32[512,384,8]{1,0,2:T(8,128)}, u32[]{:S(2)}) copy-start(f32[512,384,8]{1,0,2:T(8,128)} %get-tuple-element.517) | copy-start | bytes 18874372 | tf_op jit(solution)/shard_map/cond/branch_1_fun/while
  295.0 74.6 %copy-start.1 = (f32[1024]{0:T(1024)S(1)}, f32[1024]{0:T(1024)}, u32[]{:S(2)}) copy-start(f32[1024]{0:T(1024)} %param.21) | copy-start | bytes 12292
Sparse Core Ops, SparseCore 0:
  9.7 46.0 all-gather.2
  58.2 45.4 all-gather.4
  295.2 74.3 reduce-scatter.1
where the time goes:
time: 381 us; the launch traced here: 378 us
  matrix products  146 us (38%)
  waiting for transfers between devices  128 us (34%)
  other arithmetic  45.5 us (12%)
  blocking collectives  41.9 us (11%)
  between operations  13.1 us (3%)
    reduce_scatter x1, waiting for transfers between devices, local(): lax.psum_scatter(projected.astype(jnp.bfloat16), 'head', scatter_dimensio...  74.5 us
    dot_general x12, matrix products, attend_block(): jnp.einsum('kgrn,nkd->kgrd', weights, vals3, preferred_element_type=jnp.f...  66.5 us
    dot_general x12, matrix products, attend_block(): jnp.einsum('rkgd,nkd->kgrn', q_rows, keys3, preferred_element_type=jnp.fl...  60.4 us
    all_gather x1, waiting for transfers between devices, run_attention(): lax.all_gather(values, 'ctx', axis=0, tiled=True)  47.9 us
    reduce_sum x12, other arithmetic, attend_block(): total = total * decay + jnp.sum(expo, axis=3)  26.1 us
    all_gather x1, blocking collectives, run_attention(): lax.all_gather(value_scale, 'ctx', axis=0, tiled=True)  23.3 us
    all_gather x1, blocking collectives, run_attention(): lax.all_gather(key_scale, 'ctx', axis=0, tiled=True)  18.6 us
    add x12, other arithmetic, attend_block(): total = total * decay + jnp.sum(expo, axis=3)  15.3 us
  transfers between devices with their start and end apart: 3, of which 3 were waited for; matrix products, arithmetic and copies ran while one was open for 0% of the time, Pallas kernels for 0%

commit v1 on v0

v1 whole, which is shorter than its diff:
```python
import functools
import math

import jax
import jax.numpy as jnp
from jax import lax
from jax.experimental import pallas as pl
from jax.experimental.pallas import tpu as pltpu
from jax.sharding import PartitionSpec as P

HD = 128
GROUP = 8
BLK = 128
RANK_BLOCKS = 3
CHIPS = 8
QSCALE = math.log2(math.e) / math.sqrt(HD)
F32 = jnp.float32
BF16 = jnp.bfloat16


def fold_blocks(blocks, causal, kv, qt, top, total, accum):
    keys = jnp.concatenate([kv[b, :, :HD] for b in blocks], axis=0)
    vals_t = jnp.concatenate([kv[b, :, HD:] for b in blocks], axis=1)
    for pair in range(GROUP // 2):
        cols = pl.ds(pair * 2 * BLK, 2 * BLK)
        scores = jnp.dot(keys, qt[:, cols], preferred_element_type=F32)
        if causal:
            key_at = lax.broadcasted_iota(jnp.int32, scores.shape, 0)
            row_at = lax.broadcasted_iota(jnp.int32, scores.shape, 1) % BLK
            scores = jnp.where(key_at <= row_at, scores, -jnp.inf)
            new_top = jnp.max(scores, axis=0, keepdims=True)
            expo = jnp.exp2(scores - new_top)
            total[:, cols] = jnp.sum(expo, axis=0, keepdims=True)
            accum[:, cols] = jnp.dot(vals_t, expo.astype(BF16), preferred_element_type=F32)
        else:
            old_top = top[:, cols]
            new_top = jnp.maximum(old_top, jnp.max(scores, axis=0, keepdims=True))
            expo = jnp.exp2(scores - new_top)
            decay = jnp.exp2(old_top - new_top)
            total[:, cols] = total[:, cols] * decay + jnp.sum(expo, axis=0, keepdims=True)
            accum[:, cols] = accum[:, cols] * decay + jnp.dot(
                vals_t, expo.astype(BF16), preferred_element_type=F32
            )
        top[:, cols] = new_top


def attend_kernel(
    first_of, place, mask, q_ref, qs_ref, mine, other, o_ref, kv, qt, top, total, accum, todo, sems
):
    chip, core = place[0], place[1]

    def copies():
        made = []
        for which, source in ((0, mine), (1, other)):
            for shift in range(CHIPS):
                owner = 2 * lax.rem(chip - shift + CHIPS, CHIPS) + lax.rem(core + which, 2)
                made.append(
                    pltpu.make_async_copy(
                        source.at[pl.ds(shift * RANK_BLOCKS, RANK_BLOCKS)],
                        kv.at[pl.ds(owner * RANK_BLOCKS, RANK_BLOCKS)],
                        sems.at[which * CHIPS + shift],
                    )
                )
        return made

    @pl.when(pl.program_id(0) == 0)
    def _():
        for copy in copies():
            copy.start()

    row_block = first_of[0] + pl.program_id(0)
    for head in range(GROUP):
        cols = pl.ds(head * HD, HD)
        scale = qs_ref[:, head : head + 1].astype(F32) * QSCALE
        qt[:, cols] = (q_ref[:, cols].astype(F32) * scale).T.astype(BF16)

    def list_block(block, count):
        @pl.when(mask[row_block, block] == 1)
        def _():
            todo[count] = block

        return count + jnp.where(mask[row_block, block] == 1, 1, 0)

    count = lax.fori_loop(0, row_block, list_block, jnp.int32(0))

    @pl.when(pl.program_id(0) == 0)
    def _():
        for copy in copies():
            copy.wait()

    state = (kv, qt, top, total, accum)
    fold_blocks([row_block], True, *state)

    @pl.loop(0, count // 4)
    def _(step):
        fold_blocks([todo[4 * step + i] for i in range(4)], False, *state)

    @pl.when(count % 4 >= 2)
    def _():
        at = count // 4 * 4
        fold_blocks([todo[at], todo[at + 1]], False, *state)

    @pl.when(count % 2 == 1)
    def _():
        fold_blocks([todo[count - 1]], False, *state)

    for head in range(GROUP):
        cols = pl.ds(head * HD, HD)
        o_ref[:, cols] = (accum[:, cols] / total[:, cols]).T.astype(BF16)


def attend(first_block, place, mask, queries, query_scale, mine, other, rows):
    smem = pl.BlockSpec(memory_space=pltpu.SMEM)
    blocks = mask.shape[0]
    count = rows // BLK
    wide = GROUP * HD
    return pl.pallas_call(
        attend_kernel,
        grid=(count,),
        out_shape=jax.ShapeDtypeStruct((rows, wide), BF16),
        in_specs=[
            smem,
            smem,
            smem,
            pl.BlockSpec((BLK, wide), lambda i: (i, 0)),
            pl.BlockSpec((BLK, GROUP), lambda i: (i, 0)),
            pl.BlockSpec(memory_space=pl.ANY),
            pl.BlockSpec(memory_space=pl.ANY),
        ],
        out_specs=pl.BlockSpec((BLK, wide), lambda i: (i, 0)),
        scratch_shapes=[
            pltpu.VMEM((blocks, BLK, 2 * HD), BF16),
            pltpu.VMEM((HD, wide), BF16),
            pltpu.VMEM((1, wide), F32),
            pltpu.VMEM((1, wide), F32),
            pltpu.VMEM((HD, wide), F32),
            pltpu.SMEM((blocks,), jnp.int32),
            pltpu.SemaphoreType.DMA((2 * CHIPS,)),
        ],
        compiler_params=pltpu.CompilerParams(vmem_limit_bytes=32 << 20),
        cost_estimate=pl.CostEstimate(
            flops=4 * rows * wide * blocks * BLK // 2,
            bytes_accessed=blocks * BLK * HD * 4 + rows * wide * 4,
            transcendentals=rows * GROUP * blocks * BLK // 2,
        ),
        name="attend",
    )(first_block, place, mask, queries, query_scale, mine, other)


def pack(keys, key_scale, values, value_scale):
    scaled_k = keys.astype(F32) * key_scale.astype(F32)
    scaled_v = values.astype(F32) * value_scale.astype(F32)
    k3 = scaled_k.astype(BF16).reshape(RANK_BLOCKS, BLK, HD)
    v3 = jnp.transpose(scaled_v.astype(BF16).reshape(RANK_BLOCKS, BLK, HD), (0, 2, 1))
    return jnp.concatenate([k3, v3], axis=2)


def gather(packed):
    got = [packed]
    for shift in range(1, CHIPS):
        pairs = [(2 * a + c, 2 * (a + shift) + c) for a in range(CHIPS - shift) for c in range(2)]
        got.append(lax.ppermute(packed, "ctx", pairs))
    mine = jnp.concatenate(got, axis=0)
    other = lax.ppermute(mine, "ctx", [(i, i ^ 1) for i in range(2 * CHIPS)])
    return mine, other


def local(
    queries, query_scale, keys, key_scale, values, value_scale, block_mask, out_weight, out_scale
):
    rows = queries.shape[0]
    rank = lax.axis_index("ctx").astype(jnp.int32)
    place = jnp.stack([rank // 2, rank % 2])
    mine, other = gather(pack(keys, key_scale, values, value_scale))
    attended = attend(
        (rank * RANK_BLOCKS)[None], place, block_mask, queries, query_scale, mine, other, rows
    )
    projected = jnp.dot(attended, out_weight, preferred_element_type=F32)
    summed = lax.psum_scatter(
        projected.astype(BF16), "head", scatter_dimension=1, tiled=True
    ).astype(F32)
    return (summed * out_scale[None, :]).astype(BF16)


def solution(mesh):
    return jax.shard_map(
        local,
        mesh=mesh,
        in_specs=(
            P("ctx", "head"),
            P("ctx", "head"),
            P("ctx", "head"),
            P("ctx", "head"),
            P("ctx", "head"),
            P("ctx", "head"),
            P(),
            P("head", None),
            P("head"),
        ),
        out_specs=P("ctx", "head"),
        check_vma=False,
    )
```

time: 381 us -> 177 us (0.46)
  matrix products: 146 us -> 8.72 us
  blocking collectives: 41.9 us -> 0 us
  other arithmetic: 45.5 us -> 5.73 us
  Pallas kernels: 0 us -> 39.4 us
  waiting for transfers between devices: 128 us -> 97 us
  starting transfers between devices: 0.08 us -> 9.11 us
    dot_general x38 -> x1, matrix products: 146 us -> 8.72 us  [local(): projected = jnp.dot(attended, out_weight, preferred_element_type=F32)]
    all_gather x2 -> x0, waiting for transfers between devices: 52 us -> none  [the longest x1 47.9 us: run_attention(): lax.all_gather(values, 'ctx', axis=0, tiled=True)]
    all_gather x2 -> x0, blocking collectives: 41.9 us -> none  [the longest x1 23.3 us: run_attention(): lax.all_gather(value_scale, 'ctx', axis=0, tiled=True)]
    pallas_call x0 -> x1, Pallas kernels: none -> 39.4 us  [attend(): pl.pallas_call(attend_kernel, grid=(count,), out_shape=jax.ShapeDtypeStru...]
    reduce_sum x12 -> x0, other arithmetic: 26.1 us -> none  [attend_block(): total = total * decay + jnp.sum(expo, axis=3)]
    ppermute x0 -> x8, waiting for transfers between devices: none -> 22.2 us  [the longest x7 19.1 us: gather(): got.append(lax.ppermute(packed, 'ctx', pairs))]
    add x13 -> x0, other arithmetic: 15.3 us -> none  [the longest x12 15.3 us: attend_block(): total = total * decay + jnp.sum(expo, axis=3)]
    ppermute x0 -> x8, starting transfers between devices: none -> 9.11 us  [the longest x7 9.02 us: gather(): got.append(lax.ppermute(packed, 'ctx', pairs))]
  transfers between devices with their start and end apart: 3 -> 9, of which waited for: 3 -> 7; matrix products, arithmetic and copies ran while one was open for 0% -> 0% of each run, Pallas kernels for 0% -> 0%
where the time goes in v1:
time: 177 us; the launch traced here: 175 us
  waiting for transfers between devices  97 us (55%)
  Pallas kernels  39.4 us (22%)
  between operations  13.6 us (8%)
  starting transfers between devices  9.11 us (5%)
  matrix products  8.72 us (5%)
  other arithmetic  5.73 us (3%)
    reduce_scatter x1, waiting for transfers between devices, local(): lax.psum_scatter(projected.astype(BF16), 'head', scatter_dimension=1, til...  74.8 us
    pallas_call x1, Pallas kernels, attend(): pl.pallas_call(attend_kernel, grid=(count,), out_shape=jax.ShapeDtypeStru...  39.4 us
    ppermute x7, waiting for transfers between devices, gather(): got.append(lax.ppermute(packed, 'ctx', pairs))  19.1 us
    ppermute x7, starting transfers between devices, gather(): got.append(lax.ppermute(packed, 'ctx', pairs))  9.02 us
    dot_general x1, matrix products, local(): projected = jnp.dot(attended, out_weight, preferred_element_type=F32)  8.72 us
  transfers between devices with their start and end apart: 9, of which 7 were waited for; matrix products, arithmetic and copies ran while one was open for 0% of the time, Pallas kernels for 0%

profile of v1, /device:TPU:22, one launch (start us, length us, event | category | flops | bytes accessed | tf_op | source)
XLA Modules:
  0.0 175.2 jit_solution(12030439963356544760)
XLA Ops:
  6.5 0.0 reduce-scatter.2.cloned.1.call-start
  6.5 0.7 convert_reduce_fusion.1
  7.2 0.7 convert_reduce_fusion
  7.9 1.0 multiply_convert_fusion.1
  8.9 0.1 copy.11
  9.1 1.0 multiply_convert_fusion.2
  10.1 0.0 copy-start.2
  10.1 0.0 copy-start.1
  10.2 1.3 collective-permute-start
  11.5 1.3 collective-permute-start.1
  12.8 1.3 collective-permute-start.5
  14.1 1.3 collective-permute-start.4
  15.4 1.3 collective-permute-start.3
  16.7 3.5 %collective-permute-done = bf16[3,128,256]{2,1,0:T(8,128)(2,1)S(1)} collective-permute-done((bf16[3,128,256]{2,1,0:T(8,128)(2,1)S(1)}, bf16[3,128,256]{2,1,0:T(8,128)(2,1)S(1)}, u32[]{:S(2)}, u32[]{:S(2)}) %collective-permute-start) | collective-permute-done | bytes 196640 | tf_op jit(solution)/shard_map/ppermute | solution.py:162
  20.2 1.3 collective-permute-start.2
  21.5 1.2 collective-permute-done.1
  22.7 1.3 collective-permute-start.6
  24.0 7.1 %collective-permute-done.2 = bf16[3,128,256]{2,1,0:T(8,128)(2,1)S(1)} collective-permute-done((bf16[3,128,256]{2,1,0:T(8,128)(2,1)S(1)}, bf16[3,128,256]{2,1,0:T(8,128)(2,1)S(1)}, u32[]{:S(2)}, u32[]{:S(2)}) %collective-permute-start.2) | collective-permute-done | bytes 196640 | tf_op jit(solution)/shard_map/ppermute | solution.py:162
  31.1 0.0 collective-permute-done.3
  31.1 0.0 collective-permute-done.4
  31.2 1.6 collective-permute-done.5
  32.8 5.7 %collective-permute-done.6 = bf16[3,128,256]{2,1,0:T(8,128)(2,1)S(1)} collective-permute-done((bf16[3,128,256]{2,1,0:T(8,128)(2,1)S(1)}, bf16[3,128,256]{2,1,0:T(8,128)(2,1)S(1)}, u32[]{:S(2)}, u32[]{:S(2)}) %collective-permute-start.6) | collective-permute-done | bytes 196640 | tf_op jit(solution)/shard_map/ppermute | solution.py:162
  38.5 0.1 collective-permute-start.7
  38.6 0.0 copy-done.2
  38.6 0.2 copy.12.qs_ref
  38.8 0.1 pad_add_fusion.place
  38.8 3.1 %collective-permute-done.7.other = bf16[24,128,256]{2,1,0:T(8,128)(2,1)S(1)} collective-permute-done((bf16[24,128,256]{2,1,0:T(8,128)(2,1)S(1)}, bf16[24,128,256]{2,1,0:T(8,128)(2,1)S(1)}, u32[]{:S(2)}, u32[]{:S(2)}) %collective-permute-start.7) | collective-permute-done | bytes 1572896 | tf_op jit(solution)/shard_map/ppermute | solution.py:164
  42.0 0.0 copy-done.1
  42.0 0.0 copy-start
  42.0 1.1 copy-done
  43.1 0.0 copy-start.4
  43.1 39.4 %attend.1 = bf16[384,1024]{1,0:T(8,128)(2,1)S(1)} custom-call(s32[1]{0:T(128)} %bitcast.first_of, s32[2]{0:T(128)S(1)} %pad_add_fusion.place, s32[48,48]{1,0:T(8,128)S(1)} %copy-done.1, bf16[384,1024]{1,0:T(8,128)(2,1)S(1)} %copy-done, bf16[384,8]{1,0:T(8,128)(2,1)S(1)} %copy.12.qs_ref, bf16[24,128,256]{2,1,0:T(8,128)(2,1)S(1)} %constant_dynamic-update-slice_fusion.mine, ...), custom_call_target="tpu_custom_call" | custom-call | flops 4831838208 | bytes 4718592 | tf_op jit(solution)/shard_map/attend/pallas_call | solution.py:117
  82.5 0.0 copy-done.4
  82.6 8.7 %convolution_convert_fusion = bf16[384,8192]{1,0:T(8,128)(2,1)} fusion(bf16[384,1024]{1,0:T(8,128)(2,1)S(1)} %attend.1, bf16[1024,8192]{1,0:T(8,128)(2,1)S(1)} %copy-done.4), kind=kOutput, calls=%fused_computation | convolution fusion | flops 6445596672 | bytes 23855104 | tf_op jit(solution)/shard_map/dot_general | solution.py:178
  91.3 0.0 copy-start.3
  91.3 0.0 reduce-scatter.2.cloned.1.call-update
  91.3 74.8 %reduce-scatter.2.cloned.1.call-done = bf16[384,1024]{1,0:T(8,128)(2,1)} async-done(((bf16[384,8192]{1,0:T(8,128)(2,1)}), bf16[384,1024]{1,0:T(8,128)(2,1)}) %reduce-scatter.2.cloned.1.call-update) | async-done | bytes 786448 | tf_op jit(solution)/shard_map/reduce_scatter | solution.py:179
  166.1 0.0 copy-done.3
  166.1 2.2 %multiply_convert_fusion = bf16[384,1024]{1,0:T(8,128)(2,1)} fusion(bf16[384,1024]{1,0:T(8,128)(2,1)} %reduce-scatter.2.cloned.1.call-done, f32[1024]{0:T(1024)S(1)} %copy-done.3), kind=kLoop, calls=%fused_computation.1 | loop fusion | flops 1179648 | bytes 1576960 | tf_op jit(solution)/shard_map/convert_element_type | solution.py:182
  (8 shorter events, 0.1 us)
Async XLA Ops:
  6.5 159.6 %reduce-scatter.2.cloned.1.call-start = ((), (), s32[]{:S(2)}) async-start(), calls=%async_computation.1 | async-start | bytes 7077888 | tf_op jit(solution)/shard_map/reduce_scatter | solution.py:179
  10.1 28.5 %copy-start.2 = (bf16[384,8]{0,1:T(8,128)(2,1)S(1)}, bf16[384,8]{0,1:T(8,128)(2,1)}, u32[]{:S(2)}) copy-start(bf16[384,8]{0,1:T(8,128)(2,1)} %param.10) | copy-start | bytes 18436
  10.1 31.8 %copy-start.1 = (s32[48,48]{1,0:T(8,128)S(1)}, s32[48,48]{1,0:T(8,128)}, u32[]{:S(2)}) copy-start(s32[48,48]{1,0:T(8,128)} %mask.1) | copy-start | bytes 27652
  10.2 10.0 %collective-permute-start = (bf16[3,128,256]{2,1,0:T(8,128)(2,1)S(1)}, bf16[3,128,256]{2,1,0:T(8,128)(2,1)S(1)}, u32[]{:S(2)}, u32[]{:S(2)}) collective-permute-start(bf16[3,128,256]{2,1,0:T(8,128)(2,1)S(1)} %get-tuple-element.5), channel_id=1, source_target_pairs={{0,16},{8,24},{16,32},{24,40},{32,48},{40,56},{48,64},{56,72},{64,... | collective-permute-start | bytes 589832 | tf_op jit(solution)/shard_map/ppermute | solution.py:162
  11.5 11.2 %collective-permute-start.1 = (bf16[3,128,256]{2,1,0:T(8,128)(2,1)S(1)}, bf16[3,128,256]{2,1,0:T(8,128)(2,1)S(1)}, u32[]{:S(2)}, u32[]{:S(2)}) collective-permute-start(bf16[3,128,256]{2,1,0:T(8,128)(2,1)S(1)} %get-tuple-element.5), channel_id=1, source_target_pairs={{0,32},{8,40},{16,48},{24,56},{32,64},{40,72},{48,80},{56,88},{64,... | collective-permute-start | bytes 589832 | tf_op jit(solution)/shard_map/ppermute | solution.py:162
  12.8 20.0 %collective-permute-start.5 = (bf16[3,128,256]{2,1,0:T(8,128)(2,1)S(1)}, bf16[3,128,256]{2,1,0:T(8,128)(2,1)S(1)}, u32[]{:S(2)}, u32[]{:S(2)}) collective-permute-start(bf16[3,128,256]{2,1,0:T(8,128)(2,1)S(1)} %get-tuple-element.5), channel_id=1, source_target_pairs={{0,96},{8,104},{16,112},{24,120},{1,97},{9,105},{17,113},{25,121},... | collective-permute-start | bytes 589832 | tf_op jit(solution)/shard_map/ppermute | solution.py:162
  14.1 17.1 %collective-permute-start.4 = (bf16[3,128,256]{2,1,0:T(8,128)(2,1)S(1)}, bf16[3,128,256]{2,1,0:T(8,128)(2,1)S(1)}, u32[]{:S(2)}, u32[]{:S(2)}) collective-permute-start(bf16[3,128,256]{2,1,0:T(8,128)(2,1)S(1)} %get-tuple-element.5), channel_id=1, source_target_pairs={{0,80},{8,88},{16,96},{24,104},{32,112},{40,120},{1,81},{9,89},{17... | collective-permute-start | bytes 589832 | tf_op jit(solution)/shard_map/ppermute | solution.py:162
  15.4 15.7 %collective-permute-start.3 = (bf16[3,128,256]{2,1,0:T(8,128)(2,1)S(1)}, bf16[3,128,256]{2,1,0:T(8,128)(2,1)S(1)}, u32[]{:S(2)}, u32[]{:S(2)}) collective-permute-start(bf16[3,128,256]{2,1,0:T(8,128)(2,1)S(1)} %get-tuple-element.5), channel_id=1, source_target_pairs={{0,64},{8,72},{16,80},{24,88},{32,96},{40,104},{48,112},{56,120},{... | collective-permute-start | bytes 589832 | tf_op jit(solution)/shard_map/ppermute | solution.py:162
  20.2 10.9 %collective-permute-start.2 = (bf16[3,128,256]{2,1,0:T(8,128)(2,1)S(1)}, bf16[3,128,256]{2,1,0:T(8,128)(2,1)S(1)}, u32[]{:S(2)}, u32[]{:S(2)}) collective-permute-start(bf16[3,128,256]{2,1,0:T(8,128)(2,1)S(1)} %get-tuple-element.5), channel_id=1, source_target_pairs={{0,48},{8,56},{16,64},{24,72},{32,80},{40,88},{48,96},{56,104},{64... | collective-permute-start | bytes 589832 | tf_op jit(solution)/shard_map/ppermute | solution.py:162
  22.7 15.8 %collective-permute-start.6 = (bf16[3,128,256]{2,1,0:T(8,128)(2,1)S(1)}, bf16[3,128,256]{2,1,0:T(8,128)(2,1)S(1)}, u32[]{:S(2)}, u32[]{:S(2)}) collective-permute-start(bf16[3,128,256]{2,1,0:T(8,128)(2,1)S(1)} %get-tuple-element.5), channel_id=1, source_target_pairs={{0,112},{8,120},{1,113},{9,121},{2,114},{10,122},{3,115},{11,123},... | collective-permute-start | bytes 589832 | tf_op jit(solution)/shard_map/ppermute | solution.py:162
  38.5 3.5 %collective-permute-start.7 = (bf16[24,128,256]{2,1,0:T(8,128)(2,1)S(1)}, bf16[24,128,256]{2,1,0:T(8,128)(2,1)S(1)}, u32[]{:S(2)}, u32[]{:S(2)}) collective-permute-start(bf16[24,128,256]{2,1,0:T(8,128)(2,1)S(1)} %constant_dynamic-update-slice_fusion.mine), channel_id=1, source_target_pairs={{0,8},{8,0},{16,24},{24,16},{32,40},{40,32},{48,56},{56,48},{64,72... | collective-permute-start | bytes 4718600 | tf_op jit(solution)/shard_map/ppermute | solution.py:164
  42.0 1.1 copy-start
  43.1 39.5 %copy-start.4 = (bf16[1024,8192]{1,0:T(8,128)(2,1)S(1)}, bf16[1024,8192]{1,0:T(8,128)(2,1)}, u32[]{:S(2)}) copy-start(bf16[1024,8192]{1,0:T(8,128)(2,1)} %param.16) | copy-start | bytes 50331652
  91.3 74.9 %copy-start.3 = (f32[1024]{0:T(1024)S(1)}, f32[1024]{0:T(1024)}, u32[]{:S(2)}) copy-start(f32[1024]{0:T(1024)} %param.17) | copy-start | bytes 12292
Sparse Core Ops, SparseCore 0:
  91.4 74.6 reduce-scatter.1

commit v2 on v1

v2 whole, which is shorter than its diff:
```python
import math

import jax
import jax.numpy as jnp
from jax import lax
from jax.experimental import pallas as pl
from jax.experimental.pallas import tpu as pltpu
from jax.sharding import PartitionSpec as P

HD = 128
GROUP = 8
BLK = 128
RANK_BLOCKS = 3
CHIPS = 8
DEPTH = 4
HEADS = 8
WIDE = GROUP * HD
QSCALE = math.log2(math.e) / math.sqrt(HD)
F32 = jnp.float32
BF16 = jnp.bfloat16
CHUNKS = ((0, 2), (2, 1))
VMEM = 56 << 20
PARTS = 2


def fold_blocks(count, causal, kv, qt, qrow, top, total, accum):
    keys = jnp.concatenate([kv[b, :, :HD] for b in range(count)], axis=0)
    vals_t = jnp.concatenate([kv[b, :, HD:] for b in range(count)], axis=1)
    span = 2 * BLK
    steps = WIDE // span
    raws = [
        jnp.dot(keys, qt[:, pl.ds(step * span, span)], preferred_element_type=F32)
        for step in range(steps)
    ]
    for step in range(steps):
        cols = pl.ds(step * span, span)
        scores = raws[step] * qrow[:, cols]
        if causal:
            key_at = lax.broadcasted_iota(jnp.int32, (BLK, span), 0)
            row_at = lax.broadcasted_iota(jnp.int32, (BLK, span), 1) % BLK
            own = jnp.where(key_at <= row_at, scores[:BLK], -jnp.inf)
            scores = jnp.concatenate([own, scores[BLK:]], axis=0) if count > 1 else own
            new_top = jnp.max(scores, axis=0, keepdims=True)
            expo = jnp.exp2(scores - new_top)
            total[:, cols] = jnp.sum(expo, axis=0, keepdims=True)
            accum[:, cols] = jnp.dot(vals_t, expo.astype(BF16), preferred_element_type=F32)
        else:
            old_top = top[:, cols]
            new_top = jnp.maximum(old_top, jnp.max(scores, axis=0, keepdims=True))
            expo = jnp.exp2(scores - new_top)
            decay = jnp.exp2(old_top - new_top)
            total[:, cols] = total[:, cols] * decay + jnp.sum(expo, axis=0, keepdims=True)
            accum[:, cols] = accum[:, cols] * decay + jnp.dot(
                vals_t, expo.astype(BF16), preferred_element_type=F32
            )
        top[:, cols] = new_top


def attend_rows(
    first, place, mask, q_ref, qs_ref, mine, other, kv, qt, qrow, top, total, accum, todo, sems
):
    chip, core = place[0], place[1]
    row_block = place[2] + pl.program_id(0)
    column = lax.rem(chip, 2) if first else 1 - lax.rem(chip, 2)
    base = 1 if first else 0

    def fetch(block, slot, at):
        owner = block // RANK_BLOCKS
        index = (chip // 2 - owner // 4) * RANK_BLOCKS + block % RANK_BLOCKS
        for same, source in ((True, mine), (False, other)):

            @pl.when((owner % 2 == core) == same)
            def _():
                pltpu.make_async_copy(source.at[index], kv.at[slot, at], sems.at[slot, at]).start()

    def arrive(slot, at):
        pltpu.make_async_copy(mine.at[0], kv.at[slot, at], sems.at[slot, at]).wait()

    if first:
        fetch(row_block, 0, 0)

    def list_block(block, count):
        todo[count] = block
        wanted = lax.rem(block // (2 * RANK_BLOCKS), 2) == column
        return count + jnp.where(wanted, mask[row_block, block], 0)

    count = lax.fori_loop(0, row_block, list_block, jnp.int32(0))
    rest = count % DEPTH
    full = count // DEPTH
    for at in range(DEPTH - 1):

        @pl.when(at < rest)
        def _():
            fetch(todo[at], 0, at + base)

    def fetch_group(step, slot):
        for at in range(DEPTH):
            fetch(todo[rest + step * DEPTH + at], slot, at)

    @pl.when(full > 0)
    def _():
        fetch_group(0, 1)

    scale = qs_ref[...].astype(F32).T * QSCALE
    for head in range(GROUP):
        cols = pl.ds(head * HD, HD)
        qt[:, cols] = q_ref[:, cols].T
        qrow[:, cols] = scale[head : head + 1]

    state = (qt, qrow, top, total, accum)
    if first:
        arrive(0, 0)
    for extra in range(1 - base, DEPTH):

        @pl.when(rest == extra)
        def _():
            for at in range(extra):
                arrive(0, at + base)
            fold_blocks(extra + base, first, kv.at[0], *state)

    @pl.loop(0, full)
    def _(step):
        slot = (step + 1) % 2

        @pl.when(step + 1 < full)
        def _():
            fetch_group(step + 1, 1 - slot)

        for at in range(DEPTH):
            arrive(slot, at)
        fold_blocks(DEPTH, False, kv.at[slot], *state)


def first_kernel(
    place, mask, q_ref, qs_ref, mine, other, top, total, accum, kv, qt, qrow, todo, sems
):
    rows = (place, mask, q_ref, qs_ref, mine, other, kv, qt, qrow)
    attend_rows(True, *rows, top.at[0], total.at[0], accum.at[0], todo, sems)


def second_kernel(
    place, mask, q_ref, qs_ref, mine, other, top_in, total_in, accum_in, o_ref,
    kv, qt, qrow, top, total, accum, todo, sems,
):
    top[...] = top_in[0]
    total[...] = total_in[0]
    accum[...] = accum_in[0]
    rows = (place, mask, q_ref, qs_ref, mine, other, kv, qt, qrow)
    attend_rows(False, *rows, top, total, accum, todo, sems)
    for head in range(GROUP):
        cols = pl.ds(head * HD, HD)
        o_ref[:, cols] = (accum[:, cols] * (1.0 / total[:, cols])).astype(BF16).T


def attend(place, mask, queries, query_scale, mine, other, chunk, state):
    first, count = chunk
    blocks = mask.shape[0]
    smem = pl.BlockSpec(memory_space=pltpu.SMEM)
    hbm = pl.BlockSpec(memory_space=pl.ANY)
    in_specs = [
        smem,
        smem,
        pl.BlockSpec((BLK, WIDE), lambda i: (first + i, 0)),
        pl.BlockSpec((BLK, GROUP), lambda i: (first + i, 0)),
        hbm,
        hbm,
    ]
    row = pltpu.VMEM((1, WIDE), F32)
    held = [
        pl.BlockSpec((1, 1, WIDE), lambda i: (first + i, 0, 0)),
        pl.BlockSpec((1, 1, WIDE), lambda i: (first + i, 0, 0)),
        pl.BlockSpec((1, HD, WIDE), lambda i: (first + i, 0, 0)),
    ]
    kv = [pltpu.VMEM((2, DEPTH, BLK, 2 * HD), BF16), pltpu.VMEM((HD, WIDE), BF16), row]
    tail = [pltpu.SMEM((blocks,), jnp.int32), pltpu.SemaphoreType.DMA((2, DEPTH))]
    common = dict(
        grid=(count,),
        compiler_params=pltpu.CompilerParams(vmem_limit_bytes=VMEM),
        cost_estimate=pl.CostEstimate(
            flops=count * BLK * WIDE * 4 * 2500,
            bytes_accessed=count * blocks * BLK * HD * 2,
            transcendentals=count * BLK * GROUP * 2500,
        ),
    )
    args = (
        place + jnp.array([0, 0, first], jnp.int32),
        mask,
        queries,
        query_scale,
        mine,
        other,
    )
    if state is None:
        return pl.pallas_call(
            first_kernel,
            in_specs=in_specs,
            out_specs=held,
            out_shape=[
                jax.ShapeDtypeStruct((count, 1, WIDE), F32),
                jax.ShapeDtypeStruct((count, 1, WIDE), F32),
                jax.ShapeDtypeStruct((count, HD, WIDE), F32),
            ],
            scratch_shapes=kv + tail,
            name="attend_first",
            **common,
        )(*args)
    return pl.pallas_call(
        second_kernel,
        in_specs=in_specs + held,
        out_specs=pl.BlockSpec((BLK, WIDE), lambda i: (i, 0)),
        out_shape=jax.ShapeDtypeStruct((count * BLK, WIDE), BF16),
        scratch_shapes=kv + [row, row, pltpu.VMEM((HD, WIDE), F32)] + tail,
        name="attend_second",
        **common,
    )(*args, *state)


def pack(keys, key_scale, values, value_scale):
    scaled_k = keys.astype(F32) * key_scale.astype(F32)
    scaled_v = values.astype(F32) * value_scale.astype(F32)
    k3 = scaled_k.astype(BF16).reshape(RANK_BLOCKS, BLK, HD)
    v3 = jnp.transpose(scaled_v.astype(BF16).reshape(RANK_BLOCKS, BLK, HD), (0, 2, 1))
    return jnp.concatenate([k3, v3], axis=2)


CORE_SWAP = [(i, i ^ 1) for i in range(2 * CHIPS)]


def along_x(block):
    got = [block]
    for shift in range(1, 4):
        pairs = [(4 * x + i, 4 * (x + shift) + i) for x in range(4 - shift) for i in range(4)]
        got.append(lax.ppermute(block, "ctx", pairs))
    return got


def with_core(got):
    mine = jnp.concatenate(got, axis=0)
    return mine, lax.ppermute(mine, "ctx", CORE_SWAP)


def across_y():
    pairs = []
    for x in range(4):
        for y in range(4):
            for core in range(2):
                for z in range(4):
                    far = (y + (1 if core == 0 else 3)) % 4
                    start = ((x * 2 + y // 2) * 2 + core) * HEADS + (y % 2) * 4 + z
                    end = ((x * 2 + far // 2) * 2 + core) * HEADS + (far % 2) * 4 + z
                    pairs.append((start, end))
    return pairs


def cut_weights(weight, core, half):
    rows, width = weight.shape
    keep = rows // 2
    return lax.dynamic_slice(weight, (core * keep, (1 - half) * (width // 2)), (keep, width // 2))


def project_kernel(info, *refs):
    chunks = len(CHUNKS)
    own, near, far = refs[:chunks], refs[chunks : 2 * chunks], refs[2 * chunks : 3 * chunks]
    w_own, w_near, w_far = refs[3 * chunks : 3 * chunks + 3]
    outs = refs[3 * chunks + 3 :]
    for at, (first, count) in enumerate(CHUNKS):
        value = jnp.dot(own[at][...], w_own[...], preferred_element_type=F32)
        value += jnp.dot(near[at][...], w_near[...], preferred_element_type=F32)
        value += jnp.dot(far[at][...], w_far[...], preferred_element_type=F32)
        value = value.astype(BF16)
        for shift, out in enumerate(outs):

            @pl.when(pl.program_id(0) == shift)
            def _():
                out[pl.ds(first * BLK, count * BLK), :] = value


def project(info, own, partner, weight, near, far, part):
    tile = weight.shape[1] // HEADS // PARTS
    keep = weight.shape[0] // 2
    rows = RANK_BLOCKS * BLK
    high = [count * BLK for _, count in CHUNKS]

    def target(s, info):
        return lax.rem(info[1] + s, 4)

    def other_tile(s, info):
        return (0, target(s, info) * PARTS + part)

    return pl.pallas_call(
        project_kernel,
        grid_spec=pltpu.PrefetchScalarGridSpec(
            num_scalar_prefetch=1,
            grid=(4,),
            in_specs=[pl.BlockSpec((h, WIDE), lambda s, info: (0, 0)) for h in high]
            + [pl.BlockSpec((h, keep), lambda s, info: (0, info[2])) for h in high]
            + [pl.BlockSpec((h, keep), lambda s, info: (0, 1 - info[2])) for h in high]
            + [
                pl.BlockSpec(
                    (WIDE, tile),
                    lambda s, info: (0, (info[0] * 4 + target(s, info)) * PARTS + part),
                ),
                pl.BlockSpec((keep, tile), other_tile),
                pl.BlockSpec((keep, tile), other_tile),
            ],
            out_specs=[pl.BlockSpec((rows, tile), lambda s, info: (0, 0))] * 4,
        ),
        out_shape=[jax.ShapeDtypeStruct((rows, tile), BF16)] * 4,
        compiler_params=pltpu.CompilerParams(vmem_limit_bytes=VMEM),
        cost_estimate=pl.CostEstimate(
            flops=2 * rows * 2 * WIDE * 4 * tile,
            bytes_accessed=2 * WIDE * 4 * tile * 2 + rows * WIDE * 8,
            transcendentals=0,
        ),
        name="project",
    )(info, *own, *partner, *partner, weight, near, far)


def local(
    queries, query_scale, keys, key_scale, values, value_scale, block_mask, out_weight, out_scale
):
    rank = lax.axis_index("ctx").astype(jnp.int32)
    head = lax.axis_index("head").astype(jnp.int32)
    place = jnp.stack([rank // 2, rank % 2, rank * RANK_BLOCKS])
    info = jnp.stack([head // 4, head % 4, rank % 2])
    packed = pack(keys, key_scale, values, value_scale)
    beside = lax.ppermute(packed, "ctx", [(i, i ^ 2) for i in range(2 * CHIPS)])
    cut = cut_weights(out_weight, rank % 2, head // 4)
    cut, beside = lax.optimization_barrier((cut, beside))
    near = lax.ppermute(cut, ("ctx", "head"), across_y())
    first_kv = with_core(along_x(packed))
    state = attend(
        place, block_mask, queries, query_scale, *first_kv, (0, RANK_BLOCKS), None
    )
    later, state = lax.optimization_barrier((along_x(beside), state))
    second_kv = with_core(later)
    own, partner = [], []
    for chunk in CHUNKS:
        rows = attend(place, block_mask, queries, query_scale, *second_kv, chunk, state)
        if not own:
            near, rows = lax.optimization_barrier((near, rows))
            far = lax.ppermute(near, "ctx", CORE_SWAP)
        own.append(rows)
        partner.append(lax.ppermute(rows, "head", [(i, i ^ 4) for i in range(HEADS)]))
    parts = []
    for part in range(PARTS):
        sums = project(info, own, partner, out_weight, near, far, part)
        total = sums[0].astype(F32)
        for shift in range(1, 4):
            pairs = [(i, i // 4 * 4 + (i + shift) % 4) for i in range(HEADS)]
            total += lax.ppermute(sums[shift], "head", pairs).astype(F32)
        parts.append(total)
    return (jnp.concatenate(parts, axis=1) * out_scale[None, :]).astype(BF16)


def solution(mesh):
    return jax.shard_map(
        local,
        mesh=mesh,
        in_specs=(
            P("ctx", "head"),
            P("ctx", "head"),
            P("ctx", "head"),
            P("ctx", "head"),
            P("ctx", "head"),
            P("ctx", "head"),
            P(),
            P("head", None),
            P("head"),
        ),
        out_specs=P("ctx", "head"),
        check_vma=False,
    )
```

time: 177 us -> 137 us (0.77)
  waiting for transfers between devices: 97 us -> 44.1 us
  starting transfers between devices: 9.11 us -> 27.7 us
  between operations: 13.6 us -> 0.28 us
  Pallas kernels: 39.4 us -> 49.7 us
  matrix products: 8.72 us -> 0 us
  local copies, waits for them, and re-layouts: 1.54 us -> 8.42 us
    reduce_scatter x1 -> x0, waiting for transfers between devices: 74.8 us -> none  [local(): lax.psum_scatter(projected.astype(BF16), 'head', scatter_dimension=1, til...]
    ppermute x8 -> x19, waiting for transfers between devices: 22.2 us -> 44.1 us  [the longest x6 21.6 us: local(): total += lax.ppermute(sums[shift], 'head', pairs).astype(F32)]
    ppermute x8 -> x19, starting transfers between devices: 9.11 us -> 27.7 us  [the longest x6 9.62 us: local(): total += lax.ppermute(sums[shift], 'head', pairs).astype(F32)]
    pallas_call x1 -> x5, Pallas kernels: 39.4 us -> 49.7 us  [the longest x2 19.3 us: attend(): pl.pallas_call(second_kernel, in_specs=in_specs + held, out_specs=pl.Bloc...]
    dot_general x1 -> x0, matrix products: 8.72 us -> none  [local(): projected = jnp.dot(attended, out_weight, preferred_element_type=F32)]
    dynamic_slice x0 -> x1, local copies, waits for them, and re-layouts: none -> 4.72 us  [cut_weights(): lax.dynamic_slice(weight, (core * keep, (1 - half) * (width // 2)), (keep...]
    unnamed x17 -> x26, local copies, waits for them, and re-layouts: 1.4 us -> 3.56 us
  transfers between devices with their start and end apart: 9 -> 19, of which waited for: 7 -> 9; matrix products, arithmetic and copies ran while one was open for 0% -> 5% of each run, Pallas kernels for 0% -> 30%
where the time goes in v2:
time: 137 us
  Pallas kernels  49.7 us (36%)
  waiting for transfers between devices  44.1 us (32%)
  starting transfers between devices  27.7 us (20%)
  local copies, waits for them, and re-layouts  8.42 us (6%)
  other arithmetic  6.24 us (5%)
    ppermute x6, waiting for transfers between devices, local(): total += lax.ppermute(sums[shift], 'head', pairs).astype(F32)  21.6 us
    pallas_call x2, Pallas kernels, attend(): pl.pallas_call(second_kernel, in_specs=in_specs + held, out_specs=pl.Bloc...  19.3 us
    pallas_call x2, Pallas kernels, project(): pl.pallas_call(project_kernel, grid_spec=pltpu.PrefetchScalarGridSpec(num...  18.7 us
    pallas_call x1, Pallas kernels, attend(): pl.pallas_call(first_kernel, in_specs=in_specs, out_specs=held, out_shape...  11.8 us
    ppermute x6, starting transfers between devices, local(): total += lax.ppermute(sums[shift], 'head', pairs).astype(F32)  9.62 us
    ppermute x2, waiting for transfers between devices, local(): lax.ppermute(rows, 'head', [(i, i ^ 4) for i in range(HEADS)])  9.13 us
    ppermute x6, waiting for transfers between devices, along_x(): got.append(lax.ppermute(block, 'ctx', pairs))  8.31 us
    ppermute x6, starting transfers between devices, along_x(): got.append(lax.ppermute(block, 'ctx', pairs))  7.73 us
  transfers between devices with their start and end apart: 19, of which 9 were waited for; matrix products, arithmetic and copies ran while one was open for 5% of the time, Pallas kernels for 30%

profile of v2, /device:TPU:22, one launch (start us, length us, event | category | flops | bytes accessed | tf_op | source)
XLA Modules:
  0.0 136.5 jit_solution(3628693364550366561)
XLA Ops:
  0.0 0.7 convert_reduce_fusion
  0.7 1.0 multiply_convert_fusion
  1.7 0.1 copy.16
  1.8 0.7 convert_reduce_fusion.1
  2.5 1.0 multiply_convert_fusion.1
  3.6 0.4 collective-permute-start
  4.0 4.7 %dynamic_slice.3 = bf16[512,4096]{1,0:T(8,128)(2,1)} dynamic-slice(bf16[1024,8192]{1,0:T(8,128)(2,1)} %refs_6_.3, s32[]{:T(128)S(6)} %select_n.32, s32[]{:T(128)S(6)} %select_n.33), dynamic_slice_sizes={512,4096} | dynamic-slice | bytes 8388612 | tf_op jit(solution)/shard_map/dynamic_slice | solution.py:258
  8.7 3.1 %collective-permute-done = bf16[3,128,256]{2,1,0:T(8,128)(2,1)S(1)} collective-permute-done((bf16[3,128,256]{2,1,0:T(8,128)(2,1)S(1)}, bf16[3,128,256]{2,1,0:T(8,128)(2,1)S(1)}, u32[]{:S(2)}, u32[]{:S(2)}) %collective-permute-start) | collective-permute-done | bytes 196640 | tf_op jit(solution)/shard_map/ppermute | solution.py:327
  11.8 1.3 collective-permute-start.1
  13.1 1.3 collective-permute-start.7
  14.4 1.3 collective-permute-start.6
  15.7 1.3 collective-permute-start.5
  17.0 8.1 %collective-permute-done.7 = bf16[3,128,256]{2,1,0:T(8,128)(2,1)S(1)} collective-permute-done((bf16[3,128,256]{2,1,0:T(8,128)(2,1)S(1)}, bf16[3,128,256]{2,1,0:T(8,128)(2,1)S(1)}, u32[]{:S(2)}, u32[]{:S(2)}) %collective-permute-start.7) | collective-permute-done | bytes 196640 | tf_op jit(solution)/shard_map/ppermute | solution.py:233
  25.1 0.1 pad_maximum_fusion.mine
  25.2 0.1 collective-permute-start.8
  25.3 0.8 copy.18.qs_ref
  26.1 0.6 fusion.1
  26.8 1.3 collective-permute-start.2
  28.1 1.3 collective-permute-start.3
  29.4 1.3 collective-permute-start.4
  30.7 0.9 copy-done.9
  31.6 11.8 %attend_first.1 = (f32[3,1,1024]{2,1,0:T(1,128)}, f32[3,1,1024]{2,1,0:T(1,128)}, f32[3,128,1024]{2,1,0:T(8,128)}) custom-call(s32[3]{0:T(128)} %get-tuple-element.50.place, s32[48,48]{1,0:T(8,128)} %mask.5, bf16[384,1024]{1,0:T(8,128)(2,1)} %q_ref.5, bf16[384,8]{1,0:T(8,128)(2,1)} %copy.18.qs_ref, bf16[12,128,256]{2,1,0:T(8,128)(2,1)} %copy-done.2, ...), custom_call_target="tpu_custom_call" | custom-call | flops 3932160000 | bytes 4718592 | tf_op jit(solution)/shard_map/attend_first/pallas_call | solution.py:194
  43.4 0.2 collective-permute-done.4
  43.7 4.4 %collective-permute-start.9 = (bf16[12,128,256]{2,1,0:T(8,128)(2,1)S(1)}, bf16[12,128,256]{2,1,0:T(8,128)(2,1)S(1)}, u32[]{:S(2)}, u32[]{:S(2)}) collective-permute-start(bf16[12,128,256]{2,1,0:T(8,128)(2,1)S(1)} %constant_dynamic-update-slice_fusion.mine), channel_id=1, source_target_pairs={{0,8},{8,0},{16,24},{24,16},{32,40},{40,32},{48,56},{56,48},{64,72... | collective-permute-start | bytes 2359304 | tf_op jit(solution)/shard_map/ppermute | solution.py:239
  48.1 1.9 %collective-permute-done.9.other = bf16[12,128,256]{2,1,0:T(8,128)(2,1)S(1)} collective-permute-done((bf16[12,128,256]{2,1,0:T(8,128)(2,1)S(1)}, bf16[12,128,256]{2,1,0:T(8,128)(2,1)S(1)}, u32[]{:S(2)}, u32[]{:S(2)}) %collective-permute-start.9) | collective-permute-done | bytes 786464 | tf_op jit(solution)/shard_map/ppermute | solution.py:239
  50.0 0.9 copy-done.10
  50.9 11.6 %attend_second.2.refs_0_ = bf16[256,1024]{1,0:T(8,128)(2,1)} custom-call(s32[3]{0:T(128)} %get-tuple-element.50.place, s32[48,48]{1,0:T(8,128)} %mask.5, bf16[384,1024]{1,0:T(8,128)(2,1)} %q_ref.5, bf16[384,8]{1,0:T(8,128)(2,1)} %copy.18.qs_ref, bf16[12,128,256]{2,1,0:T(8,128)(2,1)} %copy-done.5, bf16[12,128,256]{2,1,0:T(8,128)(2,1)} %copy-done.10, ...), custom_call_target="tpu_custom_call" | custom-call | flops 2621440000 | bytes 3145728 | tf_op jit(solution)/shard_map/attend_second/pallas_call | solution.py:207
  62.6 1.9 %collective-permute-start.12 = (bf16[512,4096]{1,0:T(8,128)(2,1)}, bf16[512,4096]{1,0:T(8,128)(2,1)}, u32[]{:S(2)}, u32[]{:S(2)}) collective-permute-start(bf16[512,4096]{1,0:T(8,128)(2,1)} %collective-permute-done.1.refs_7_), channel_id=1, source_target_pairs={{0,8},{8,0},{16,24},{24,16},{32,40},{40,32},{48,56},{56,48},{64,72... | collective-permute-start | bytes 12582920 | tf_op jit(solution)/shard_map/ppermute | solution.py:342
  64.5 1.6 %collective-permute-start.10 = (bf16[256,1024]{1,0:T(8,128)(2,1)}, bf16[256,1024]{1,0:T(8,128)(2,1)S(1)}, u32[]{:S(2)}, u32[]{:S(2)}) collective-permute-start(bf16[256,1024]{1,0:T(8,128)(2,1)} %attend_second.2.refs_0_), channel_id=1, source_target_pairs={{0,4},{1,5},{2,6},{3,7},{4,0},{5,1},{6,2},{7,3},{8,12},{9,13},{10,... | collective-permute-start | bytes 1572872 | tf_op jit(solution)/shard_map/ppermute | solution.py:344
  66.1 7.7 %attend_second.3.refs_1_ = bf16[128,1024]{1,0:T(8,128)(2,1)} custom-call(s32[3]{0:T(128)} %get-tuple-element.49.place, s32[48,48]{1,0:T(8,128)} %mask.5, bf16[384,1024]{1,0:T(8,128)(2,1)} %q_ref.5, bf16[384,8]{1,0:T(8,128)(2,1)} %copy.18.qs_ref, bf16[12,128,256]{2,1,0:T(8,128)(2,1)} %copy-done.5, bf16[12,128,256]{2,1,0:T(8,128)(2,1)} %copy-done.10, ...), custom_call_target="tpu_custom_call" | custom-call | flops 1310720000 | bytes 1572864 | tf_op jit(solution)/shard_map/attend_second/pallas_call | solution.py:207
  73.7 0.7 collective-permute-start.11
  74.5 0.7 pad_add_fusion.info
  75.1 9.1 %collective-permute-done.11.refs_3_.refs_5_ = bf16[128,1024]{1,0:T(8,128)(2,1)S(1)} collective-permute-done((bf16[128,1024]{1,0:T(8,128)(2,1)}, bf16[128,1024]{1,0:T(8,128)(2,1)S(1)}, u32[]{:S(2)}, u32[]{:S(2)}) %collective-permute-start.11) | collective-permute-done | bytes 262176 | tf_op jit(solution)/shard_map/ppermute | solution.py:344
  84.3 0.7 copy-done.1
  84.9 0.2 copy-done
  85.1 9.4 %project.3 = (bf16[384,512]{1,0:T(8,128)(2,1)}, bf16[384,512]{1,0:T(8,128)(2,1)}, bf16[384,512]{1,0:T(8,128)(2,1)}, bf16[384,512]{1,0:T(8,128)(2,1)}) custom-call(s32[3]{0:T(128)} %pad_add_fusion.info, bf16[256,1024]{1,0:T(8,128)(2,1)} %attend_second.2.refs_0_, bf16[128,1024]{1,0:T(8,128)(2,1)} %attend_second.3.refs_1_, bf16[256,1024]{1,0:T(8,128)(2,1)} %copy-done, ...), custom_call_target="tpu_custom_call" | custom-call | flops 3221225472 | bytes 11534336 | tf_op jit(solution)/shard_map/project/pallas_call | solution.py:290
  94.5 4.0 %collective-permute-start.18 = (bf16[384,512]{1,0:T(8,128)(2,1)}, bf16[384,512]{1,0:T(8,128)(2,1)S(1)}, u32[]{:S(2)}, u32[]{:S(2)}) collective-permute-start(bf16[384,512]{1,0:T(8,128)(2,1)} %get-tuple-element.48), channel_id=1, source_target_pairs={{0,3},{1,0},{2,1},{3,2},{4,7},{5,4},{6,5},{7,6},{8,11},{9,8},{10,9... | collective-permute-start | bytes 1179656 | tf_op jit(solution)/shard_map/ppermute | solution.py:351
  98.5 1.3 collective-permute-start.16
  99.8 9.3 %project.2 = (bf16[384,512]{1,0:T(8,128)(2,1)}, bf16[384,512]{1,0:T(8,128)(2,1)}, bf16[384,512]{1,0:T(8,128)(2,1)}, bf16[384,512]{1,0:T(8,128)(2,1)}) custom-call(s32[3]{0:T(128)} %pad_add_fusion.info, bf16[256,1024]{1,0:T(8,128)(2,1)} %attend_second.2.refs_0_, bf16[128,1024]{1,0:T(8,128)(2,1)} %attend_second.3.refs_1_, bf16[256,1024]{1,0:T(8,128)(2,1)} %copy-done, ...), custom_call_target="tpu_custom_call" | custom-call | flops 3221225472 | bytes 11534336 | tf_op jit(solution)/shard_map/project/pallas_call | solution.py:290
  109.1 2.0 %collective-permute-start.15 = (bf16[384,512]{1,0:T(8,128)(2,1)}, bf16[384,512]{1,0:T(8,128)(2,1)S(1)}, u32[]{:S(2)}, u32[]{:S(2)}) collective-permute-start(bf16[384,512]{1,0:T(8,128)(2,1)} %get-tuple-element.44), channel_id=1, source_target_pairs={{0,3},{1,0},{2,1},{3,2},{4,7},{5,4},{6,5},{7,6},{8,11},{9,8},{10,9... | collective-permute-start | bytes 1179656 | tf_op jit(solution)/shard_map/ppermute | solution.py:351
  111.1 2.3 %collective-permute-start.14 = (bf16[384,512]{1,0:T(8,128)(2,1)}, bf16[384,512]{1,0:T(8,128)(2,1)S(1)}, u32[]{:S(2)}, u32[]{:S(2)}) collective-permute-start(bf16[384,512]{1,0:T(8,128)(2,1)} %get-tuple-element.43), channel_id=1, source_target_pairs={{0,2},{1,3},{2,0},{3,1},{4,6},{5,7},{6,4},{7,5},{8,10},{9,11},{10,... | collective-permute-start | bytes 1179656 | tf_op jit(solution)/shard_map/ppermute | solution.py:351
  113.4 3.4 %collective-permute-done.18 = bf16[384,512]{1,0:T(8,128)(2,1)S(1)} collective-permute-done((bf16[384,512]{1,0:T(8,128)(2,1)}, bf16[384,512]{1,0:T(8,128)(2,1)S(1)}, u32[]{:S(2)}, u32[]{:S(2)}) %collective-permute-start.18) | collective-permute-done | bytes 393248 | tf_op jit(solution)/shard_map/ppermute | solution.py:351
  116.8 8.5 %collective-permute-done.16 = bf16[384,512]{1,0:T(8,128)(2,1)S(1)} collective-permute-done((bf16[384,512]{1,0:T(8,128)(2,1)}, bf16[384,512]{1,0:T(8,128)(2,1)S(1)}, u32[]{:S(2)}, u32[]{:S(2)}) %collective-permute-start.16) | collective-permute-done | bytes 393248 | tf_op jit(solution)/shard_map/ppermute | solution.py:351
  125.3 0.2 convert_add_fusion
  125.6 6.4 %collective-permute-done.15 = bf16[384,512]{1,0:T(8,128)(2,1)S(1)} collective-permute-done((bf16[384,512]{1,0:T(8,128)(2,1)}, bf16[384,512]{1,0:T(8,128)(2,1)S(1)}, u32[]{:S(2)}, u32[]{:S(2)}) %collective-permute-start.15) | collective-permute-done | bytes 393248 | tf_op jit(solution)/shard_map/ppermute | solution.py:351
  131.9 3.3 %collective-permute-done.13 = bf16[384,512]{1,0:T(8,128)(2,1)S(1)} collective-permute-done((bf16[384,512]{1,0:T(8,128)(2,1)}, bf16[384,512]{1,0:T(8,128)(2,1)S(1)}, u32[]{:S(2)}, u32[]{:S(2)}) %collective-permute-start.13) | collective-permute-done | bytes 393248 | tf_op jit(solution)/shard_map/ppermute | solution.py:351
  135.2 0.2 convert_add_fusion.1
  135.5 1.0 fusion
  (35 shorter events, 0.2 us)
Async XLA Ops:
  3.6 8.2 %collective-permute-start = (bf16[3,128,256]{2,1,0:T(8,128)(2,1)S(1)}, bf16[3,128,256]{2,1,0:T(8,128)(2,1)S(1)}, u32[]{:S(2)}, u32[]{:S(2)}) collective-permute-start(bf16[3,128,256]{2,1,0:T(8,128)(2,1)S(1)} %pad_maximum_fusion.1), channel_id=1, source_target_pairs={{0,16},{8,24},{16,0},{24,8},{32,48},{40,56},{48,32},{56,40},{64,80... | collective-permute-start | bytes 589832 | tf_op jit(solution)/shard_map/ppermute | solution.py:327
  8.7 16.5 %copy-start.6 = (bf16[384,8]{0,1:T(8,128)(2,1)S(1)}, bf16[384,8]{0,1:T(8,128)(2,1)}, u32[]{:S(2)}) copy-start(bf16[384,8]{0,1:T(8,128)(2,1)} %param.13) | copy-start | bytes 18436
  8.7 17.4 %copy-start.8 = (s32[3]{0:T(128)S(1)}, s32[3]{0:T(128)}, u32[]{:S(2)}) copy-start(s32[3]{0:T(128)} %constant.73.clone) | copy-start | bytes 40
  11.8 50.7 %collective-permute-start.1 = (bf16[512,4096]{1,0:T(8,128)(2,1)}, bf16[512,4096]{1,0:T(8,128)(2,1)}, u32[]{:S(2)}, u32[]{:S(2)}) collective-permute-start(bf16[512,4096]{1,0:T(8,128)(2,1)} %dynamic_slice.3), channel_id=1, source_target_pairs={{0,4},{1,5},{2,6},{3,7},{8,28},{9,29},{10,30},{11,31},{4,16},{5,17... | collective-permute-start | bytes 12582920 | tf_op jit(solution)/shard_map/ppermute | solution.py:330
  13.1 12.0 %collective-permute-start.7 = (bf16[3,128,256]{2,1,0:T(8,128)(2,1)S(1)}, bf16[3,128,256]{2,1,0:T(8,128)(2,1)S(1)}, u32[]{:S(2)}, u32[]{:S(2)}) collective-permute-start(bf16[3,128,256]{2,1,0:T(8,128)(2,1)S(1)} %pad_maximum_fusion.1), channel_id=1, source_target_pairs={{0,96},{8,104},{16,112},{24,120},{1,97},{9,105},{17,113},{25,121},... | collective-permute-start | bytes 589832 | tf_op jit(solution)/shard_map/ppermute | solution.py:233
  14.4 10.7 %collective-permute-start.6 = (bf16[3,128,256]{2,1,0:T(8,128)(2,1)S(1)}, bf16[3,128,256]{2,1,0:T(8,128)(2,1)S(1)}, u32[]{:S(2)}, u32[]{:S(2)}) collective-permute-start(bf16[3,128,256]{2,1,0:T(8,128)(2,1)S(1)} %pad_maximum_fusion.1), channel_id=1, source_target_pairs={{0,64},{8,72},{16,80},{24,88},{32,96},{40,104},{48,112},{56,120},{... | collective-permute-start | bytes 589832 | tf_op jit(solution)/shard_map/ppermute | solution.py:233
  15.7 9.4 %collective-permute-start.5 = (bf16[3,128,256]{2,1,0:T(8,128)(2,1)S(1)}, bf16[3,128,256]{2,1,0:T(8,128)(2,1)S(1)}, u32[]{:S(2)}, u32[]{:S(2)}) collective-permute-start(bf16[3,128,256]{2,1,0:T(8,128)(2,1)S(1)} %pad_maximum_fusion.1), channel_id=1, source_target_pairs={{0,32},{8,40},{16,48},{24,56},{32,64},{40,72},{48,80},{56,88},{64,... | collective-permute-start | bytes 589832 | tf_op jit(solution)/shard_map/ppermute | solution.py:233
  25.1 5.5 %copy-start.2 = (bf16[12,128,256]{2,1,0:T(8,128)(2,1)}, bf16[12,128,256]{2,1,0:T(8,128)(2,1)S(1)}, u32[]{:S(2)}) copy-start(bf16[12,128,256]{2,1,0:T(8,128)(2,1)S(1)} %pad_maximum_fusion.mine) | copy-start | bytes 2359300
  25.2 5.5 %collective-permute-start.8 = (bf16[12,128,256]{2,1,0:T(8,128)(2,1)S(1)}, bf16[12,128,256]{2,1,0:T(8,128)(2,1)S(1)}, u32[]{:S(2)}, u32[]{:S(2)}) collective-permute-start(bf16[12,128,256]{2,1,0:T(8,128)(2,1)S(1)} %pad_maximum_fusion.mine), channel_id=1, source_target_pairs={{0,8},{8,0},{16,24},{24,16},{32,40},{40,32},{48,56},{56,48},{64,72... | collective-permute-start | bytes 2359304 | tf_op jit(solution)/shard_map/ppermute | solution.py:239
  26.8 16.6 %collective-permute-start.2 = (bf16[3,128,256]{2,1,0:T(8,128)(2,1)S(1)}, bf16[3,128,256]{2,1,0:T(8,128)(2,1)S(1)}, u32[]{:S(2)}, u32[]{:S(2)}) collective-permute-start(bf16[3,128,256]{2,1,0:T(8,128)(2,1)S(1)} %collective-permute-done), channel_id=1, source_target_pairs={{0,32},{8,40},{16,48},{24,56},{32,64},{40,72},{48,80},{56,88},{64,... | collective-permute-start | bytes 589832 | tf_op jit(solution)/shard_map/ppermute | solution.py:233
  28.1 15.3 %collective-permute-start.3 = (bf16[3,128,256]{2,1,0:T(8,128)(2,1)S(1)}, bf16[3,128,256]{2,1,0:T(8,128)(2,1)S(1)}, u32[]{:S(2)}, u32[]{:S(2)}) collective-permute-start(bf16[3,128,256]{2,1,0:T(8,128)(2,1)S(1)} %collective-permute-done), channel_id=1, source_target_pairs={{0,64},{8,72},{16,80},{24,88},{32,96},{40,104},{48,112},{56,120},{... | collective-permute-start | bytes 589832 | tf_op jit(solution)/shard_map/ppermute | solution.py:233
  29.4 14.2 %collective-permute-start.4 = (bf16[3,128,256]{2,1,0:T(8,128)(2,1)S(1)}, bf16[3,128,256]{2,1,0:T(8,128)(2,1)S(1)}, u32[]{:S(2)}, u32[]{:S(2)}) collective-permute-start(bf16[3,128,256]{2,1,0:T(8,128)(2,1)S(1)} %collective-permute-done), channel_id=1, source_target_pairs={{0,96},{8,104},{16,112},{24,120},{1,97},{9,105},{17,113},{25,121},... | collective-permute-start | bytes 589832 | tf_op jit(solution)/shard_map/ppermute | solution.py:233
  30.7 0.9 copy-start.9
  43.7 6.3 %copy-start.5 = (bf16[12,128,256]{2,1,0:T(8,128)(2,1)}, bf16[12,128,256]{2,1,0:T(8,128)(2,1)S(1)}, u32[]{:S(2)}) copy-start(bf16[12,128,256]{2,1,0:T(8,128)(2,1)S(1)} %constant_dynamic-update-slice_fusion.mine) | copy-start | bytes 2359300
  43.7 6.3 %collective-permute-start.9 = (bf16[12,128,256]{2,1,0:T(8,128)(2,1)S(1)}, bf16[12,128,256]{2,1,0:T(8,128)(2,1)S(1)}, u32[]{:S(2)}, u32[]{:S(2)}) collective-permute-start(bf16[12,128,256]{2,1,0:T(8,128)(2,1)S(1)} %constant_dynamic-update-slice_fusion.mine), channel_id=1, source_target_pairs={{0,8},{8,0},{16,24},{24,16},{32,40},{40,32},{48,56},{56,48},{64,72... | collective-permute-start | bytes 2359304 | tf_op jit(solution)/shard_map/ppermute | solution.py:239
  50.0 0.9 copy-start.10
  62.6 21.7 %collective-permute-start.12 = (bf16[512,4096]{1,0:T(8,128)(2,1)}, bf16[512,4096]{1,0:T(8,128)(2,1)}, u32[]{:S(2)}, u32[]{:S(2)}) collective-permute-start(bf16[512,4096]{1,0:T(8,128)(2,1)} %collective-permute-done.1.refs_7_), channel_id=1, source_target_pairs={{0,8},{8,0},{16,24},{24,16},{32,40},{40,32},{48,56},{56,48},{64,72... | collective-permute-start | bytes 12582920 | tf_op jit(solution)/shard_map/ppermute | solution.py:342
  64.5 19.8 %collective-permute-start.10 = (bf16[256,1024]{1,0:T(8,128)(2,1)}, bf16[256,1024]{1,0:T(8,128)(2,1)S(1)}, u32[]{:S(2)}, u32[]{:S(2)}) collective-permute-start(bf16[256,1024]{1,0:T(8,128)(2,1)} %attend_second.2.refs_0_), channel_id=1, source_target_pairs={{0,4},{1,5},{2,6},{3,7},{4,0},{5,1},{6,2},{7,3},{8,12},{9,13},{10,... | collective-permute-start | bytes 1572872 | tf_op jit(solution)/shard_map/ppermute | solution.py:344
  73.7 10.5 %collective-permute-start.11 = (bf16[128,1024]{1,0:T(8,128)(2,1)}, bf16[128,1024]{1,0:T(8,128)(2,1)S(1)}, u32[]{:S(2)}, u32[]{:S(2)}) collective-permute-start(bf16[128,1024]{1,0:T(8,128)(2,1)} %attend_second.3.refs_1_), channel_id=1, source_target_pairs={{0,4},{1,5},{2,6},{3,7},{4,0},{5,1},{6,2},{7,3},{8,12},{9,13},{10,... | collective-permute-start | bytes 786440 | tf_op jit(solution)/shard_map/ppermute | solution.py:344
  84.2 0.7 copy-start.1
  84.2 0.9 copy-start
  94.5 22.3 %collective-permute-start.18 = (bf16[384,512]{1,0:T(8,128)(2,1)}, bf16[384,512]{1,0:T(8,128)(2,1)S(1)}, u32[]{:S(2)}, u32[]{:S(2)}) collective-permute-start(bf16[384,512]{1,0:T(8,128)(2,1)} %get-tuple-element.48), channel_id=1, source_target_pairs={{0,3},{1,0},{2,1},{3,2},{4,7},{5,4},{6,5},{7,6},{8,11},{9,8},{10,9... | collective-permute-start | bytes 1179656 | tf_op jit(solution)/shard_map/ppermute | solution.py:351
  98.5 18.3 %collective-permute-start.17 = (bf16[384,512]{1,0:T(8,128)(2,1)}, bf16[384,512]{1,0:T(8,128)(2,1)S(1)}, u32[]{:S(2)}, u32[]{:S(2)}) collective-permute-start(bf16[384,512]{1,0:T(8,128)(2,1)} %get-tuple-element.47), channel_id=1, source_target_pairs={{0,2},{1,3},{2,0},{3,1},{4,6},{5,7},{6,4},{7,5},{8,10},{9,11},{10,... | collective-permute-start | bytes 1179656 | tf_op jit(solution)/shard_map/ppermute | solution.py:351
  98.5 26.8 %copy-start.4 = (bf16[384,512]{1,0:T(8,128)(2,1)S(1)}, bf16[384,512]{1,0:T(8,128)(2,1)}, u32[]{:S(2)}) copy-start(bf16[384,512]{1,0:T(8,128)(2,1)} %get-tuple-element.45) | copy-start | bytes 1179652
  98.5 26.8 %collective-permute-start.16 = (bf16[384,512]{1,0:T(8,128)(2,1)}, bf16[384,512]{1,0:T(8,128)(2,1)S(1)}, u32[]{:S(2)}, u32[]{:S(2)}) collective-permute-start(bf16[384,512]{1,0:T(8,128)(2,1)} %get-tuple-element.46), channel_id=1, source_target_pairs={{0,1},{1,2},{2,3},{3,0},{4,5},{5,6},{6,7},{7,4},{8,9},{9,10},{10,1... | collective-permute-start | bytes 1179656 | tf_op jit(solution)/shard_map/ppermute | solution.py:351
  109.1 26.1 %copy-start.3 = (bf16[384,512]{1,0:T(8,128)(2,1)S(1)}, bf16[384,512]{1,0:T(8,128)(2,1)}, u32[]{:S(2)}) copy-start(bf16[384,512]{1,0:T(8,128)(2,1)} %get-tuple-element.41) | copy-start | bytes 1179652
  109.1 22.8 %collective-permute-start.15 = (bf16[384,512]{1,0:T(8,128)(2,1)}, bf16[384,512]{1,0:T(8,128)(2,1)S(1)}, u32[]{:S(2)}, u32[]{:S(2)}) collective-permute-start(bf16[384,512]{1,0:T(8,128)(2,1)} %get-tuple-element.44), channel_id=1, source_target_pairs={{0,3},{1,0},{2,1},{3,2},{4,7},{5,4},{6,5},{7,6},{8,11},{9,8},{10,9... | collective-permute-start | bytes 1179656 | tf_op jit(solution)/shard_map/ppermute | solution.py:351
  111.1 20.8 %collective-permute-start.14 = (bf16[384,512]{1,0:T(8,128)(2,1)}, bf16[384,512]{1,0:T(8,128)(2,1)S(1)}, u32[]{:S(2)}, u32[]{:S(2)}) collective-permute-start(bf16[384,512]{1,0:T(8,128)(2,1)} %get-tuple-element.43), channel_id=1, source_target_pairs={{0,2},{1,3},{2,0},{3,1},{4,6},{5,7},{6,4},{7,5},{8,10},{9,11},{10,... | collective-permute-start | bytes 1179656 | tf_op jit(solution)/shard_map/ppermute | solution.py:351
  116.8 18.4 %collective-permute-start.13 = (bf16[384,512]{1,0:T(8,128)(2,1)}, bf16[384,512]{1,0:T(8,128)(2,1)S(1)}, u32[]{:S(2)}, u32[]{:S(2)}) collective-permute-start(bf16[384,512]{1,0:T(8,128)(2,1)} %get-tuple-element.42), channel_id=1, source_target_pairs={{0,1},{1,2},{2,3},{3,0},{4,5},{5,6},{6,7},{7,4},{8,9},{9,10},{10,1... | collective-permute-start | bytes 1179656 | tf_op jit(solution)/shard_map/ppermute | solution.py:351
  125.5 9.9 %copy-start.7 = (f32[1024]{0:T(1024)S(1)}, f32[1024]{0:T(1024)}, u32[]{:S(2)}) copy-start(f32[1024]{0:T(1024)} %param.20) | copy-start | bytes 12292

commit v3 on v2

--- a/solution.py
+++ b/solution.py
@@ -1,3 +1,4 @@
+import functools
 import math
 
 import jax
@@ -18,7 +19,7 @@
 QSCALE = math.log2(math.e) / math.sqrt(HD)
 F32 = jnp.float32
 BF16 = jnp.bfloat16
-CHUNKS = ((0, 2), (2, 1))
+CHUNKS = ((0, 1), (1, 1), (2, 1))
 VMEM = 56 << 20
 PARTS = 2
 
@@ -101,7 +102,7 @@
     def _():
         fetch_group(0, 1)
 
-    scale = qs_ref[...].astype(F32).T * QSCALE
+    scale = qs_ref[...].astype(F32) * QSCALE
     for head in range(GROUP):
         cols = pl.ds(head * HD, HD)
         qt[:, cols] = q_ref[:, cols].T
@@ -161,7 +162,7 @@
         smem,
         smem,
         pl.BlockSpec((BLK, WIDE), lambda i: (first + i, 0)),
-        pl.BlockSpec((BLK, GROUP), lambda i: (first + i, 0)),
+        pl.BlockSpec((GROUP, BLK), lambda i: (0, first + i)),
         hbm,
         hbm,
     ]
@@ -186,7 +187,7 @@
         place + jnp.array([0, 0, first], jnp.int32),
         mask,
         queries,
-        query_scale,
+        query_scale.T,
         mine,
         other,
     )
@@ -215,12 +216,67 @@
     )(*args, *state)
 
 
+def pack_kernel(keys, key_scale, values, value_scale, packed):
+    for block in range(RANK_BLOCKS):
+        rows = pl.ds(block * BLK, BLK)
+        by_row = jnp.broadcast_to(key_scale[:, rows].astype(F32), (HD, BLK)).T
+        packed[block, :, :HD] = (keys[rows].astype(F32) * by_row).astype(BF16)
+        turned = values[rows].T.astype(F32) * value_scale[:, rows].astype(F32)
+        packed[block, :, HD:] = turned.astype(BF16)
+
+
 def pack(keys, key_scale, values, value_scale):
-    scaled_k = keys.astype(F32) * key_scale.astype(F32)
-    scaled_v = values.astype(F32) * value_scale.astype(F32)
-    k3 = scaled_k.astype(BF16).reshape(RANK_BLOCKS, BLK, HD)
-    v3 = jnp.transpose(scaled_v.astype(BF16).reshape(RANK_BLOCKS, BLK, HD), (0, 2, 1))
-    return jnp.concatenate([k3, v3], axis=2)
+    vmem = pl.BlockSpec(memory_space=pltpu.VMEM)
+    return pl.pallas_call(
+        pack_kernel,
+        in_specs=[vmem] * 4,
+        out_specs=vmem,
+        out_shape=jax.ShapeDtypeStruct((RANK_BLOCKS, BLK, 2 * HD), BF16),
+        name="pack",
+    )(keys, key_scale.T, values, value_scale.T)
+
+
+def cut_kernel(info, weight, cut, stage, in_sems, out_sems):
+    pieces, high, tile = cut.shape
+    source = pl.ds(pl.multiple_of(info[2] * high, high), high)
+
+    def copies(piece):
+        first = pl.multiple_of(((1 - info[0]) * pieces + piece) * tile, tile)
+        return (
+            pltpu.make_async_copy(
+                weight.at[source, pl.ds(first, tile)], stage.at[piece], in_sems.at[piece]
+            ),
+            pltpu.make_async_copy(stage.at[piece], cut.at[piece], out_sems.at[piece]),
+        )
+
+    loads = [copies(piece) for piece in range(pieces)]
+    for load, _ in loads:
+        load.start()
+    for load, store in loads:
+        load.wait()
+        store.start()
+    for _, store in loads:
+        store.wait()
+
+
+def cut_weights(info, weight):
+    hbm = pl.BlockSpec(memory_space=pltpu.HBM)
+    pieces = 4 * PARTS
+    shape = (pieces, weight.shape[0] // 2, weight.shape[1] // 2 // pieces)
+    return pl.pallas_call(
+        cut_kernel,
+        in_specs=[pl.BlockSpec(memory_space=pltpu.SMEM), hbm],
+        out_specs=hbm,
+        out_shape=jax.ShapeDtypeStruct(shape, BF16),
+        scratch_shapes=[
+            pltpu.VMEM(shape, BF16),
+            pltpu.SemaphoreType.DMA((pieces,)),
+            pltpu.SemaphoreType.DMA((pieces,)),
+        ],
+        compiler_params=pltpu.CompilerParams(vmem_limit_bytes=VMEM),
+        cost_estimate=pl.CostEstimate(flops=0, bytes_accessed=16 << 20, transcendentals=0),
+        name="cut",
+    )(info, weight)
 
 
 CORE_SWAP = [(i, i ^ 1) for i in range(2 * CHIPS)]
@@ -252,68 +308,136 @@
     return pairs
 
 
-def cut_weights(weight, core, half):
-    rows, width = weight.shape
-    keep = rows // 2
-    return lax.dynamic_slice(weight, (core * keep, (1 - half) * (width // 2)), (keep, width // 2))
-
-
-def project_kernel(info, *refs):
+def own_kernel(info, *refs):
     chunks = len(CHUNKS)
-    own, near, far = refs[:chunks], refs[chunks : 2 * chunks], refs[2 * chunks : 3 * chunks]
-    w_own, w_near, w_far = refs[3 * chunks : 3 * chunks + 3]
-    outs = refs[3 * chunks + 3 :]
+    own = refs[:chunks]
+    weight, out, left, held, sems = refs[chunks:]
+    tile = held.shape[2]
+
+    def copies(shift):
+        target = lax.rem(info[1] + shift, 4)
+        mine = pl.ds(pl.multiple_of((info[0] * 4 + target) * tile, tile), tile)
+        yield pltpu.make_async_copy(weight.at[:, mine], held.at[shift], sems.at[shift])
+
+    for shift in range(4):
+        for copy in copies(shift):
+            copy.start()
     for at, (first, count) in enumerate(CHUNKS):
-        value = jnp.dot(own[at][...], w_own[...], preferred_element_type=F32)
-        value += jnp.dot(near[at][...], w_near[...], preferred_element_type=F32)
-        value += jnp.dot(far[at][...], w_far[...], preferred_element_type=F32)
-        value = value.astype(BF16)
-        for shift, out in enumerate(outs):
-
-            @pl.when(pl.program_id(0) == shift)
-            def _():
-                out[pl.ds(first * BLK, count * BLK), :] = value
-
-
-def project(info, own, partner, weight, near, far, part):
-    tile = weight.shape[1] // HEADS // PARTS
-    keep = weight.shape[0] // 2
+        left[pl.ds(first * BLK, count * BLK), :] = own[at][...]
+    for shift in range(4):
+        for copy in copies(shift):
+            copy.wait()
+        for at in range(RANK_BLOCKS):
+            rows = pl.ds(at * BLK, BLK)
+            value = jnp.dot(left[rows], held[shift], preferred_element_type=F32)
+            width = out.shape[3]
+            for part in range(PARTS):
+                half = value[:, part * width : (part + 1) * width]
+                out[part, shift, rows] = half.astype(BF16)
+
+
+def project_own(info, own, weight):
+    tile = weight.shape[1] // HEADS
     rows = RANK_BLOCKS * BLK
-    high = [count * BLK for _, count in CHUNKS]
-
-    def target(s, info):
-        return lax.rem(info[1] + s, 4)
-
-    def other_tile(s, info):
-        return (0, target(s, info) * PARTS + part)
-
+    vmem = pl.BlockSpec(memory_space=pltpu.VMEM)
     return pl.pallas_call(
-        project_kernel,
-        grid_spec=pltpu.PrefetchScalarGridSpec(
-            num_scalar_prefetch=1,
-            grid=(4,),
-            in_specs=[pl.BlockSpec((h, WIDE), lambda s, info: (0, 0)) for h in high]
-            + [pl.BlockSpec((h, keep), lambda s, info: (0, info[2])) for h in high]
-            + [pl.BlockSpec((h, keep), lambda s, info: (0, 1 - info[2])) for h in high]
-            + [
-                pl.BlockSpec(
-                    (WIDE, tile),
-                    lambda s, info: (0, (info[0] * 4 + target(s, info)) * PARTS + part),
-                ),
-                pl.BlockSpec((keep, tile), other_tile),
-                pl.BlockSpec((keep, tile), other_tile),
-            ],
-            out_specs=[pl.BlockSpec((rows, tile), lambda s, info: (0, 0))] * 4,
-        ),
-        out_shape=[jax.ShapeDtypeStruct((rows, tile), BF16)] * 4,
+        own_kernel,
+        in_specs=[pl.BlockSpec(memory_space=pltpu.SMEM)]
+        + [vmem] * len(CHUNKS)
+        + [pl.BlockSpec(memory_space=pltpu.HBM)],
+        out_specs=vmem,
+        out_shape=jax.ShapeDtypeStruct((PARTS, 4, rows, tile // PARTS), BF16),
+        scratch_shapes=[
+            pltpu.VMEM((rows, WIDE), BF16),
+            pltpu.VMEM((4, weight.shape[0], tile), BF16),
+            pltpu.SemaphoreType.DMA((4,)),
+        ],
         compiler_params=pltpu.CompilerParams(vmem_limit_bytes=VMEM),
         cost_estimate=pl.CostEstimate(
-            flops=2 * rows * 2 * WIDE * 4 * tile,
-            bytes_accessed=2 * WIDE * 4 * tile * 2 + rows * WIDE * 8,
+            flops=2 * rows * WIDE * 4 * tile,
+            bytes_accessed=WIDE * 4 * tile * 2 + rows * WIDE * 10,
             transcendentals=0,
         ),
-        name="project",
-    )(info, *own, *partner, *partner, weight, near, far)
+        name="project_own",
+    )(info, *own, weight)
+
+
+ORDER = (2, 1, 3, 0)
+
+
+def partner_kernel(part, info, *refs):
+    chunks = len(CHUNKS)
+    partner = refs[:chunks]
+    base, near, far = refs[chunks : chunks + 3]
+    outs = refs[chunks + 3 :][:4]
+    left, held, begun, sems = refs[-4:]
+    keep = near.shape[1]
+
+    def copies(at):
+        shift = ORDER[at]
+        piece = lax.rem(info[1] + shift, 4) * PARTS + part
+        for which, source in ((0, near), (1, far)):
+            half = lax.rem(info[2] + which, 2)
+            rows = pl.ds(pl.multiple_of(half * keep, keep), keep)
+            yield pltpu.make_async_copy(
+                source.at[piece], held.at[shift, rows], sems.at[shift, which]
+            )
+        yield pltpu.make_async_copy(base.at[part, shift], begun.at[shift], sems.at[shift, 2])
+
+    for at in range(2):
+        for copy in copies(at):
+            copy.start()
+    for at, (first, count) in enumerate(CHUNKS):
+        left[pl.ds(first * BLK, count * BLK), :] = partner[at][...]
+    for at, shift in enumerate(ORDER):
+        for copy in copies(at):
+            copy.wait()
+        if at + 2 < len(ORDER):
+            for copy in copies(at + 2):
+                copy.start()
+        for block in range(RANK_BLOCKS):
+            rows = pl.ds(block * BLK, BLK)
+            value = jnp.dot(left[rows], held[shift], preferred_element_type=F32)
+            outs[shift][rows] = (value + begun[shift, rows].astype(F32)).astype(BF16)
+
+
+def project_partner(info, partner, base, near, far, part):
+    _, _, rows, tile = base.shape
+    vmem = pl.BlockSpec(memory_space=pltpu.VMEM)
+    hbm = pl.BlockSpec(memory_space=pltpu.HBM)
+    return pl.pallas_call(
+        functools.partial(partner_kernel, part),
+        in_specs=[pl.BlockSpec(memory_space=pltpu.SMEM)] + [vmem] * len(CHUNKS) + [hbm] * 3,
+        out_specs=[vmem] * 4,
+        out_shape=[jax.ShapeDtypeStruct((rows, tile), BF16)] * 4,
+        scratch_shapes=[
+            pltpu.VMEM((rows, WIDE), BF16),
+            pltpu.VMEM((4, WIDE, tile), BF16),
+            pltpu.VMEM((4, rows, tile), BF16),
+            pltpu.SemaphoreType.DMA((4, 3)),
+        ],
+        compiler_params=pltpu.CompilerParams(vmem_limit_bytes=VMEM),
+        cost_estimate=pl.CostEstimate(
+            flops=2 * rows * WIDE * 4 * tile,
+            bytes_accessed=WIDE * 4 * tile * 2 + rows * WIDE * 8,
+            transcendentals=0,
+        ),
+        name="project_partner",
+    )(info, *partner, base, near, far)
+
+
+def ring(block, step):
+    return lax.ppermute(block, "head", [(i, i // 4 * 4 + (i + step) % 4) for i in range(HEADS)])
+
+
+def sum_over_z(sums, clockwise):
+    own, ahead, across, behind = sums
+    step = 1 if clockwise else -1
+    first, second = (ahead, behind) if clockwise else (behind, ahead)
+    passed = ring(across, step)
+    direct = ring(second, -step)
+    joined = ring((first.astype(F32) + passed.astype(F32)).astype(BF16), step)
+    return own.astype(F32) + direct.astype(F32) + joined.astype(F32)
 
 
 def local(
@@ -324,32 +448,34 @@
     place = jnp.stack([rank // 2, rank % 2, rank * RANK_BLOCKS])
     info = jnp.stack([head // 4, head % 4, rank % 2])
     packed = pack(keys, key_scale, values, value_scale)
+    cut = cut_weights(info, out_weight)
     beside = lax.ppermute(packed, "ctx", [(i, i ^ 2) for i in range(2 * CHIPS)])
-    cut = cut_weights(out_weight, rank % 2, head // 4)
+    along = along_x(packed)
     cut, beside = lax.optimization_barrier((cut, beside))
     near = lax.ppermute(cut, ("ctx", "head"), across_y())
-    first_kv = with_core(along_x(packed))
+    first_kv = with_core(along)
     state = attend(
         place, block_mask, queries, query_scale, *first_kv, (0, RANK_BLOCKS), None
     )
     later, state = lax.optimization_barrier((along_x(beside), state))
     second_kv = with_core(later)
     own, partner = [], []
-    for chunk in CHUNKS:
+    for at, chunk in enumerate(CHUNKS):
         rows = attend(place, block_mask, queries, query_scale, *second_kv, chunk, state)
-        if not own:
-            near, rows = lax.optimization_barrier((near, rows))
-            far = lax.ppermute(near, "ctx", CORE_SWAP)
+        rows, state = lax.optimization_barrier((rows, state))
         own.append(rows)
         partner.append(lax.ppermute(rows, "head", [(i, i ^ 4) for i in range(HEADS)]))
+        if at == 0:
+            near, state = lax.optimization_barrier((near, state))
+            far = lax.ppermute(near, "ctx", CORE_SWAP)
+        if at == 1:
+            partner[0], state = lax.optimization_barrier((partner[0], state))
+    own, partner[1] = lax.optimization_barrier((own, partner[1]))
+    base = project_own(info, own, out_weight)
     parts = []
     for part in range(PARTS):
-        sums = project(info, own, partner, out_weight, near, far, part)
-        total = sums[0].astype(F32)
-        for shift in range(1, 4):
-            pairs = [(i, i // 4 * 4 + (i + shift) % 4) for i in range(HEADS)]
-            total += lax.ppermute(sums[shift], "head", pairs).astype(F32)
-        parts.append(total)
+        sums = project_partner(info, partner, base, near, far, part)
+        parts.append(sum_over_z(sums, part % 2 == 0))
     return (jnp.concatenate(parts, axis=1) * out_scale[None, :]).astype(BF16)
 
 

time: 137 us -> 131 us (0.956); the launches traced: 137 us -> 129 us
  waiting for transfers between devices: 44.1 us -> 32.1 us
  Pallas kernels: 49.7 us -> 61.1 us
  local copies, waits for them, and re-layouts: 8.42 us -> 4.58 us
  other arithmetic: 6.24 us -> 4.58 us
  starting transfers between devices: 27.7 us -> 26.1 us
    ppermute x2 -> x3, waiting for transfers between devices: 9.13 us -> 0.01 us  [local(): lax.ppermute(rows, 'head', [(i, i ^ 4) for i in range(HEADS)])]
    pallas_call x2 -> x5, Pallas kernels: 18.7 us -> 26.6 us  [the longest x2 11.8 us: project_partner(): pl.pallas_call(functools.partial(partner_kernel, part), in_specs=[pl.Bloc...]
    ppermute x6, waiting for transfers between devices: 21.6 us -> 15.9 us  [ring(): lax.ppermute(block, 'head', [(i, i // 4 * 4 + (i + step) % 4) for i in ra...]
    dynamic_slice x1 -> x0, local copies, waits for them, and re-layouts: 4.72 us -> none  [cut_weights(): lax.dynamic_slice(weight, (core * keep, (1 - half) * (width // 2)), (keep...]
    pallas_call x1, Pallas kernels: 11.8 us -> 14.1 us  [attend(): pl.pallas_call(first_kernel, in_specs=in_specs, out_specs=held, out_shape...]
    ppermute x2, starting transfers between devices: 4.48 us -> 2.39 us  [with_core(): return (mine, lax.ppermute(mine, 'ctx', CORE_SWAP))]
    ppermute x6, waiting for transfers between devices: 8.31 us -> 10.4 us  [along_x(): got.append(lax.ppermute(block, 'ctx', pairs))]
    ppermute x1, starting transfers between devices: 1.94 us -> 0.01 us  [local(): far = lax.ppermute(near, 'ctx', CORE_SWAP)]
  transfers between devices with their start and end apart: 19 -> 20, of which waited for: 9 -> 10; matrix products, arithmetic and copies ran while one was open for 5% -> 3% of each run, Pallas kernels for 30% -> 41%
where the time goes in v3:
time: 131 us; the launch traced here: 129 us
  Pallas kernels  61.1 us (47%)
  waiting for transfers between devices  32.1 us (25%)
  starting transfers between devices  26.1 us (20%)
  other arithmetic  4.58 us (3%)
  local copies, waits for them, and re-layouts  4.58 us (3%)
    pallas_call x3, Pallas kernels, attend(): pl.pallas_call(second_kernel, in_specs=in_specs + held, out_specs=pl.Bloc...  20.4 us
    ppermute x6, waiting for transfers between devices, ring(): lax.ppermute(block, 'head', [(i, i // 4 * 4 + (i + step) % 4) for i in ra...  15.9 us
    pallas_call x1, Pallas kernels, attend(): pl.pallas_call(first_kernel, in_specs=in_specs, out_specs=held, out_shape...  14.1 us
    pallas_call x2, Pallas kernels, project_partner(): pl.pallas_call(functools.partial(partner_kernel, part), in_specs=[pl.Bloc...  11.8 us
    ppermute x6, starting transfers between devices, ring(): lax.ppermute(block, 'head', [(i, i // 4 * 4 + (i + step) % 4) for i in ra...  10.9 us
    ppermute x6, waiting for transfers between devices, along_x(): got.append(lax.ppermute(block, 'ctx', pairs))  10.4 us
    pallas_call x1, Pallas kernels, project_own(): pl.pallas_call(own_kernel, in_specs=[pl.BlockSpec(memory_space=pltpu.SMEM...  8.45 us
    ppermute x6, starting transfers between devices, along_x(): got.append(lax.ppermute(block, 'ctx', pairs))  7.73 us
  transfers between devices with their start and end apart: 20, of which 10 were waited for; matrix products, arithmetic and copies ran while one was open for 3% of the time, Pallas kernels for 41%

profile of v3, /device:TPU:22, one launch (start us, length us, event | category | flops | bytes accessed | tf_op | source)
XLA Modules:
  0.0 128.9 jit_solution(8888928937108609873)
XLA Ops:
  0.0 1.8 %pack.1 = bf16[3,128,256]{2,1,0:T(8,128)(2,1)} custom-call(bf16[384,128]{1,0:T(8,128)(2,1)} %keys.1, bf16[1,384]{1,0:T(2,128)(2,1)} %bitcast.8, bf16[384,128]{1,0:T(8,128)(2,1)} %values.1, bf16[1,384]{1,0:T(2,128)(2,1)} %bitcast.9), custom_call_target="tpu_custom_call" | custom-call | tf_op jit(solution)/shard_map/pack/pallas_call | solution.py:230
  1.8 0.3 collective-permute-start
  2.1 0.7 pad_add_fusion.info
  2.8 4.5 %cut.1 = bf16[8,512,512]{2,1,0:T(8,128)(2,1)} custom-call(s32[3]{0:T(128)} %pad_add_fusion.info, bf16[1024,8192]{1,0:T(8,128)(2,1)} %refs_3_.1), custom_call_target="tpu_custom_call" | custom-call | bytes 16777216 | tf_op jit(solution)/shard_map/cut/pallas_call | solution.py:266
  7.3 2.8 %collective-permute-done = bf16[3,128,256]{2,1,0:T(8,128)(2,1)S(1)} collective-permute-done((bf16[3,128,256]{2,1,0:T(8,128)(2,1)}, bf16[3,128,256]{2,1,0:T(8,128)(2,1)S(1)}, u32[]{:S(2)}, u32[]{:S(2)}) %collective-permute-start) | collective-permute-done | bytes 196640 | tf_op jit(solution)/shard_map/ppermute | solution.py:452
  10.1 1.3 collective-permute-start.10
  11.4 1.3 collective-permute-start.4
  12.7 1.3 %collective-permute-start.5 = (bf16[3,128,256]{2,1,0:T(8,128)(2,1)S(1)}, bf16[3,128,256]{2,1,0:T(8,128)(2,1)S(1)}, u32[]{:S(2)}, u32[]{:S(2)}) collective-permute-start(bf16[3,128,256]{2,1,0:T(8,128)(2,1)S(1)} %copy-done.4), channel_id=1, source_target_pairs={{0,64},{8,72},{16,80},{24,88},{32,96},{40,104},{48,112},{56,120},{... | collective-permute-start | bytes 589832 | tf_op jit(solution)/shard_map/ppermute | solution.py:289
  14.0 1.3 %collective-permute-start.6 = (bf16[3,128,256]{2,1,0:T(8,128)(2,1)S(1)}, bf16[3,128,256]{2,1,0:T(8,128)(2,1)S(1)}, u32[]{:S(2)}, u32[]{:S(2)}) collective-permute-start(bf16[3,128,256]{2,1,0:T(8,128)(2,1)S(1)} %copy-done.4), channel_id=1, source_target_pairs={{0,96},{8,104},{16,112},{24,120},{1,97},{9,105},{17,113},{25,121},... | collective-permute-start | bytes 589832 | tf_op jit(solution)/shard_map/ppermute | solution.py:289
  15.3 3.7 %collective-permute-done.4 = bf16[3,128,256]{2,1,0:T(8,128)(2,1)S(1)} collective-permute-done((bf16[3,128,256]{2,1,0:T(8,128)(2,1)S(1)}, bf16[3,128,256]{2,1,0:T(8,128)(2,1)S(1)}, u32[]{:S(2)}, u32[]{:S(2)}) %collective-permute-start.4) | collective-permute-done | bytes 196640 | tf_op jit(solution)/shard_map/ppermute | solution.py:289
  19.0 2.9 %collective-permute-done.5 = bf16[3,128,256]{2,1,0:T(8,128)(2,1)S(1)} collective-permute-done((bf16[3,128,256]{2,1,0:T(8,128)(2,1)S(1)}, bf16[3,128,256]{2,1,0:T(8,128)(2,1)S(1)}, u32[]{:S(2)}, u32[]{:S(2)}) %collective-permute-start.5) | collective-permute-done | bytes 196640 | tf_op jit(solution)/shard_map/ppermute | solution.py:289
  21.9 3.8 %collective-permute-done.6 = bf16[3,128,256]{2,1,0:T(8,128)(2,1)S(1)} collective-permute-done((bf16[3,128,256]{2,1,0:T(8,128)(2,1)S(1)}, bf16[3,128,256]{2,1,0:T(8,128)(2,1)S(1)}, u32[]{:S(2)}, u32[]{:S(2)}) %collective-permute-start.6) | collective-permute-done | bytes 196640 | tf_op jit(solution)/shard_map/ppermute | solution.py:289
  25.9 0.7 fusion.1
  26.7 1.3 collective-permute-start.1
  27.9 1.3 %collective-permute-start.2 = (bf16[3,128,256]{2,1,0:T(8,128)(2,1)S(1)}, bf16[3,128,256]{2,1,0:T(8,128)(2,1)S(1)}, u32[]{:S(2)}, u32[]{:S(2)}) collective-permute-start(bf16[3,128,256]{2,1,0:T(8,128)(2,1)S(1)} %collective-permute-done), channel_id=1, source_target_pairs={{0,64},{8,72},{16,80},{24,88},{32,96},{40,104},{48,112},{56,120},{... | collective-permute-start | bytes 589832 | tf_op jit(solution)/shard_map/ppermute | solution.py:289
  29.2 1.3 %collective-permute-start.3 = (bf16[3,128,256]{2,1,0:T(8,128)(2,1)S(1)}, bf16[3,128,256]{2,1,0:T(8,128)(2,1)S(1)}, u32[]{:S(2)}, u32[]{:S(2)}) collective-permute-start(bf16[3,128,256]{2,1,0:T(8,128)(2,1)S(1)} %collective-permute-done), channel_id=1, source_target_pairs={{0,96},{8,104},{16,112},{24,120},{1,97},{9,105},{17,113},{25,121},... | collective-permute-start | bytes 589832 | tf_op jit(solution)/shard_map/ppermute | solution.py:289
  30.6 0.9 copy-done.13
  31.4 14.1 %attend_first.1 = (f32[3,1,1024]{2,1,0:T(1,128)}, f32[3,1,1024]{2,1,0:T(1,128)}, f32[3,128,1024]{2,1,0:T(8,128)}) custom-call(s32[3]{0:T(128)} %get-tuple-element.88.place, s32[48,48]{1,0:T(8,128)} %mask.7, bf16[384,1024]{1,0:T(8,128)(2,1)} %q_ref.7, bf16[8,384]{1,0:T(8,128)(2,1)} %bitcast.10, bf16[12,128,256]{2,1,0:T(8,128)(2,1)} %copy-done.5, ...), custom_call_target="tpu_custom_call" | custom-call | flops 3932160000 | bytes 4718592 | tf_op jit(solution)/shard_map/attend_first/pallas_call | solution.py:195
  45.6 2.3 %collective-permute-start.8 = (bf16[12,128,256]{2,1,0:T(8,128)(2,1)S(1)}, bf16[12,128,256]{2,1,0:T(8,128)(2,1)S(1)}, u32[]{:S(2)}, u32[]{:S(2)}) collective-permute-start(bf16[12,128,256]{2,1,0:T(8,128)(2,1)S(1)} %constant_dynamic-update-slice_fusion.mine), channel_id=1, source_target_pairs={{0,8},{8,0},{16,24},{24,16},{32,40},{40,32},{48,56},{56,48},{64,72... | collective-permute-start | bytes 2359304 | tf_op jit(solution)/shard_map/ppermute | solution.py:295
  48.0 1.9 %collective-permute-done.8.other = bf16[12,128,256]{2,1,0:T(8,128)(2,1)S(1)} collective-permute-done((bf16[12,128,256]{2,1,0:T(8,128)(2,1)S(1)}, bf16[12,128,256]{2,1,0:T(8,128)(2,1)S(1)}, u32[]{:S(2)}, u32[]{:S(2)}) %collective-permute-start.8) | collective-permute-done | bytes 786464 | tf_op jit(solution)/shard_map/ppermute | solution.py:295
  49.9 0.9 copy-done.14
  50.8 7.0 %attend_second.3.refs_0_ = bf16[128,1024]{1,0:T(8,128)(2,1)} custom-call(s32[3]{0:T(128)} %get-tuple-element.88.place, s32[48,48]{1,0:T(8,128)} %mask.7, bf16[384,1024]{1,0:T(8,128)(2,1)} %q_ref.7, bf16[8,384]{1,0:T(8,128)(2,1)} %bitcast.11, bf16[12,128,256]{2,1,0:T(8,128)(2,1)} %copy-done.9, bf16[12,128,256]{2,1,0:T(8,128)(2,1)} %copy-done.14, ...), custom_call_target="tpu_custom_call" | custom-call | flops 1310720000 | bytes 1572864 | tf_op jit(solution)/shard_map/attend_second/pallas_call | solution.py:208
  57.8 1.2 collective-permute-done.10.refs_4_
  59.0 1.3 collective-permute-start.9
  60.3 0.5 add.44.place
  60.8 6.7 %attend_second.4.refs_1_ = bf16[128,1024]{1,0:T(8,128)(2,1)} custom-call(s32[3]{0:T(128)} %add.44.place, s32[48,48]{1,0:T(8,128)} %mask.7, bf16[384,1024]{1,0:T(8,128)(2,1)} %q_ref.7, bf16[8,384]{1,0:T(8,128)(2,1)} %bitcast.12, bf16[12,128,256]{2,1,0:T(8,128)(2,1)} %copy-done.9, bf16[12,128,256]{2,1,0:T(8,128)(2,1)} %copy-done.14, ...), custom_call_target="tpu_custom_call" | custom-call | flops 1310720000 | bytes 1572864 | tf_op jit(solution)/shard_map/attend_second/pallas_call | solution.py:208
  67.5 0.8 collective-permute-start.11
  68.3 6.7 %attend_second.5.refs_2_ = bf16[128,1024]{1,0:T(8,128)(2,1)} custom-call(s32[3]{0:T(128)} %get-tuple-element.87.place, s32[48,48]{1,0:T(8,128)} %mask.7, bf16[384,1024]{1,0:T(8,128)(2,1)} %q_ref.7, bf16[8,384]{1,0:T(8,128)(2,1)} %bitcast.13, bf16[12,128,256]{2,1,0:T(8,128)(2,1)} %copy-done.9, bf16[12,128,256]{2,1,0:T(8,128)(2,1)} %copy-done.14, ...), custom_call_target="tpu_custom_call" | custom-call | flops 1310720000 | bytes 1572864 | tf_op jit(solution)/shard_map/attend_second/pallas_call | solution.py:208
  75.1 1.4 %collective-permute-start.12 = (bf16[128,1024]{1,0:T(8,128)(2,1)}, bf16[128,1024]{1,0:T(8,128)(2,1)S(1)}, u32[]{:S(2)}, u32[]{:S(2)}) collective-permute-start(bf16[128,1024]{1,0:T(8,128)(2,1)} %attend_second.5.refs_2_), channel_id=1, source_target_pairs={{0,4},{1,5},{2,6},{3,7},{4,0},{5,1},{6,2},{7,3},{8,12},{9,13},{10,... | collective-permute-start | bytes 786440 | tf_op jit(solution)/shard_map/ppermute | solution.py:467
  76.4 8.5 %project_own.1.refs_3_ = bf16[2,4,384,512]{3,2,1,0:T(8,128)(2,1)} custom-call(s32[3]{0:T(128)} %pad_add_fusion.info, bf16[128,1024]{1,0:T(8,128)(2,1)} %attend_second.3.refs_0_, bf16[128,1024]{1,0:T(8,128)(2,1)} %attend_second.4.refs_1_, bf16[128,1024]{1,0:T(8,128)(2,1)} %attend_second.5.refs_2_, bf16[1024,8192]{1,0:T(8,128)(2,1)} %refs_3_.1), custom_call_target="tpu_custom_call" | custom-call | flops 3221225472 | bytes 12320768 | tf_op jit(solution)/shard_map/project_own/pallas_call | solution.py:343
  84.9 0.7 copy-done.3
  85.6 2.0 %copy-done = bf16[8,512,512]{2,1,0:T(8,128)(2,1)} copy-done((bf16[8,512,512]{2,1,0:T(8,128)(2,1)}, bf16[8,512,512]{2,1,0:T(8,128)(2,1)S(1)}, u32[]{:S(2)}) %copy-start) | copy-done | bytes 4194328
  87.6 5.9 %project_partner.2 = (bf16[384,512]{1,0:T(8,128)(2,1)}, bf16[384,512]{1,0:T(8,128)(2,1)}, bf16[384,512]{1,0:T(8,128)(2,1)}, bf16[384,512]{1,0:T(8,128)(2,1)}) custom-call(s32[3]{0:T(128)} %pad_add_fusion.info, bf16[128,1024]{1,0:T(8,128)(2,1)} %copy-done.1, bf16[128,1024]{1,0:T(8,128)(2,1)} %copy-done.2, bf16[128,1024]{1,0:T(8,128)(2,1)} %copy-done.3, ...), custom_call_target="tpu_custom_call" | custom-call | flops 1610612736 | bytes 7340032 | tf_op jit(solution)/shard_map/project_partner/pallas_call | solution.py:408
  93.6 2.0 %collective-permute-start.15 = (bf16[384,512]{1,0:T(8,128)(2,1)}, bf16[384,512]{1,0:T(8,128)(2,1)S(1)}, u32[]{:S(2)}, u32[]{:S(2)}) collective-permute-start(bf16[384,512]{1,0:T(8,128)(2,1)} %get-tuple-element.82), channel_id=1, source_target_pairs={{0,1},{1,2},{2,3},{3,0},{4,5},{5,6},{6,7},{7,4},{8,9},{9,10},{10,1... | collective-permute-start | bytes 1179656 | tf_op jit(solution)/shard_map/ppermute | solution.py:430
  95.6 5.9 %project_partner.3 = (bf16[384,512]{1,0:T(8,128)(2,1)}, bf16[384,512]{1,0:T(8,128)(2,1)}, bf16[384,512]{1,0:T(8,128)(2,1)}, bf16[384,512]{1,0:T(8,128)(2,1)}) custom-call(s32[3]{0:T(128)} %pad_add_fusion.info, bf16[128,1024]{1,0:T(8,128)(2,1)} %copy-done.1, bf16[128,1024]{1,0:T(8,128)(2,1)} %copy-done.2, bf16[128,1024]{1,0:T(8,128)(2,1)} %copy-done.3, ...), custom_call_target="tpu_custom_call" | custom-call | flops 1610612736 | bytes 7340032 | tf_op jit(solution)/shard_map/project_partner/pallas_call | solution.py:408
  101.5 2.3 %collective-permute-start.18 = (bf16[384,512]{1,0:T(8,128)(2,1)}, bf16[384,512]{1,0:T(8,128)(2,1)S(1)}, u32[]{:S(2)}, u32[]{:S(2)}) collective-permute-start(bf16[384,512]{1,0:T(8,128)(2,1)} %get-tuple-element.86), channel_id=1, source_target_pairs={{0,3},{1,0},{2,1},{3,2},{4,7},{5,4},{6,5},{7,6},{8,11},{9,8},{10,9... | collective-permute-start | bytes 1179656 | tf_op jit(solution)/shard_map/ppermute | solution.py:430
  103.7 2.0 %collective-permute-start.14 = (bf16[384,512]{1,0:T(8,128)(2,1)S(1)}, bf16[384,512]{1,0:T(8,128)(2,1)S(1)}, u32[]{:S(2)}, u32[]{:S(2)}) collective-permute-start(bf16[384,512]{1,0:T(8,128)(2,1)S(1)} %copy-done.15), channel_id=1, source_target_pairs={{0,3},{1,0},{2,1},{3,2},{4,7},{5,4},{6,5},{7,6},{8,11},{9,8},{10,9... | collective-permute-start | bytes 1179656 | tf_op jit(solution)/shard_map/ppermute | solution.py:430
  105.8 0.1 collective-permute-start.16
  105.9 1.1 collective-permute-start.17
  107.0 6.8 %collective-permute-done.18 = bf16[384,512]{1,0:T(8,128)(2,1)S(1)} collective-permute-done((bf16[384,512]{1,0:T(8,128)(2,1)}, bf16[384,512]{1,0:T(8,128)(2,1)S(1)}, u32[]{:S(2)}, u32[]{:S(2)}) %collective-permute-start.18) | collective-permute-done | bytes 393248 | tf_op jit(solution)/shard_map/ppermute | solution.py:430
  113.8 1.1 add_convert_fusion
  114.9 3.5 %collective-permute-start.19 = (bf16[384,512]{1,0:T(8,128)(2,1)S(1)}, bf16[384,512]{1,0:T(8,128)(2,1)S(1)}, u32[]{:S(2)}, u32[]{:S(2)}) collective-permute-start(bf16[384,512]{1,0:T(8,128)(2,1)S(1)} %add_convert_fusion), channel_id=1, source_target_pairs={{0,3},{1,0},{2,1},{3,2},{4,7},{5,4},{6,5},{7,6},{8,11},{9,8},{10,9... | collective-permute-start | bytes 1179656 | tf_op jit(solution)/shard_map/ppermute | solution.py:430
  118.4 3.8 %collective-permute-done.14 = bf16[384,512]{1,0:T(8,128)(2,1)S(1)} collective-permute-done((bf16[384,512]{1,0:T(8,128)(2,1)S(1)}, bf16[384,512]{1,0:T(8,128)(2,1)S(1)}, u32[]{:S(2)}, u32[]{:S(2)}) %collective-permute-start.14) | collective-permute-done | bytes 393248 | tf_op jit(solution)/shard_map/ppermute | solution.py:430
  122.2 0.1 convert_add_fusion.1
  122.4 1.5 %collective-permute-done.17 = bf16[384,512]{1,0:T(8,128)(2,1)S(1)} collective-permute-done((bf16[384,512]{1,0:T(8,128)(2,1)}, bf16[384,512]{1,0:T(8,128)(2,1)S(1)}, u32[]{:S(2)}, u32[]{:S(2)}) %collective-permute-start.17) | collective-permute-done | bytes 393248 | tf_op jit(solution)/shard_map/ppermute | solution.py:430
  123.8 3.8 %collective-permute-done.19 = bf16[384,512]{1,0:T(8,128)(2,1)S(1)} collective-permute-done((bf16[384,512]{1,0:T(8,128)(2,1)S(1)}, bf16[384,512]{1,0:T(8,128)(2,1)S(1)}, u32[]{:S(2)}, u32[]{:S(2)}) %collective-permute-start.19) | collective-permute-done | bytes 393248 | tf_op jit(solution)/shard_map/ppermute | solution.py:430
  127.7 0.1 convert_add_fusion
  127.8 1.0 fusion
  (48 shorter events, 0.4 us)
Async XLA Ops:
  1.8 8.4 %collective-permute-start = (bf16[3,128,256]{2,1,0:T(8,128)(2,1)}, bf16[3,128,256]{2,1,0:T(8,128)(2,1)S(1)}, u32[]{:S(2)}, u32[]{:S(2)}) collective-permute-start(bf16[3,128,256]{2,1,0:T(8,128)(2,1)} %pack.1), channel_id=1, source_target_pairs={{0,16},{8,24},{16,0},{24,8},{32,48},{40,56},{48,32},{56,40},{64,80... | collective-permute-start | bytes 589832 | tf_op jit(solution)/shard_map/ppermute | solution.py:452
  2.8 8.7 %copy-start.4 = (bf16[3,128,256]{2,1,0:T(8,128)(2,1)S(1)}, bf16[3,128,256]{2,1,0:T(8,128)(2,1)}, u32[]{:S(2)}) copy-start(bf16[3,128,256]{2,1,0:T(8,128)(2,1)} %pack.1) | copy-start | bytes 589828
  7.3 18.6 %copy-start.11 = (s32[3]{0:T(128)S(1)}, s32[3]{0:T(128)}, u32[]{:S(2)}) copy-start(s32[3]{0:T(128)} %constant.62.clone) | copy-start | bytes 40
  10.1 48.8 %collective-permute-start.10 = (bf16[8,512,512]{2,1,0:T(8,128)(2,1)}, bf16[8,512,512]{2,1,0:T(8,128)(2,1)}, u32[]{:S(2)}, u32[]{:S(2)}) collective-permute-start(bf16[8,512,512]{2,1,0:T(8,128)(2,1)} %cut.1), channel_id=1, source_target_pairs={{0,4},{1,5},{2,6},{3,7},{8,28},{9,29},{10,30},{11,31},{4,16},{5,17... | collective-permute-start | bytes 12582920 | tf_op jit(solution)/shard_map/ppermute | solution.py:455
  11.4 7.6 %collective-permute-start.4 = (bf16[3,128,256]{2,1,0:T(8,128)(2,1)S(1)}, bf16[3,128,256]{2,1,0:T(8,128)(2,1)S(1)}, u32[]{:S(2)}, u32[]{:S(2)}) collective-permute-start(bf16[3,128,256]{2,1,0:T(8,128)(2,1)S(1)} %copy-done.4), channel_id=1, source_target_pairs={{0,32},{8,40},{16,48},{24,56},{32,64},{40,72},{48,80},{56,88},{64,... | collective-permute-start | bytes 589832 | tf_op jit(solution)/shard_map/ppermute | solution.py:289
  12.7 9.2 %collective-permute-start.5 = (bf16[3,128,256]{2,1,0:T(8,128)(2,1)S(1)}, bf16[3,128,256]{2,1,0:T(8,128)(2,1)S(1)}, u32[]{:S(2)}, u32[]{:S(2)}) collective-permute-start(bf16[3,128,256]{2,1,0:T(8,128)(2,1)S(1)} %copy-done.4), channel_id=1, source_target_pairs={{0,64},{8,72},{16,80},{24,88},{32,96},{40,104},{48,112},{56,120},{... | collective-permute-start | bytes 589832 | tf_op jit(solution)/shard_map/ppermute | solution.py:289
  14.0 11.7 %collective-permute-start.6 = (bf16[3,128,256]{2,1,0:T(8,128)(2,1)S(1)}, bf16[3,128,256]{2,1,0:T(8,128)(2,1)S(1)}, u32[]{:S(2)}, u32[]{:S(2)}) collective-permute-start(bf16[3,128,256]{2,1,0:T(8,128)(2,1)S(1)} %copy-done.4), channel_id=1, source_target_pairs={{0,96},{8,104},{16,112},{24,120},{1,97},{9,105},{17,113},{25,121},... | collective-permute-start | bytes 589832 | tf_op jit(solution)/shard_map/ppermute | solution.py:289
  25.8 4.8 %copy-start.5 = (bf16[12,128,256]{2,1,0:T(8,128)(2,1)}, bf16[12,128,256]{2,1,0:T(8,128)(2,1)S(1)}, u32[]{:S(2)}) copy-start(bf16[12,128,256]{2,1,0:T(8,128)(2,1)S(1)} %pad_maximum_fusion.mine) | copy-start | bytes 2359300
  25.8 4.7 %collective-permute-start.7 = (bf16[12,128,256]{2,1,0:T(8,128)(2,1)S(1)}, bf16[12,128,256]{2,1,0:T(8,128)(2,1)S(1)}, u32[]{:S(2)}, u32[]{:S(2)}) collective-permute-start(bf16[12,128,256]{2,1,0:T(8,128)(2,1)S(1)} %pad_maximum_fusion.mine), channel_id=1, source_target_pairs={{0,8},{8,0},{16,24},{24,16},{32,40},{40,32},{48,56},{56,48},{64,72... | collective-permute-start | bytes 2359304 | tf_op jit(solution)/shard_map/ppermute | solution.py:295
  26.7 18.8 %collective-permute-start.1 = (bf16[3,128,256]{2,1,0:T(8,128)(2,1)S(1)}, bf16[3,128,256]{2,1,0:T(8,128)(2,1)S(1)}, u32[]{:S(2)}, u32[]{:S(2)}) collective-permute-start(bf16[3,128,256]{2,1,0:T(8,128)(2,1)S(1)} %collective-permute-done), channel_id=1, source_target_pairs={{0,32},{8,40},{16,48},{24,56},{32,64},{40,72},{48,80},{56,88},{64,... | collective-permute-start | bytes 589832 | tf_op jit(solution)/shard_map/ppermute | solution.py:289
  27.9 17.6 %collective-permute-start.2 = (bf16[3,128,256]{2,1,0:T(8,128)(2,1)S(1)}, bf16[3,128,256]{2,1,0:T(8,128)(2,1)S(1)}, u32[]{:S(2)}, u32[]{:S(2)}) collective-permute-start(bf16[3,128,256]{2,1,0:T(8,128)(2,1)S(1)} %collective-permute-done), channel_id=1, source_target_pairs={{0,64},{8,72},{16,80},{24,88},{32,96},{40,104},{48,112},{56,120},{... | collective-permute-start | bytes 589832 | tf_op jit(solution)/shard_map/ppermute | solution.py:289
  29.2 16.3 %collective-permute-start.3 = (bf16[3,128,256]{2,1,0:T(8,128)(2,1)S(1)}, bf16[3,128,256]{2,1,0:T(8,128)(2,1)S(1)}, u32[]{:S(2)}, u32[]{:S(2)}) collective-permute-start(bf16[3,128,256]{2,1,0:T(8,128)(2,1)S(1)} %collective-permute-done), channel_id=1, source_target_pairs={{0,96},{8,104},{16,112},{24,120},{1,97},{9,105},{17,113},{25,121},... | collective-permute-start | bytes 589832 | tf_op jit(solution)/shard_map/ppermute | solution.py:289
  30.5 0.9 copy-start.13
  45.6 4.3 %copy-start.9 = (bf16[12,128,256]{2,1,0:T(8,128)(2,1)}, bf16[12,128,256]{2,1,0:T(8,128)(2,1)S(1)}, u32[]{:S(2)}) copy-start(bf16[12,128,256]{2,1,0:T(8,128)(2,1)S(1)} %constant_dynamic-update-slice_fusion.mine) | copy-start | bytes 2359300
  45.6 14.6 %copy-start.12 = (s32[3]{0:T(128)S(1)}, s32[3]{0:T(128)}, u32[]{:S(2)}) copy-start(s32[3]{0:T(128)} %get-tuple-element.88.place) | copy-start | bytes 40
  45.6 14.6 %copy-start.16 = (s32[3]{0:T(128)S(1)}, s32[3]{0:T(128)}, u32[]{:S(2)}) copy-start(s32[3]{0:T(128)} %constant.61.clone) | copy-start | bytes 40
  45.6 4.2 %collective-permute-start.8 = (bf16[12,128,256]{2,1,0:T(8,128)(2,1)S(1)}, bf16[12,128,256]{2,1,0:T(8,128)(2,1)S(1)}, u32[]{:S(2)}, u32[]{:S(2)}) collective-permute-start(bf16[12,128,256]{2,1,0:T(8,128)(2,1)S(1)} %constant_dynamic-update-slice_fusion.mine), channel_id=1, source_target_pairs={{0,8},{8,0},{16,24},{24,16},{32,40},{40,32},{48,56},{56,48},{64,72... | collective-permute-start | bytes 2359304 | tf_op jit(solution)/shard_map/ppermute | solution.py:295
  49.9 0.9 copy-start.14
  59.0 25.9 %collective-permute-start.13 = (bf16[8,512,512]{2,1,0:T(8,128)(2,1)}, bf16[8,512,512]{2,1,0:T(8,128)(2,1)S(1)}, u32[]{:S(2)}, u32[]{:S(2)}) collective-permute-start(bf16[8,512,512]{2,1,0:T(8,128)(2,1)} %collective-permute-done.10.refs_4_), channel_id=1, source_target_pairs={{0,8},{8,0},{16,24},{24,16},{32,40},{40,32},{48,56},{56,48},{64,72... | collective-permute-start | bytes 12582920 | tf_op jit(solution)/shard_map/ppermute | solution.py:470
  59.0 9.3 %collective-permute-start.9 = (bf16[128,1024]{1,0:T(8,128)(2,1)}, bf16[128,1024]{1,0:T(8,128)(2,1)S(1)}, u32[]{:S(2)}, u32[]{:S(2)}) collective-permute-start(bf16[128,1024]{1,0:T(8,128)(2,1)} %attend_second.3.refs_0_), channel_id=1, source_target_pairs={{0,4},{1,5},{2,6},{3,7},{4,0},{5,1},{6,2},{7,3},{8,12},{9,13},{10,... | collective-permute-start | bytes 786440 | tf_op jit(solution)/shard_map/ppermute | solution.py:467
  67.5 8.9 %collective-permute-start.11 = (bf16[128,1024]{1,0:T(8,128)(2,1)}, bf16[128,1024]{1,0:T(8,128)(2,1)S(1)}, u32[]{:S(2)}, u32[]{:S(2)}) collective-permute-start(bf16[128,1024]{1,0:T(8,128)(2,1)} %attend_second.4.refs_1_), channel_id=1, source_target_pairs={{0,4},{1,5},{2,6},{3,7},{4,0},{5,1},{6,2},{7,3},{8,12},{9,13},{10,... | collective-permute-start | bytes 786440 | tf_op jit(solution)/shard_map/ppermute | solution.py:467
  68.3 6.7 %copy-start.1 = (bf16[128,1024]{1,0:T(8,128)(2,1)}, bf16[128,1024]{1,0:T(8,128)(2,1)S(1)}, u32[]{:S(2)}) copy-start(bf16[128,1024]{1,0:T(8,128)(2,1)S(1)} %collective-permute-done.9.refs_0_) | copy-start | bytes 786436
  75.1 9.8 %collective-permute-start.12 = (bf16[128,1024]{1,0:T(8,128)(2,1)}, bf16[128,1024]{1,0:T(8,128)(2,1)S(1)}, u32[]{:S(2)}, u32[]{:S(2)}) collective-permute-start(bf16[128,1024]{1,0:T(8,128)(2,1)} %attend_second.5.refs_2_), channel_id=1, source_target_pairs={{0,4},{1,5},{2,6},{3,7},{4,0},{5,1},{6,2},{7,3},{8,12},{9,13},{10,... | collective-permute-start | bytes 786440 | tf_op jit(solution)/shard_map/ppermute | solution.py:467
  76.4 8.5 %copy-start.2 = (bf16[128,1024]{1,0:T(8,128)(2,1)}, bf16[128,1024]{1,0:T(8,128)(2,1)S(1)}, u32[]{:S(2)}) copy-start(bf16[128,1024]{1,0:T(8,128)(2,1)S(1)} %collective-permute-done.11.refs_1_) | copy-start | bytes 786436
  84.9 0.7 copy-start.3
  85.6 2.0 %copy-start = (bf16[8,512,512]{2,1,0:T(8,128)(2,1)}, bf16[8,512,512]{2,1,0:T(8,128)(2,1)S(1)}, u32[]{:S(2)}) copy-start(bf16[8,512,512]{2,1,0:T(8,128)(2,1)S(1)} %collective-permute-done.13.refs_5_) | copy-start | bytes 12582916
  93.6 10.2 %copy-start.15 = (bf16[384,512]{1,0:T(8,128)(2,1)S(1)}, bf16[384,512]{1,0:T(8,128)(2,1)}, u32[]{:S(2)}) copy-start(bf16[384,512]{1,0:T(8,128)(2,1)} %get-tuple-element.80) | copy-start | bytes 1179652
  93.6 12.1 %copy-start.6 = (bf16[384,512]{1,0:T(8,128)(2,1)S(1)}, bf16[384,512]{1,0:T(8,128)(2,1)}, u32[]{:S(2)}) copy-start(bf16[384,512]{1,0:T(8,128)(2,1)} %get-tuple-element.81) | copy-start | bytes 1179652
  93.6 12.1 %collective-permute-start.15 = (bf16[384,512]{1,0:T(8,128)(2,1)}, bf16[384,512]{1,0:T(8,128)(2,1)S(1)}, u32[]{:S(2)}, u32[]{:S(2)}) collective-permute-start(bf16[384,512]{1,0:T(8,128)(2,1)} %get-tuple-element.82), channel_id=1, source_target_pairs={{0,1},{1,2},{2,3},{3,0},{4,5},{5,6},{6,7},{7,4},{8,9},{9,10},{10,1... | collective-permute-start | bytes 1179656 | tf_op jit(solution)/shard_map/ppermute | solution.py:430
  101.5 20.8 %copy-start.8 = (bf16[384,512]{1,0:T(8,128)(2,1)S(1)}, bf16[384,512]{1,0:T(8,128)(2,1)}, u32[]{:S(2)}) copy-start(bf16[384,512]{1,0:T(8,128)(2,1)} %get-tuple-element.79) | copy-start | bytes 1179652
  101.5 12.3 %collective-permute-start.18 = (bf16[384,512]{1,0:T(8,128)(2,1)}, bf16[384,512]{1,0:T(8,128)(2,1)S(1)}, u32[]{:S(2)}, u32[]{:S(2)}) collective-permute-start(bf16[384,512]{1,0:T(8,128)(2,1)} %get-tuple-element.86), channel_id=1, source_target_pairs={{0,3},{1,0},{2,1},{3,2},{4,7},{5,4},{6,5},{7,6},{8,11},{9,8},{10,9... | collective-permute-start | bytes 1179656 | tf_op jit(solution)/shard_map/ppermute | solution.py:430
  103.7 18.5 %collective-permute-start.14 = (bf16[384,512]{1,0:T(8,128)(2,1)S(1)}, bf16[384,512]{1,0:T(8,128)(2,1)S(1)}, u32[]{:S(2)}, u32[]{:S(2)}) collective-permute-start(bf16[384,512]{1,0:T(8,128)(2,1)S(1)} %copy-done.15), channel_id=1, source_target_pairs={{0,3},{1,0},{2,1},{3,2},{4,7},{5,4},{6,5},{7,6},{8,11},{9,8},{10,9... | collective-permute-start | bytes 1179656 | tf_op jit(solution)/shard_map/ppermute | solution.py:430
  105.8 16.4 %collective-permute-start.16 = (bf16[384,512]{1,0:T(8,128)(2,1)S(1)}, bf16[384,512]{1,0:T(8,128)(2,1)S(1)}, u32[]{:S(2)}, u32[]{:S(2)}) collective-permute-start(bf16[384,512]{1,0:T(8,128)(2,1)S(1)} %add_convert_fusion.1), channel_id=1, source_target_pairs={{0,1},{1,2},{2,3},{3,0},{4,5},{5,6},{6,7},{7,4},{8,9},{9,10},{10,1... | collective-permute-start | bytes 1179656 | tf_op jit(solution)/shard_map/ppermute | solution.py:430
  105.9 17.9 %collective-permute-start.17 = (bf16[384,512]{1,0:T(8,128)(2,1)}, bf16[384,512]{1,0:T(8,128)(2,1)S(1)}, u32[]{:S(2)}, u32[]{:S(2)}) collective-permute-start(bf16[384,512]{1,0:T(8,128)(2,1)} %get-tuple-element.84), channel_id=1, source_target_pairs={{0,1},{1,2},{2,3},{3,0},{4,5},{5,6},{6,7},{7,4},{8,9},{9,10},{10,1... | collective-permute-start | bytes 1179656 | tf_op jit(solution)/shard_map/ppermute | solution.py:430
  113.8 13.9 %copy-start.7 = (bf16[384,512]{1,0:T(8,128)(2,1)S(1)}, bf16[384,512]{1,0:T(8,128)(2,1)}, u32[]{:S(2)}) copy-start(bf16[384,512]{1,0:T(8,128)(2,1)} %get-tuple-element.83) | copy-start | bytes 1179652
  114.9 12.7 %collective-permute-start.19 = (bf16[384,512]{1,0:T(8,128)(2,1)S(1)}, bf16[384,512]{1,0:T(8,128)(2,1)S(1)}, u32[]{:S(2)}, u32[]{:S(2)}) collective-permute-start(bf16[384,512]{1,0:T(8,128)(2,1)S(1)} %add_convert_fusion), channel_id=1, source_target_pairs={{0,3},{1,0},{2,1},{3,2},{4,7},{5,4},{6,5},{7,6},{8,11},{9,8},{10,9... | collective-permute-start | bytes 1179656 | tf_op jit(solution)/shard_map/ppermute | solution.py:430
  122.2 5.6 %copy-start.10 = (f32[1024]{0:T(1024)S(1)}, f32[1024]{0:T(1024)}, u32[]{:S(2)}) copy-start(f32[1024]{0:T(1024)} %param.21) | copy-start | bytes 12292

commit v4 on v3

--- a/solution.py
+++ b/solution.py
@@ -20,7 +20,7 @@
 F32 = jnp.float32
 BF16 = jnp.bfloat16
 CHUNKS = ((0, 1), (1, 1), (2, 1))
-VMEM = 56 << 20
+VMEM = 48 << 20
 PARTS = 2
 
 
@@ -416,7 +416,7 @@
             pltpu.VMEM((4, rows, tile), BF16),
             pltpu.SemaphoreType.DMA((4, 3)),
         ],
-        compiler_params=pltpu.CompilerParams(vmem_limit_bytes=VMEM),
+        compiler_params=pltpu.CompilerParams(vmem_limit_bytes=20 << 20),
         cost_estimate=pl.CostEstimate(
             flops=2 * rows * WIDE * 4 * tile,
             bytes_accessed=WIDE * 4 * tile * 2 + rows * WIDE * 8,
@@ -453,6 +453,7 @@
     along = along_x(packed)
     cut, beside = lax.optimization_barrier((cut, beside))
     near = lax.ppermute(cut, ("ctx", "head"), across_y())
+    along, beside = lax.optimization_barrier((along, beside))
     first_kv = with_core(along)
     state = attend(
         place, block_mask, queries, query_scale, *first_kv, (0, RANK_BLOCKS), None
@@ -465,13 +466,9 @@
         rows, state = lax.optimization_barrier((rows, state))
         own.append(rows)
         partner.append(lax.ppermute(rows, "head", [(i, i ^ 4) for i in range(HEADS)]))
-        if at == 0:
-            near, state = lax.optimization_barrier((near, state))
-            far = lax.ppermute(near, "ctx", CORE_SWAP)
-        if at == 1:
-            partner[0], state = lax.optimization_barrier((partner[0], state))
-    own, partner[1] = lax.optimization_barrier((own, partner[1]))
+    own, partner[:2], near = lax.optimization_barrier((own, partner[:2], near))
     base = project_own(info, own, out_weight)
+    far = lax.ppermute(near, "ctx", CORE_SWAP)
     parts = []
     for part in range(PARTS):
         sums = project_partner(info, partner, base, near, far, part)

time: 131 us -> 126 us (0.962)
  waiting for transfers between devices: 32.1 us -> 40.1 us
  Pallas kernels: 61.1 us -> 53.3 us
  local copies, waits for them, and re-layouts: 4.58 us -> 0.16 us
  other arithmetic: 4.58 us -> 1.67 us
  starting transfers between devices: 26.1 us -> 28.9 us
    ppermute x3, waiting for transfers between devices: 0.01 us -> 6.21 us  [local(): lax.ppermute(rows, 'head', [(i, i ^ 4) for i in range(HEADS)])]
    unnamed x37 -> x20, local copies, waits for them, and re-layouts: 4.57 us -> 0.13 us
    ppermute x2, starting transfers between devices: 2.39 us -> 5.35 us  [with_core(): return (mine, lax.ppermute(mine, 'ctx', CORE_SWAP))]
    pallas_call x2, Pallas kernels: 11.8 us -> 9.03 us  [project_partner(): pl.pallas_call(functools.partial(partner_kernel, part), in_specs=[pl.Bloc...]
    pallas_call x1, Pallas kernels: 8.45 us -> 6.15 us  [project_own(): pl.pallas_call(own_kernel, in_specs=[pl.BlockSpec(memory_space=pltpu.SMEM...]
    ppermute x6, waiting for transfers between devices: 15.9 us -> 18 us  [ring(): lax.ppermute(block, 'head', [(i, i // 4 * 4 + (i + step) % 4) for i in ra...]
    pallas_call x1, Pallas kernels: 14.1 us -> 12.6 us  [attend(): pl.pallas_call(first_kernel, in_specs=in_specs, out_specs=held, out_shape...]
  transfers between devices with their start and end apart: 20 -> 20, of which waited for: 10 -> 12; matrix products, arithmetic and copies ran while one was open for 3% -> 0% of each run, Pallas kernels for 41% -> 38%
where the time goes in v4:
time: 126 us; the launch traced here: 125 us
  Pallas kernels  53.3 us (42%)
  waiting for transfers between devices  40.1 us (32%)
  starting transfers between devices  28.9 us (23%)
  other arithmetic  1.67 us (1%)
    pallas_call x3, Pallas kernels, attend(): pl.pallas_call(second_kernel, in_specs=in_specs + held, out_specs=pl.Bloc...  19.5 us
    ppermute x6, waiting for transfers between devices, ring(): lax.ppermute(block, 'head', [(i, i // 4 * 4 + (i + step) % 4) for i in ra...  18 us
    pallas_call x1, Pallas kernels, attend(): pl.pallas_call(first_kernel, in_specs=in_specs, out_specs=held, out_shape...  12.6 us
    ppermute x6, starting transfers between devices, ring(): lax.ppermute(block, 'head', [(i, i // 4 * 4 + (i + step) % 4) for i in ra...  11.2 us
    ppermute x6, waiting for transfers between devices, along_x(): got.append(lax.ppermute(block, 'ctx', pairs))  10.4 us
    pallas_call x2, Pallas kernels, project_partner(): pl.pallas_call(functools.partial(partner_kernel, part), in_specs=[pl.Bloc...  9.03 us
    ppermute x6, starting transfers between devices, along_x(): got.append(lax.ppermute(block, 'ctx', pairs))  7.73 us
    ppermute x3, waiting for transfers between devices, local(): lax.ppermute(rows, 'head', [(i, i ^ 4) for i in range(HEADS)])  6.21 us
  transfers between devices with their start and end apart: 20, of which 12 were waited for; matrix products, arithmetic and copies ran while one was open for 0% of the time, Pallas kernels for 38%

profile of v4, /device:TPU:22, one launch (start us, length us, event | category | flops | bytes accessed | tf_op | source)
XLA Modules:
  0.0 124.5 jit_solution(5386137777978089225)
XLA Ops:
  0.0 1.8 %pack.1 = bf16[3,128,256]{2,1,0:T(8,128)(2,1)} custom-call(bf16[384,128]{1,0:T(8,128)(2,1)} %keys.1, bf16[1,384]{1,0:T(2,128)(2,1)} %bitcast.12, bf16[384,128]{1,0:T(8,128)(2,1)} %values.1, bf16[1,384]{1,0:T(2,128)(2,1)} %bitcast.13), custom_call_target="tpu_custom_call" | custom-call | tf_op jit(solution)/shard_map/pack/pallas_call | solution.py:230
  1.8 0.3 collective-permute-start.3
  2.1 0.1 pad_add_fusion.info
  2.2 4.3 %cut.1 = bf16[8,512,512]{2,1,0:T(8,128)(2,1)} custom-call(s32[3]{0:T(128)S(1)} %pad_add_fusion.info, bf16[1024,8192]{1,0:T(8,128)(2,1)} %refs_3_.1), custom_call_target="tpu_custom_call" | custom-call | bytes 16777216 | tf_op jit(solution)/shard_map/cut/pallas_call | solution.py:266
  6.5 0.0 copy-start.5
  6.5 3.6 %collective-permute-done.3 = bf16[3,128,256]{2,1,0:T(8,128)(2,1)S(1)} collective-permute-done((bf16[3,128,256]{2,1,0:T(8,128)(2,1)}, bf16[3,128,256]{2,1,0:T(8,128)(2,1)S(1)}, u32[]{:S(2)}, u32[]{:S(2)}) %collective-permute-start.3) | collective-permute-done | bytes 196640 | tf_op jit(solution)/shard_map/ppermute | solution.py:452
  10.1 1.3 %collective-permute-start.11 = (bf16[8,512,512]{2,1,0:T(8,128)(2,1)}, bf16[8,512,512]{2,1,0:T(8,128)(2,1)}, u32[]{:S(2)}, u32[]{:S(2)}) collective-permute-start(bf16[8,512,512]{2,1,0:T(8,128)(2,1)} %cut.1), channel_id=1, source_target_pairs={{0,4},{1,5},{2,6},{3,7},{8,28},{9,29},{10,30},{11,31},{4,16},{5,17... | collective-permute-start | bytes 12582920 | tf_op jit(solution)/shard_map/ppermute | solution.py:455
  11.4 1.3 %collective-permute-start = (bf16[3,128,256]{2,1,0:T(8,128)(2,1)S(1)}, bf16[3,128,256]{2,1,0:T(8,128)(2,1)S(1)}, u32[]{:S(2)}, u32[]{:S(2)}) collective-permute-start(bf16[3,128,256]{2,1,0:T(8,128)(2,1)S(1)} %copy-done.3), channel_id=1, source_target_pairs={{0,32},{8,40},{16,48},{24,56},{32,64},{40,72},{48,80},{56,88},{64,... | collective-permute-start | bytes 589832 | tf_op jit(solution)/shard_map/ppermute | solution.py:289
  12.7 1.3 %collective-permute-start.1 = (bf16[3,128,256]{2,1,0:T(8,128)(2,1)S(1)}, bf16[3,128,256]{2,1,0:T(8,128)(2,1)S(1)}, u32[]{:S(2)}, u32[]{:S(2)}) collective-permute-start(bf16[3,128,256]{2,1,0:T(8,128)(2,1)S(1)} %copy-done.3), channel_id=1, source_target_pairs={{0,64},{8,72},{16,80},{24,88},{32,96},{40,104},{48,112},{56,120},{... | collective-permute-start | bytes 589832 | tf_op jit(solution)/shard_map/ppermute | solution.py:289
  14.0 1.3 %collective-permute-start.2 = (bf16[3,128,256]{2,1,0:T(8,128)(2,1)S(1)}, bf16[3,128,256]{2,1,0:T(8,128)(2,1)S(1)}, u32[]{:S(2)}, u32[]{:S(2)}) collective-permute-start(bf16[3,128,256]{2,1,0:T(8,128)(2,1)S(1)} %copy-done.3), channel_id=1, source_target_pairs={{0,96},{8,104},{16,112},{24,120},{1,97},{9,105},{17,113},{25,121},... | collective-permute-start | bytes 589832 | tf_op jit(solution)/shard_map/ppermute | solution.py:289
  15.3 3.7 %collective-permute-done = bf16[3,128,256]{2,1,0:T(8,128)(2,1)S(1)} collective-permute-done((bf16[3,128,256]{2,1,0:T(8,128)(2,1)S(1)}, bf16[3,128,256]{2,1,0:T(8,128)(2,1)S(1)}, u32[]{:S(2)}, u32[]{:S(2)}) %collective-permute-start) | collective-permute-done | bytes 196640 | tf_op jit(solution)/shard_map/ppermute | solution.py:289
  19.0 2.9 %collective-permute-done.1 = bf16[3,128,256]{2,1,0:T(8,128)(2,1)S(1)} collective-permute-done((bf16[3,128,256]{2,1,0:T(8,128)(2,1)S(1)}, bf16[3,128,256]{2,1,0:T(8,128)(2,1)S(1)}, u32[]{:S(2)}, u32[]{:S(2)}) %collective-permute-start.1) | collective-permute-done | bytes 196640 | tf_op jit(solution)/shard_map/ppermute | solution.py:289
  21.9 3.8 %collective-permute-done.2 = bf16[3,128,256]{2,1,0:T(8,128)(2,1)S(1)} collective-permute-done((bf16[3,128,256]{2,1,0:T(8,128)(2,1)S(1)}, bf16[3,128,256]{2,1,0:T(8,128)(2,1)S(1)}, u32[]{:S(2)}, u32[]{:S(2)}) %collective-permute-start.2) | collective-permute-done | bytes 196640 | tf_op jit(solution)/shard_map/ppermute | solution.py:289
  25.8 0.1 collective-permute-start.7
  25.9 0.1 fusion.1
  26.0 1.3 %collective-permute-start.4 = (bf16[3,128,256]{2,1,0:T(8,128)(2,1)S(1)}, bf16[3,128,256]{2,1,0:T(8,128)(2,1)S(1)}, u32[]{:S(2)}, u32[]{:S(2)}) collective-permute-start(bf16[3,128,256]{2,1,0:T(8,128)(2,1)S(1)} %collective-permute-done.3), channel_id=1, source_target_pairs={{0,32},{8,40},{16,48},{24,56},{32,64},{40,72},{48,80},{56,88},{64,... | collective-permute-start | bytes 589832 | tf_op jit(solution)/shard_map/ppermute | solution.py:289
  27.3 1.3 %collective-permute-start.5 = (bf16[3,128,256]{2,1,0:T(8,128)(2,1)S(1)}, bf16[3,128,256]{2,1,0:T(8,128)(2,1)S(1)}, u32[]{:S(2)}, u32[]{:S(2)}) collective-permute-start(bf16[3,128,256]{2,1,0:T(8,128)(2,1)S(1)} %collective-permute-done.3), channel_id=1, source_target_pairs={{0,64},{8,72},{16,80},{24,88},{32,96},{40,104},{48,112},{56,120},{... | collective-permute-start | bytes 589832 | tf_op jit(solution)/shard_map/ppermute | solution.py:289
  28.6 1.3 %collective-permute-start.6 = (bf16[3,128,256]{2,1,0:T(8,128)(2,1)S(1)}, bf16[3,128,256]{2,1,0:T(8,128)(2,1)S(1)}, u32[]{:S(2)}, u32[]{:S(2)}) collective-permute-start(bf16[3,128,256]{2,1,0:T(8,128)(2,1)S(1)} %collective-permute-done.3), channel_id=1, source_target_pairs={{0,96},{8,104},{16,112},{24,120},{1,97},{9,105},{17,113},{25,121},... | collective-permute-start | bytes 589832 | tf_op jit(solution)/shard_map/ppermute | solution.py:289
  29.9 12.6 %attend_first.1 = (f32[3,1,1024]{2,1,0:T(1,128)S(1)}, f32[3,1,1024]{2,1,0:T(1,128)S(1)}, f32[3,128,1024]{2,1,0:T(8,128)S(1)}) custom-call(s32[3]{0:T(128)S(1)} %get-tuple-element.86.place, s32[48,48]{1,0:T(8,128)S(1)} %copy-done.1, bf16[384,1024]{1,0:T(8,128)(2,1)S(1)} %copy-done, bf16[8,384]{1,0:T(8,128)(2,1)S(1)} %bitcast.8, ...), custom_call_target="tpu_custom_call" | custom-call | flops 3932160000 | bytes 4718592 | tf_op jit(solution)/shard_map/attend_first/pallas_call | solution.py:195
  42.7 5.3 %collective-permute-start.8 = (bf16[12,128,256]{2,1,0:T(8,128)(2,1)S(1)}, bf16[12,128,256]{2,1,0:T(8,128)(2,1)S(1)}, u32[]{:S(2)}, u32[]{:S(2)}) collective-permute-start(bf16[12,128,256]{2,1,0:T(8,128)(2,1)S(1)} %constant_dynamic-update-slice_fusion.4.mine), channel_id=1, source_target_pairs={{0,8},{8,0},{16,24},{24,16},{32,40},{40,32},{48,56},{56,48},{64,72... | collective-permute-start | bytes 2359304 | tf_op jit(solution)/shard_map/ppermute | solution.py:295
  47.9 1.9 %collective-permute-done.8.other = bf16[12,128,256]{2,1,0:T(8,128)(2,1)S(1)} collective-permute-done((bf16[12,128,256]{2,1,0:T(8,128)(2,1)S(1)}, bf16[12,128,256]{2,1,0:T(8,128)(2,1)S(1)}, u32[]{:S(2)}, u32[]{:S(2)}) %collective-permute-start.8) | collective-permute-done | bytes 786464 | tf_op jit(solution)/shard_map/ppermute | solution.py:295
  49.8 6.1 %attend_second.3.refs_0_ = bf16[128,1024]{1,0:T(8,128)(2,1)S(1)} custom-call(s32[3]{0:T(128)S(1)} %get-tuple-element.86.place, s32[48,48]{1,0:T(8,128)S(1)} %copy-done.1, bf16[384,1024]{1,0:T(8,128)(2,1)S(1)} %copy-done, bf16[8,384]{1,0:T(8,128)(2,1)S(1)} %bitcast.9, bf16[12,128,256]{2,1,0:T(8,128)(2,1)S(1)} %constant_dynamic-update-slice_fusion.4.mine, ...), custom_call_target="tpu_custom_call" | custom-call | flops 1310720000 | bytes 1572864 | tf_op jit(solution)/shard_map/attend_second/pallas_call | solution.py:208
  56.0 5.9 %attend_second.4.refs_1_ = bf16[128,1024]{1,0:T(8,128)(2,1)S(1)} custom-call(s32[3]{0:T(128)S(1)} %add.44.place, s32[48,48]{1,0:T(8,128)S(1)} %copy-done.1, bf16[384,1024]{1,0:T(8,128)(2,1)S(1)} %copy-done, bf16[8,384]{1,0:T(8,128)(2,1)S(1)} %bitcast.10, bf16[12,128,256]{2,1,0:T(8,128)(2,1)S(1)} %constant_dynamic-update-slice_fusion.4.mine, ...), custom_call_target="tpu_custom_call" | custom-call | flops 1310720000 | bytes 1572864 | tf_op jit(solution)/shard_map/attend_second/pallas_call | solution.py:208
  61.9 0.9 collective-permute-start.10
  62.8 1.2 collective-permute-start.9
  64.0 7.5 %attend_second.5.refs_2_ = bf16[128,1024]{1,0:T(8,128)(2,1)S(1)} custom-call(s32[3]{0:T(128)S(1)} %get-tuple-element.85.place, s32[48,48]{1,0:T(8,128)S(1)} %copy-done.1, bf16[384,1024]{1,0:T(8,128)(2,1)S(1)} %copy-done, bf16[8,384]{1,0:T(8,128)(2,1)S(1)} %bitcast.11, bf16[12,128,256]{2,1,0:T(8,128)(2,1)S(1)} %constant_dynamic-update-slice_fusion.4.mine, ...), custom_call_target="tpu_custom_call" | custom-call | flops 1310720000 | bytes 1572864 | tf_op jit(solution)/shard_map/attend_second/pallas_call | solution.py:208
  71.5 4.5 %collective-permute-done.9.refs_0_ = bf16[128,1024]{1,0:T(8,128)(2,1)S(1)} collective-permute-done((bf16[128,1024]{1,0:T(8,128)(2,1)S(1)}, bf16[128,1024]{1,0:T(8,128)(2,1)S(1)}, u32[]{:S(2)}, u32[]{:S(2)}) %collective-permute-start.9) | collective-permute-done | bytes 262176 | tf_op jit(solution)/shard_map/ppermute | solution.py:468
  76.0 0.9 collective-permute-start.12
  76.8 6.1 %project_own.1.refs_3_ = bf16[2,4,384,512]{3,2,1,0:T(8,128)(2,1)S(1)} custom-call(s32[3]{0:T(128)S(1)} %pad_add_fusion.info, bf16[128,1024]{1,0:T(8,128)(2,1)S(1)} %attend_second.3.refs_0_, bf16[128,1024]{1,0:T(8,128)(2,1)S(1)} %attend_second.4.refs_1_, bf16[128,1024]{1,0:T(8,128)(2,1)S(1)} %attend_second.5.refs_2_, bf16[1024,8192]{1,0:T(8,128)(2,1)} %refs_3_.1), custom_call_target="tpu_custom_call" | custom-call | flops 3221225472 | bytes 12320768 | tf_op jit(solution)/shard_map/project_own/pallas_call | solution.py:343
  83.0 1.7 %collective-permute-done.12.refs_2_ = bf16[128,1024]{1,0:T(8,128)(2,1)S(1)} collective-permute-done((bf16[128,1024]{1,0:T(8,128)(2,1)S(1)}, bf16[128,1024]{1,0:T(8,128)(2,1)S(1)}, u32[]{:S(2)}, u32[]{:S(2)}) %collective-permute-start.12) | collective-permute-done | bytes 262176 | tf_op jit(solution)/shard_map/ppermute | solution.py:468
  84.7 4.5 %project_partner.2 = (bf16[384,512]{1,0:T(8,128)(2,1)S(1)}, bf16[384,512]{1,0:T(8,128)(2,1)S(1)}, bf16[384,512]{1,0:T(8,128)(2,1)S(1)}, bf16[384,512]{1,0:T(8,128)(2,1)S(1)}) custom-call(s32[3]{0:T(128)S(1)} %pad_add_fusion.info, bf16[128,1024]{1,0:T(8,128)(2,1)S(1)} %collective-permute-done.9.refs_0_, ...), custom_call_target="tpu_custom_call" | custom-call | flops 1610612736 | bytes 7340032 | tf_op jit(solution)/shard_map/project_partner/pallas_call | solution.py:408
  89.2 2.0 %collective-permute-start.15 = (bf16[384,512]{1,0:T(8,128)(2,1)S(1)}, bf16[384,512]{1,0:T(8,128)(2,1)S(1)}, u32[]{:S(2)}, u32[]{:S(2)}) collective-permute-start(bf16[384,512]{1,0:T(8,128)(2,1)S(1)} %get-tuple-element.80), channel_id=1, source_target_pairs={{0,1},{1,2},{2,3},{3,0},{4,5},{5,6},{6,7},{7,4},{8,9},{9,10},{10,1... | collective-permute-start | bytes 1179656 | tf_op jit(solution)/shard_map/ppermute | solution.py:430
  91.2 4.5 %project_partner.3 = (bf16[384,512]{1,0:T(8,128)(2,1)S(1)}, bf16[384,512]{1,0:T(8,128)(2,1)S(1)}, bf16[384,512]{1,0:T(8,128)(2,1)S(1)}, bf16[384,512]{1,0:T(8,128)(2,1)S(1)}) custom-call(s32[3]{0:T(128)S(1)} %pad_add_fusion.info, bf16[128,1024]{1,0:T(8,128)(2,1)S(1)} %collective-permute-done.9.refs_0_, ...), custom_call_target="tpu_custom_call" | custom-call | flops 1610612736 | bytes 7340032 | tf_op jit(solution)/shard_map/project_partner/pallas_call | solution.py:408
  95.7 2.2 %collective-permute-start.18 = (bf16[384,512]{1,0:T(8,128)(2,1)S(1)}, bf16[384,512]{1,0:T(8,128)(2,1)S(1)}, u32[]{:S(2)}, u32[]{:S(2)}) collective-permute-start(bf16[384,512]{1,0:T(8,128)(2,1)S(1)} %get-tuple-element.84), channel_id=1, source_target_pairs={{0,3},{1,0},{2,1},{3,2},{4,7},{5,4},{6,5},{7,6},{8,11},{9,8},{10,9... | collective-permute-start | bytes 1179656 | tf_op jit(solution)/shard_map/ppermute | solution.py:430
  97.9 2.0 %collective-permute-start.14 = (bf16[384,512]{1,0:T(8,128)(2,1)S(1)}, bf16[384,512]{1,0:T(8,128)(2,1)S(1)}, u32[]{:S(2)}, u32[]{:S(2)}) collective-permute-start(bf16[384,512]{1,0:T(8,128)(2,1)S(1)} %get-tuple-element.78), channel_id=1, source_target_pairs={{0,3},{1,0},{2,1},{3,2},{4,7},{5,4},{6,5},{7,6},{8,11},{9,8},{10,9... | collective-permute-start | bytes 1179656 | tf_op jit(solution)/shard_map/ppermute | solution.py:430
  99.9 2.4 %collective-permute-done.15 = bf16[384,512]{1,0:T(8,128)(2,1)S(1)} collective-permute-done((bf16[384,512]{1,0:T(8,128)(2,1)S(1)}, bf16[384,512]{1,0:T(8,128)(2,1)S(1)}, u32[]{:S(2)}, u32[]{:S(2)}) %collective-permute-start.15) | collective-permute-done | bytes 393248 | tf_op jit(solution)/shard_map/ppermute | solution.py:430
  102.3 0.1 add_convert_fusion.1
  102.4 0.1 collective-permute-start.16
  102.5 1.5 %collective-permute-start.17 = (bf16[384,512]{1,0:T(8,128)(2,1)S(1)}, bf16[384,512]{1,0:T(8,128)(2,1)S(1)}, u32[]{:S(2)}, u32[]{:S(2)}) collective-permute-start(bf16[384,512]{1,0:T(8,128)(2,1)S(1)} %get-tuple-element.82), channel_id=1, source_target_pairs={{0,1},{1,2},{2,3},{3,0},{4,5},{5,6},{6,7},{7,4},{8,9},{9,10},{10,1... | collective-permute-start | bytes 1179656 | tf_op jit(solution)/shard_map/ppermute | solution.py:430
  104.0 3.8 %collective-permute-done.18 = bf16[384,512]{1,0:T(8,128)(2,1)S(1)} collective-permute-done((bf16[384,512]{1,0:T(8,128)(2,1)S(1)}, bf16[384,512]{1,0:T(8,128)(2,1)S(1)}, u32[]{:S(2)}, u32[]{:S(2)}) %collective-permute-start.18) | collective-permute-done | bytes 393248 | tf_op jit(solution)/shard_map/ppermute | solution.py:430
  107.8 0.1 add_convert_fusion
  107.9 3.4 %collective-permute-start.19 = (bf16[384,512]{1,0:T(8,128)(2,1)S(1)}, bf16[384,512]{1,0:T(8,128)(2,1)S(1)}, u32[]{:S(2)}, u32[]{:S(2)}) collective-permute-start(bf16[384,512]{1,0:T(8,128)(2,1)S(1)} %add_convert_fusion), channel_id=1, source_target_pairs={{0,3},{1,0},{2,1},{3,2},{4,7},{5,4},{6,5},{7,6},{8,11},{9,8},{10,9... | collective-permute-start | bytes 1179656 | tf_op jit(solution)/shard_map/ppermute | solution.py:430
  111.3 4.9 %collective-permute-done.14 = bf16[384,512]{1,0:T(8,128)(2,1)S(1)} collective-permute-done((bf16[384,512]{1,0:T(8,128)(2,1)S(1)}, bf16[384,512]{1,0:T(8,128)(2,1)S(1)}, u32[]{:S(2)}, u32[]{:S(2)}) %collective-permute-start.14) | collective-permute-done | bytes 393248 | tf_op jit(solution)/shard_map/ppermute | solution.py:430
  116.3 0.1 convert_add_fusion.1
  116.4 5.9 %collective-permute-done.17 = bf16[384,512]{1,0:T(8,128)(2,1)S(1)} collective-permute-done((bf16[384,512]{1,0:T(8,128)(2,1)S(1)}, bf16[384,512]{1,0:T(8,128)(2,1)S(1)}, u32[]{:S(2)}, u32[]{:S(2)}) %collective-permute-start.17) | collective-permute-done | bytes 393248 | tf_op jit(solution)/shard_map/ppermute | solution.py:430
  122.3 1.0 collective-permute-done.19
  123.3 0.1 convert_add_fusion
  123.5 1.0 fusion
  (31 shorter events, 0.2 us)
Async XLA Ops:
  1.8 8.4 %collective-permute-start.3 = (bf16[3,128,256]{2,1,0:T(8,128)(2,1)}, bf16[3,128,256]{2,1,0:T(8,128)(2,1)S(1)}, u32[]{:S(2)}, u32[]{:S(2)}) collective-permute-start(bf16[3,128,256]{2,1,0:T(8,128)(2,1)} %pack.1), channel_id=1, source_target_pairs={{0,16},{8,24},{16,0},{24,8},{32,48},{40,56},{48,32},{56,40},{64,80... | collective-permute-start | bytes 589832 | tf_op jit(solution)/shard_map/ppermute | solution.py:452
  2.2 9.2 %copy-start.3 = (bf16[3,128,256]{2,1,0:T(8,128)(2,1)S(1)}, bf16[3,128,256]{2,1,0:T(8,128)(2,1)}, u32[]{:S(2)}) copy-start(bf16[3,128,256]{2,1,0:T(8,128)(2,1)} %pack.1) | copy-start | bytes 589828
  6.5 19.4 %copy-start.5 = (s32[3]{0:T(128)S(1)}, s32[3]{0:T(128)}, u32[]{:S(2)}) copy-start(s32[3]{0:T(128)} %constant.62.clone) | copy-start | bytes 40
  6.5 23.4 %copy-start = (bf16[384,1024]{1,0:T(8,128)(2,1)S(1)}, bf16[384,1024]{1,0:T(8,128)(2,1)}, u32[]{:S(2)}) copy-start(bf16[384,1024]{1,0:T(8,128)(2,1)} %q_ref.7) | copy-start | bytes 2359300
  6.5 23.4 %copy-start.1 = (s32[48,48]{1,0:T(8,128)S(1)}, s32[48,48]{1,0:T(8,128)}, u32[]{:S(2)}) copy-start(s32[48,48]{1,0:T(8,128)} %mask.7) | copy-start | bytes 27652
  6.5 23.4 %copy-start.2 = (bf16[384,8]{0,1:T(8,128)(2,1)S(1)}, bf16[384,8]{0,1:T(8,128)(2,1)}, u32[]{:S(2)}) copy-start(bf16[384,8]{0,1:T(8,128)(2,1)} %param.14) | copy-start | bytes 18436
  10.1 65.8 %collective-permute-start.11 = (bf16[8,512,512]{2,1,0:T(8,128)(2,1)}, bf16[8,512,512]{2,1,0:T(8,128)(2,1)}, u32[]{:S(2)}, u32[]{:S(2)}) collective-permute-start(bf16[8,512,512]{2,1,0:T(8,128)(2,1)} %cut.1), channel_id=1, source_target_pairs={{0,4},{1,5},{2,6},{3,7},{8,28},{9,29},{10,30},{11,31},{4,16},{5,17... | collective-permute-start | bytes 12582920 | tf_op jit(solution)/shard_map/ppermute | solution.py:455
  11.4 7.6 %collective-permute-start = (bf16[3,128,256]{2,1,0:T(8,128)(2,1)S(1)}, bf16[3,128,256]{2,1,0:T(8,128)(2,1)S(1)}, u32[]{:S(2)}, u32[]{:S(2)}) collective-permute-start(bf16[3,128,256]{2,1,0:T(8,128)(2,1)S(1)} %copy-done.3), channel_id=1, source_target_pairs={{0,32},{8,40},{16,48},{24,56},{32,64},{40,72},{48,80},{56,88},{64,... | collective-permute-start | bytes 589832 | tf_op jit(solution)/shard_map/ppermute | solution.py:289
  12.7 9.2 %collective-permute-start.1 = (bf16[3,128,256]{2,1,0:T(8,128)(2,1)S(1)}, bf16[3,128,256]{2,1,0:T(8,128)(2,1)S(1)}, u32[]{:S(2)}, u32[]{:S(2)}) collective-permute-start(bf16[3,128,256]{2,1,0:T(8,128)(2,1)S(1)} %copy-done.3), channel_id=1, source_target_pairs={{0,64},{8,72},{16,80},{24,88},{32,96},{40,104},{48,112},{56,120},{... | collective-permute-start | bytes 589832 | tf_op jit(solution)/shard_map/ppermute | solution.py:289
  14.0 11.7 %collective-permute-start.2 = (bf16[3,128,256]{2,1,0:T(8,128)(2,1)S(1)}, bf16[3,128,256]{2,1,0:T(8,128)(2,1)S(1)}, u32[]{:S(2)}, u32[]{:S(2)}) collective-permute-start(bf16[3,128,256]{2,1,0:T(8,128)(2,1)S(1)} %copy-done.3), channel_id=1, source_target_pairs={{0,96},{8,104},{16,112},{24,120},{1,97},{9,105},{17,113},{25,121},... | collective-permute-start | bytes 589832 | tf_op jit(solution)/shard_map/ppermute | solution.py:289
  25.8 4.1 %collective-permute-start.7 = (bf16[12,128,256]{2,1,0:T(8,128)(2,1)S(1)}, bf16[12,128,256]{2,1,0:T(8,128)(2,1)S(1)}, u32[]{:S(2)}, u32[]{:S(2)}) collective-permute-start(bf16[12,128,256]{2,1,0:T(8,128)(2,1)S(1)} %constant_dynamic-update-slice_fusion.mine), channel_id=1, source_target_pairs={{0,8},{8,0},{16,24},{24,16},{32,40},{40,32},{48,56},{56,48},{64,72... | collective-permute-start | bytes 2359304 | tf_op jit(solution)/shard_map/ppermute | solution.py:295
  26.0 16.6 %collective-permute-start.4 = (bf16[3,128,256]{2,1,0:T(8,128)(2,1)S(1)}, bf16[3,128,256]{2,1,0:T(8,128)(2,1)S(1)}, u32[]{:S(2)}, u32[]{:S(2)}) collective-permute-start(bf16[3,128,256]{2,1,0:T(8,128)(2,1)S(1)} %collective-permute-done.3), channel_id=1, source_target_pairs={{0,32},{8,40},{16,48},{24,56},{32,64},{40,72},{48,80},{56,88},{64,... | collective-permute-start | bytes 589832 | tf_op jit(solution)/shard_map/ppermute | solution.py:289
  27.3 15.3 %collective-permute-start.5 = (bf16[3,128,256]{2,1,0:T(8,128)(2,1)S(1)}, bf16[3,128,256]{2,1,0:T(8,128)(2,1)S(1)}, u32[]{:S(2)}, u32[]{:S(2)}) collective-permute-start(bf16[3,128,256]{2,1,0:T(8,128)(2,1)S(1)} %collective-permute-done.3), channel_id=1, source_target_pairs={{0,64},{8,72},{16,80},{24,88},{32,96},{40,104},{48,112},{56,120},{... | collective-permute-start | bytes 589832 | tf_op jit(solution)/shard_map/ppermute | solution.py:289
  28.6 14.0 %collective-permute-start.6 = (bf16[3,128,256]{2,1,0:T(8,128)(2,1)S(1)}, bf16[3,128,256]{2,1,0:T(8,128)(2,1)S(1)}, u32[]{:S(2)}, u32[]{:S(2)}) collective-permute-start(bf16[3,128,256]{2,1,0:T(8,128)(2,1)S(1)} %collective-permute-done.3), channel_id=1, source_target_pairs={{0,96},{8,104},{16,112},{24,120},{1,97},{9,105},{17,113},{25,121},... | collective-permute-start | bytes 589832 | tf_op jit(solution)/shard_map/ppermute | solution.py:289
  42.5 5.4 %copy-start.6 = (s32[3]{0:T(128)S(1)}, s32[3]{0:T(128)}, u32[]{:S(2)}) copy-start(s32[3]{0:T(128)} %constant.61.clone) | copy-start | bytes 40
  42.7 7.2 %collective-permute-start.8 = (bf16[12,128,256]{2,1,0:T(8,128)(2,1)S(1)}, bf16[12,128,256]{2,1,0:T(8,128)(2,1)S(1)}, u32[]{:S(2)}, u32[]{:S(2)}) collective-permute-start(bf16[12,128,256]{2,1,0:T(8,128)(2,1)S(1)} %constant_dynamic-update-slice_fusion.4.mine), channel_id=1, source_target_pairs={{0,8},{8,0},{16,24},{24,16},{32,40},{40,32},{48,56},{56,48},{64,72... | collective-permute-start | bytes 2359304 | tf_op jit(solution)/shard_map/ppermute | solution.py:295
  61.9 9.6 %collective-permute-start.10 = (bf16[128,1024]{1,0:T(8,128)(2,1)S(1)}, bf16[128,1024]{1,0:T(8,128)(2,1)S(1)}, u32[]{:S(2)}, u32[]{:S(2)}) collective-permute-start(bf16[128,1024]{1,0:T(8,128)(2,1)S(1)} %attend_second.4.refs_1_), channel_id=1, source_target_pairs={{0,4},{1,5},{2,6},{3,7},{4,0},{5,1},{6,2},{7,3},{8,12},{9,13},{10,... | collective-permute-start | bytes 786440 | tf_op jit(solution)/shard_map/ppermute | solution.py:468
  62.8 13.1 %collective-permute-start.9 = (bf16[128,1024]{1,0:T(8,128)(2,1)S(1)}, bf16[128,1024]{1,0:T(8,128)(2,1)S(1)}, u32[]{:S(2)}, u32[]{:S(2)}) collective-permute-start(bf16[128,1024]{1,0:T(8,128)(2,1)S(1)} %attend_second.3.refs_0_), channel_id=1, source_target_pairs={{0,4},{1,5},{2,6},{3,7},{4,0},{5,1},{6,2},{7,3},{8,12},{9,13},{10,... | collective-permute-start | bytes 786440 | tf_op jit(solution)/shard_map/ppermute | solution.py:468
  76.0 8.7 %collective-permute-start.13 = (bf16[8,512,512]{2,1,0:T(8,128)(2,1)}, bf16[8,512,512]{2,1,0:T(8,128)(2,1)S(1)}, u32[]{:S(2)}, u32[]{:S(2)}) collective-permute-start(bf16[8,512,512]{2,1,0:T(8,128)(2,1)} %collective-permute-done.11.refs_4_), channel_id=1, source_target_pairs={{0,8},{8,0},{16,24},{24,16},{32,40},{40,32},{48,56},{56,48},{64,72... | collective-permute-start | bytes 12582920 | tf_op jit(solution)/shard_map/ppermute | solution.py:471
  76.0 8.7 %collective-permute-start.12 = (bf16[128,1024]{1,0:T(8,128)(2,1)S(1)}, bf16[128,1024]{1,0:T(8,128)(2,1)S(1)}, u32[]{:S(2)}, u32[]{:S(2)}) collective-permute-start(bf16[128,1024]{1,0:T(8,128)(2,1)S(1)} %attend_second.5.refs_2_), channel_id=1, source_target_pairs={{0,4},{1,5},{2,6},{3,7},{4,0},{5,1},{6,2},{7,3},{8,12},{9,13},{10,... | collective-permute-start | bytes 786440 | tf_op jit(solution)/shard_map/ppermute | solution.py:468
  89.2 13.1 %collective-permute-start.15 = (bf16[384,512]{1,0:T(8,128)(2,1)S(1)}, bf16[384,512]{1,0:T(8,128)(2,1)S(1)}, u32[]{:S(2)}, u32[]{:S(2)}) collective-permute-start(bf16[384,512]{1,0:T(8,128)(2,1)S(1)} %get-tuple-element.80), channel_id=1, source_target_pairs={{0,1},{1,2},{2,3},{3,0},{4,5},{5,6},{6,7},{7,4},{8,9},{9,10},{10,1... | collective-permute-start | bytes 1179656 | tf_op jit(solution)/shard_map/ppermute | solution.py:430
  95.7 12.1 %collective-permute-start.18 = (bf16[384,512]{1,0:T(8,128)(2,1)S(1)}, bf16[384,512]{1,0:T(8,128)(2,1)S(1)}, u32[]{:S(2)}, u32[]{:S(2)}) collective-permute-start(bf16[384,512]{1,0:T(8,128)(2,1)S(1)} %get-tuple-element.84), channel_id=1, source_target_pairs={{0,3},{1,0},{2,1},{3,2},{4,7},{5,4},{6,5},{7,6},{8,11},{9,8},{10,9... | collective-permute-start | bytes 1179656 | tf_op jit(solution)/shard_map/ppermute | solution.py:430
  97.9 18.3 %collective-permute-start.14 = (bf16[384,512]{1,0:T(8,128)(2,1)S(1)}, bf16[384,512]{1,0:T(8,128)(2,1)S(1)}, u32[]{:S(2)}, u32[]{:S(2)}) collective-permute-start(bf16[384,512]{1,0:T(8,128)(2,1)S(1)} %get-tuple-element.78), channel_id=1, source_target_pairs={{0,3},{1,0},{2,1},{3,2},{4,7},{5,4},{6,5},{7,6},{8,11},{9,8},{10,9... | collective-permute-start | bytes 1179656 | tf_op jit(solution)/shard_map/ppermute | solution.py:430
  102.4 13.8 %collective-permute-start.16 = (bf16[384,512]{1,0:T(8,128)(2,1)S(1)}, bf16[384,512]{1,0:T(8,128)(2,1)S(1)}, u32[]{:S(2)}, u32[]{:S(2)}) collective-permute-start(bf16[384,512]{1,0:T(8,128)(2,1)S(1)} %add_convert_fusion.1), channel_id=1, source_target_pairs={{0,1},{1,2},{2,3},{3,0},{4,5},{5,6},{6,7},{7,4},{8,9},{9,10},{10,1... | collective-permute-start | bytes 1179656 | tf_op jit(solution)/shard_map/ppermute | solution.py:430
  102.5 19.8 %collective-permute-start.17 = (bf16[384,512]{1,0:T(8,128)(2,1)S(1)}, bf16[384,512]{1,0:T(8,128)(2,1)S(1)}, u32[]{:S(2)}, u32[]{:S(2)}) collective-permute-start(bf16[384,512]{1,0:T(8,128)(2,1)S(1)} %get-tuple-element.82), channel_id=1, source_target_pairs={{0,1},{1,2},{2,3},{3,0},{4,5},{5,6},{6,7},{7,4},{8,9},{9,10},{10,1... | collective-permute-start | bytes 1179656 | tf_op jit(solution)/shard_map/ppermute | solution.py:430
  107.9 15.4 %collective-permute-start.19 = (bf16[384,512]{1,0:T(8,128)(2,1)S(1)}, bf16[384,512]{1,0:T(8,128)(2,1)S(1)}, u32[]{:S(2)}, u32[]{:S(2)}) collective-permute-start(bf16[384,512]{1,0:T(8,128)(2,1)S(1)} %add_convert_fusion), channel_id=1, source_target_pairs={{0,3},{1,0},{2,1},{3,2},{4,7},{5,4},{6,5},{7,6},{8,11},{9,8},{10,9... | collective-permute-start | bytes 1179656 | tf_op jit(solution)/shard_map/ppermute | solution.py:430
  116.3 7.2 %copy-start.4 = (f32[1024]{0:T(1024)S(1)}, f32[1024]{0:T(1024)}, u32[]{:S(2)}) copy-start(f32[1024]{0:T(1024)} %param.21) | copy-start | bytes 12292

commit v5 on v4

--- a/solution.py
+++ b/solution.py
@@ -466,7 +466,9 @@
         rows, state = lax.optimization_barrier((rows, state))
         own.append(rows)
         partner.append(lax.ppermute(rows, "head", [(i, i ^ 4) for i in range(HEADS)]))
-    own, partner[:2], near = lax.optimization_barrier((own, partner[:2], near))
+        if at == 1:
+            partner[0], state = lax.optimization_barrier((partner[0], state))
+    own, partner[1], near = lax.optimization_barrier((own, partner[1], near))
     base = project_own(info, own, out_weight)
     far = lax.ppermute(near, "ctx", CORE_SWAP)
     parts = []

time: 126 us -> 122 us (0.968)
  waiting for transfers between devices: 40.1 us -> 35.5 us
    ppermute x3, waiting for transfers between devices: 6.21 us -> 1.63 us  [local(): lax.ppermute(rows, 'head', [(i, i ^ 4) for i in range(HEADS)])]
  transfers between devices with their start and end apart: 20 -> 20, of which waited for: 12 -> 11; matrix products, arithmetic and copies ran while one was open for 0% -> 1% of each run, Pallas kernels for 38% -> 39%
where the time goes in v5:
time: 122 us
  Pallas kernels  54 us (44%)
  waiting for transfers between devices  35.5 us (29%)
  starting transfers between devices  29.8 us (24%)
  other arithmetic  1.67 us (1%)
    pallas_call x3, Pallas kernels, attend(): pl.pallas_call(second_kernel, in_specs=in_specs + held, out_specs=pl.Bloc...  20 us
    ppermute x6, waiting for transfers between devices, ring(): lax.ppermute(block, 'head', [(i, i // 4 * 4 + (i + step) % 4) for i in ra...  17.9 us
    pallas_call x1, Pallas kernels, attend(): pl.pallas_call(first_kernel, in_specs=in_specs, out_specs=held, out_shape...  12.8 us
    ppermute x6, starting transfers between devices, ring(): lax.ppermute(block, 'head', [(i, i // 4 * 4 + (i + step) % 4) for i in ra...  11.2 us
    ppermute x6, waiting for transfers between devices, along_x(): got.append(lax.ppermute(block, 'ctx', pairs))  10.4 us
    pallas_call x2, Pallas kernels, project_partner(): pl.pallas_call(functools.partial(partner_kernel, part), in_specs=[pl.Bloc...  9.04 us
    ppermute x6, starting transfers between devices, along_x(): got.append(lax.ppermute(block, 'ctx', pairs))  7.73 us
    pallas_call x1, Pallas kernels, project_own(): pl.pallas_call(own_kernel, in_specs=[pl.BlockSpec(memory_space=pltpu.SMEM...  6.15 us
  transfers between devices with their start and end apart: 20, of which 11 were waited for; matrix products, arithmetic and copies ran while one was open for 1% of the time, Pallas kernels for 39%

profile of v5, /device:TPU:22, one launch (start us, length us, event | category | flops | bytes accessed | tf_op | source)
XLA Modules:
  0.0 121.5 jit_solution(48490669660993097)
XLA Ops:
  0.0 1.8 %pack.1 = bf16[3,128,256]{2,1,0:T(8,128)(2,1)} custom-call(bf16[384,128]{1,0:T(8,128)(2,1)} %keys.1, bf16[1,384]{1,0:T(2,128)(2,1)} %bitcast.12, bf16[384,128]{1,0:T(8,128)(2,1)} %values.1, bf16[1,384]{1,0:T(2,128)(2,1)} %bitcast.13), custom_call_target="tpu_custom_call" | custom-call | tf_op jit(solution)/shard_map/pack/pallas_call | solution.py:230
  1.8 0.3 collective-permute-start.3
  2.1 0.1 pad_add_fusion.info
  2.2 4.3 %cut.1 = bf16[8,512,512]{2,1,0:T(8,128)(2,1)} custom-call(s32[3]{0:T(128)S(1)} %pad_add_fusion.info, bf16[1024,8192]{1,0:T(8,128)(2,1)} %refs_3_.1), custom_call_target="tpu_custom_call" | custom-call | bytes 16777216 | tf_op jit(solution)/shard_map/cut/pallas_call | solution.py:266
  6.5 0.0 copy-start.5
  6.5 3.6 %collective-permute-done.3 = bf16[3,128,256]{2,1,0:T(8,128)(2,1)S(1)} collective-permute-done((bf16[3,128,256]{2,1,0:T(8,128)(2,1)}, bf16[3,128,256]{2,1,0:T(8,128)(2,1)S(1)}, u32[]{:S(2)}, u32[]{:S(2)}) %collective-permute-start.3) | collective-permute-done | bytes 196640 | tf_op jit(solution)/shard_map/ppermute | solution.py:452
  10.1 1.3 %collective-permute-start.11 = (bf16[8,512,512]{2,1,0:T(8,128)(2,1)}, bf16[8,512,512]{2,1,0:T(8,128)(2,1)}, u32[]{:S(2)}, u32[]{:S(2)}) collective-permute-start(bf16[8,512,512]{2,1,0:T(8,128)(2,1)} %cut.1), channel_id=1, source_target_pairs={{0,4},{1,5},{2,6},{3,7},{8,28},{9,29},{10,30},{11,31},{4,16},{5,17... | collective-permute-start | bytes 12582920 | tf_op jit(solution)/shard_map/ppermute | solution.py:455
  11.4 1.3 %collective-permute-start = (bf16[3,128,256]{2,1,0:T(8,128)(2,1)S(1)}, bf16[3,128,256]{2,1,0:T(8,128)(2,1)S(1)}, u32[]{:S(2)}, u32[]{:S(2)}) collective-permute-start(bf16[3,128,256]{2,1,0:T(8,128)(2,1)S(1)} %copy-done.3), channel_id=1, source_target_pairs={{0,32},{8,40},{16,48},{24,56},{32,64},{40,72},{48,80},{56,88},{64,... | collective-permute-start | bytes 589832 | tf_op jit(solution)/shard_map/ppermute | solution.py:289
  12.7 1.3 %collective-permute-start.1 = (bf16[3,128,256]{2,1,0:T(8,128)(2,1)S(1)}, bf16[3,128,256]{2,1,0:T(8,128)(2,1)S(1)}, u32[]{:S(2)}, u32[]{:S(2)}) collective-permute-start(bf16[3,128,256]{2,1,0:T(8,128)(2,1)S(1)} %copy-done.3), channel_id=1, source_target_pairs={{0,64},{8,72},{16,80},{24,88},{32,96},{40,104},{48,112},{56,120},{... | collective-permute-start | bytes 589832 | tf_op jit(solution)/shard_map/ppermute | solution.py:289
  14.0 1.3 %collective-permute-start.2 = (bf16[3,128,256]{2,1,0:T(8,128)(2,1)S(1)}, bf16[3,128,256]{2,1,0:T(8,128)(2,1)S(1)}, u32[]{:S(2)}, u32[]{:S(2)}) collective-permute-start(bf16[3,128,256]{2,1,0:T(8,128)(2,1)S(1)} %copy-done.3), channel_id=1, source_target_pairs={{0,96},{8,104},{16,112},{24,120},{1,97},{9,105},{17,113},{25,121},... | collective-permute-start | bytes 589832 | tf_op jit(solution)/shard_map/ppermute | solution.py:289
  15.3 3.7 %collective-permute-done = bf16[3,128,256]{2,1,0:T(8,128)(2,1)S(1)} collective-permute-done((bf16[3,128,256]{2,1,0:T(8,128)(2,1)S(1)}, bf16[3,128,256]{2,1,0:T(8,128)(2,1)S(1)}, u32[]{:S(2)}, u32[]{:S(2)}) %collective-permute-start) | collective-permute-done | bytes 196640 | tf_op jit(solution)/shard_map/ppermute | solution.py:289
  19.0 2.9 %collective-permute-done.1 = bf16[3,128,256]{2,1,0:T(8,128)(2,1)S(1)} collective-permute-done((bf16[3,128,256]{2,1,0:T(8,128)(2,1)S(1)}, bf16[3,128,256]{2,1,0:T(8,128)(2,1)S(1)}, u32[]{:S(2)}, u32[]{:S(2)}) %collective-permute-start.1) | collective-permute-done | bytes 196640 | tf_op jit(solution)/shard_map/ppermute | solution.py:289
  21.9 3.8 %collective-permute-done.2 = bf16[3,128,256]{2,1,0:T(8,128)(2,1)S(1)} collective-permute-done((bf16[3,128,256]{2,1,0:T(8,128)(2,1)S(1)}, bf16[3,128,256]{2,1,0:T(8,128)(2,1)S(1)}, u32[]{:S(2)}, u32[]{:S(2)}) %collective-permute-start.2) | collective-permute-done | bytes 196640 | tf_op jit(solution)/shard_map/ppermute | solution.py:289
  25.8 0.1 collective-permute-start.7
  25.9 0.1 fusion.1
  26.0 1.3 %collective-permute-start.4 = (bf16[3,128,256]{2,1,0:T(8,128)(2,1)S(1)}, bf16[3,128,256]{2,1,0:T(8,128)(2,1)S(1)}, u32[]{:S(2)}, u32[]{:S(2)}) collective-permute-start(bf16[3,128,256]{2,1,0:T(8,128)(2,1)S(1)} %collective-permute-done.3), channel_id=1, source_target_pairs={{0,32},{8,40},{16,48},{24,56},{32,64},{40,72},{48,80},{56,88},{64,... | collective-permute-start | bytes 589832 | tf_op jit(solution)/shard_map/ppermute | solution.py:289
  27.3 1.3 %collective-permute-start.5 = (bf16[3,128,256]{2,1,0:T(8,128)(2,1)S(1)}, bf16[3,128,256]{2,1,0:T(8,128)(2,1)S(1)}, u32[]{:S(2)}, u32[]{:S(2)}) collective-permute-start(bf16[3,128,256]{2,1,0:T(8,128)(2,1)S(1)} %collective-permute-done.3), channel_id=1, source_target_pairs={{0,64},{8,72},{16,80},{24,88},{32,96},{40,104},{48,112},{56,120},{... | collective-permute-start | bytes 589832 | tf_op jit(solution)/shard_map/ppermute | solution.py:289
  28.6 1.3 %collective-permute-start.6 = (bf16[3,128,256]{2,1,0:T(8,128)(2,1)S(1)}, bf16[3,128,256]{2,1,0:T(8,128)(2,1)S(1)}, u32[]{:S(2)}, u32[]{:S(2)}) collective-permute-start(bf16[3,128,256]{2,1,0:T(8,128)(2,1)S(1)} %collective-permute-done.3), channel_id=1, source_target_pairs={{0,96},{8,104},{16,112},{24,120},{1,97},{9,105},{17,113},{25,121},... | collective-permute-start | bytes 589832 | tf_op jit(solution)/shard_map/ppermute | solution.py:289
  29.9 12.8 %attend_first.1 = (f32[3,1,1024]{2,1,0:T(1,128)S(1)}, f32[3,1,1024]{2,1,0:T(1,128)S(1)}, f32[3,128,1024]{2,1,0:T(8,128)S(1)}) custom-call(s32[3]{0:T(128)S(1)} %get-tuple-element.92.place, s32[48,48]{1,0:T(8,128)S(1)} %copy-done.1, bf16[384,1024]{1,0:T(8,128)(2,1)S(1)} %copy-done, bf16[8,384]{1,0:T(8,128)(2,1)S(1)} %bitcast.8, ...), custom_call_target="tpu_custom_call" | custom-call | flops 3932160000 | bytes 4718592 | tf_op jit(solution)/shard_map/attend_first/pallas_call | solution.py:195
  42.8 6.0 %collective-permute-start.8 = (bf16[12,128,256]{2,1,0:T(8,128)(2,1)S(1)}, bf16[12,128,256]{2,1,0:T(8,128)(2,1)S(1)}, u32[]{:S(2)}, u32[]{:S(2)}) collective-permute-start(bf16[12,128,256]{2,1,0:T(8,128)(2,1)S(1)} %constant_dynamic-update-slice_fusion.4.mine), channel_id=1, source_target_pairs={{0,8},{8,0},{16,24},{24,16},{32,40},{40,32},{48,56},{56,48},{64,72... | collective-permute-start | bytes 2359304 | tf_op jit(solution)/shard_map/ppermute | solution.py:295
  48.8 1.9 %collective-permute-done.8.other = bf16[12,128,256]{2,1,0:T(8,128)(2,1)S(1)} collective-permute-done((bf16[12,128,256]{2,1,0:T(8,128)(2,1)S(1)}, bf16[12,128,256]{2,1,0:T(8,128)(2,1)S(1)}, u32[]{:S(2)}, u32[]{:S(2)}) %collective-permute-start.8) | collective-permute-done | bytes 786464 | tf_op jit(solution)/shard_map/ppermute | solution.py:295
  50.7 7.0 %attend_second.3.refs_0_ = bf16[128,1024]{1,0:T(8,128)(2,1)S(1)} custom-call(s32[3]{0:T(128)S(1)} %get-tuple-element.92.place, s32[48,48]{1,0:T(8,128)S(1)} %copy-done.1, bf16[384,1024]{1,0:T(8,128)(2,1)S(1)} %copy-done, bf16[8,384]{1,0:T(8,128)(2,1)S(1)} %bitcast.9, bf16[12,128,256]{2,1,0:T(8,128)(2,1)S(1)} %constant_dynamic-update-slice_fusion.4.mine, ...), custom_call_target="tpu_custom_call" | custom-call | flops 1310720000 | bytes 1572864 | tf_op jit(solution)/shard_map/attend_second/pallas_call | solution.py:208
  57.7 0.9 collective-permute-start.9
  58.7 7.0 %attend_second.4.refs_1_ = bf16[128,1024]{1,0:T(8,128)(2,1)S(1)} custom-call(s32[3]{0:T(128)S(1)} %add.44.place, s32[48,48]{1,0:T(8,128)S(1)} %copy-done.1, bf16[384,1024]{1,0:T(8,128)(2,1)S(1)} %copy-done, bf16[8,384]{1,0:T(8,128)(2,1)S(1)} %bitcast.10, bf16[12,128,256]{2,1,0:T(8,128)(2,1)S(1)} %constant_dynamic-update-slice_fusion.4.mine, ...), custom_call_target="tpu_custom_call" | custom-call | flops 1310720000 | bytes 1572864 | tf_op jit(solution)/shard_map/attend_second/pallas_call | solution.py:208
  65.6 1.2 %collective-permute-start.10 = (bf16[128,1024]{1,0:T(8,128)(2,1)S(1)}, bf16[128,1024]{1,0:T(8,128)(2,1)S(1)}, u32[]{:S(2)}, u32[]{:S(2)}) collective-permute-start(bf16[128,1024]{1,0:T(8,128)(2,1)S(1)} %attend_second.4.refs_1_), channel_id=1, source_target_pairs={{0,4},{1,5},{2,6},{3,7},{4,0},{5,1},{6,2},{7,3},{8,12},{9,13},{10,... | collective-permute-start | bytes 786440 | tf_op jit(solution)/shard_map/ppermute | solution.py:468
  66.9 6.1 %attend_second.5.refs_2_ = bf16[128,1024]{1,0:T(8,128)(2,1)S(1)} custom-call(s32[3]{0:T(128)S(1)} %get-tuple-element.91.place, s32[48,48]{1,0:T(8,128)S(1)} %copy-done.1, bf16[384,1024]{1,0:T(8,128)(2,1)S(1)} %copy-done, bf16[8,384]{1,0:T(8,128)(2,1)S(1)} %bitcast.11, bf16[12,128,256]{2,1,0:T(8,128)(2,1)S(1)} %constant_dynamic-update-slice_fusion.4.mine, ...), custom_call_target="tpu_custom_call" | custom-call | flops 1310720000 | bytes 1572864 | tf_op jit(solution)/shard_map/attend_second/pallas_call | solution.py:208
  73.0 0.1 collective-permute-start.13
  73.1 0.9 collective-permute-start.12
  74.0 6.1 %project_own.1.refs_3_ = bf16[2,4,384,512]{3,2,1,0:T(8,128)(2,1)S(1)} custom-call(s32[3]{0:T(128)S(1)} %pad_add_fusion.info, bf16[128,1024]{1,0:T(8,128)(2,1)S(1)} %attend_second.3.refs_0_, bf16[128,1024]{1,0:T(8,128)(2,1)S(1)} %attend_second.4.refs_1_, bf16[128,1024]{1,0:T(8,128)(2,1)S(1)} %attend_second.5.refs_2_, bf16[1024,8192]{1,0:T(8,128)(2,1)} %refs_3_.1), custom_call_target="tpu_custom_call" | custom-call | flops 3221225472 | bytes 12320768 | tf_op jit(solution)/shard_map/project_own/pallas_call | solution.py:343
  80.2 1.6 %collective-permute-done.12.refs_2_ = bf16[128,1024]{1,0:T(8,128)(2,1)S(1)} collective-permute-done((bf16[128,1024]{1,0:T(8,128)(2,1)S(1)}, bf16[128,1024]{1,0:T(8,128)(2,1)S(1)}, u32[]{:S(2)}, u32[]{:S(2)}) %collective-permute-start.12) | collective-permute-done | bytes 262176 | tf_op jit(solution)/shard_map/ppermute | solution.py:468
  81.8 4.5 %project_partner.2 = (bf16[384,512]{1,0:T(8,128)(2,1)S(1)}, bf16[384,512]{1,0:T(8,128)(2,1)S(1)}, bf16[384,512]{1,0:T(8,128)(2,1)S(1)}, bf16[384,512]{1,0:T(8,128)(2,1)S(1)}) custom-call(s32[3]{0:T(128)S(1)} %pad_add_fusion.info, bf16[128,1024]{1,0:T(8,128)(2,1)S(1)} %collective-permute-done.9.refs_0_, ...), custom_call_target="tpu_custom_call" | custom-call | flops 1610612736 | bytes 7340032 | tf_op jit(solution)/shard_map/project_partner/pallas_call | solution.py:408
  86.3 2.0 %collective-permute-start.15 = (bf16[384,512]{1,0:T(8,128)(2,1)S(1)}, bf16[384,512]{1,0:T(8,128)(2,1)S(1)}, u32[]{:S(2)}, u32[]{:S(2)}) collective-permute-start(bf16[384,512]{1,0:T(8,128)(2,1)S(1)} %get-tuple-element.86), channel_id=1, source_target_pairs={{0,1},{1,2},{2,3},{3,0},{4,5},{5,6},{6,7},{7,4},{8,9},{9,10},{10,1... | collective-permute-start | bytes 1179656 | tf_op jit(solution)/shard_map/ppermute | solution.py:430
  88.3 4.5 %project_partner.3 = (bf16[384,512]{1,0:T(8,128)(2,1)S(1)}, bf16[384,512]{1,0:T(8,128)(2,1)S(1)}, bf16[384,512]{1,0:T(8,128)(2,1)S(1)}, bf16[384,512]{1,0:T(8,128)(2,1)S(1)}) custom-call(s32[3]{0:T(128)S(1)} %pad_add_fusion.info, bf16[128,1024]{1,0:T(8,128)(2,1)S(1)} %collective-permute-done.9.refs_0_, ...), custom_call_target="tpu_custom_call" | custom-call | flops 1610612736 | bytes 7340032 | tf_op jit(solution)/shard_map/project_partner/pallas_call | solution.py:408
  92.8 2.2 %collective-permute-start.18 = (bf16[384,512]{1,0:T(8,128)(2,1)S(1)}, bf16[384,512]{1,0:T(8,128)(2,1)S(1)}, u32[]{:S(2)}, u32[]{:S(2)}) collective-permute-start(bf16[384,512]{1,0:T(8,128)(2,1)S(1)} %get-tuple-element.90), channel_id=1, source_target_pairs={{0,3},{1,0},{2,1},{3,2},{4,7},{5,4},{6,5},{7,6},{8,11},{9,8},{10,9... | collective-permute-start | bytes 1179656 | tf_op jit(solution)/shard_map/ppermute | solution.py:430
  95.0 2.0 %collective-permute-start.14 = (bf16[384,512]{1,0:T(8,128)(2,1)S(1)}, bf16[384,512]{1,0:T(8,128)(2,1)S(1)}, u32[]{:S(2)}, u32[]{:S(2)}) collective-permute-start(bf16[384,512]{1,0:T(8,128)(2,1)S(1)} %get-tuple-element.84), channel_id=1, source_target_pairs={{0,3},{1,0},{2,1},{3,2},{4,7},{5,4},{6,5},{7,6},{8,11},{9,8},{10,9... | collective-permute-start | bytes 1179656 | tf_op jit(solution)/shard_map/ppermute | solution.py:430
  97.1 2.3 %collective-permute-done.15 = bf16[384,512]{1,0:T(8,128)(2,1)S(1)} collective-permute-done((bf16[384,512]{1,0:T(8,128)(2,1)S(1)}, bf16[384,512]{1,0:T(8,128)(2,1)S(1)}, u32[]{:S(2)}, u32[]{:S(2)}) %collective-permute-start.15) | collective-permute-done | bytes 393248 | tf_op jit(solution)/shard_map/ppermute | solution.py:430
  99.4 0.1 add_convert_fusion.1
  99.5 0.1 collective-permute-start.16
  99.5 1.5 %collective-permute-start.17 = (bf16[384,512]{1,0:T(8,128)(2,1)S(1)}, bf16[384,512]{1,0:T(8,128)(2,1)S(1)}, u32[]{:S(2)}, u32[]{:S(2)}) collective-permute-start(bf16[384,512]{1,0:T(8,128)(2,1)S(1)} %get-tuple-element.88), channel_id=1, source_target_pairs={{0,1},{1,2},{2,3},{3,0},{4,5},{5,6},{6,7},{7,4},{8,9},{9,10},{10,1... | collective-permute-start | bytes 1179656 | tf_op jit(solution)/shard_map/ppermute | solution.py:430
  101.1 3.9 %collective-permute-done.18 = bf16[384,512]{1,0:T(8,128)(2,1)S(1)} collective-permute-done((bf16[384,512]{1,0:T(8,128)(2,1)S(1)}, bf16[384,512]{1,0:T(8,128)(2,1)S(1)}, u32[]{:S(2)}, u32[]{:S(2)}) %collective-permute-start.18) | collective-permute-done | bytes 393248 | tf_op jit(solution)/shard_map/ppermute | solution.py:430
  105.0 0.1 add_convert_fusion
  105.1 3.4 %collective-permute-start.19 = (bf16[384,512]{1,0:T(8,128)(2,1)S(1)}, bf16[384,512]{1,0:T(8,128)(2,1)S(1)}, u32[]{:S(2)}, u32[]{:S(2)}) collective-permute-start(bf16[384,512]{1,0:T(8,128)(2,1)S(1)} %add_convert_fusion), channel_id=1, source_target_pairs={{0,3},{1,0},{2,1},{3,2},{4,7},{5,4},{6,5},{7,6},{8,11},{9,8},{10,9... | collective-permute-start | bytes 1179656 | tf_op jit(solution)/shard_map/ppermute | solution.py:430
  108.5 4.9 %collective-permute-done.14 = bf16[384,512]{1,0:T(8,128)(2,1)S(1)} collective-permute-done((bf16[384,512]{1,0:T(8,128)(2,1)S(1)}, bf16[384,512]{1,0:T(8,128)(2,1)S(1)}, u32[]{:S(2)}, u32[]{:S(2)}) %collective-permute-start.14) | collective-permute-done | bytes 393248 | tf_op jit(solution)/shard_map/ppermute | solution.py:430
  113.4 0.1 convert_add_fusion.1
  113.5 5.7 %collective-permute-done.17 = bf16[384,512]{1,0:T(8,128)(2,1)S(1)} collective-permute-done((bf16[384,512]{1,0:T(8,128)(2,1)S(1)}, bf16[384,512]{1,0:T(8,128)(2,1)S(1)}, u32[]{:S(2)}, u32[]{:S(2)}) %collective-permute-start.17) | collective-permute-done | bytes 393248 | tf_op jit(solution)/shard_map/ppermute | solution.py:430
  119.2 1.1 collective-permute-done.19
  120.3 0.1 convert_add_fusion
  120.5 1.0 fusion
  (31 shorter events, 0.2 us)
Async XLA Ops:
  1.8 8.4 %collective-permute-start.3 = (bf16[3,128,256]{2,1,0:T(8,128)(2,1)}, bf16[3,128,256]{2,1,0:T(8,128)(2,1)S(1)}, u32[]{:S(2)}, u32[]{:S(2)}) collective-permute-start(bf16[3,128,256]{2,1,0:T(8,128)(2,1)} %pack.1), channel_id=1, source_target_pairs={{0,16},{8,24},{16,0},{24,8},{32,48},{40,56},{48,32},{56,40},{64,80... | collective-permute-start | bytes 589832 | tf_op jit(solution)/shard_map/ppermute | solution.py:452
  2.2 9.2 %copy-start.3 = (bf16[3,128,256]{2,1,0:T(8,128)(2,1)S(1)}, bf16[3,128,256]{2,1,0:T(8,128)(2,1)}, u32[]{:S(2)}) copy-start(bf16[3,128,256]{2,1,0:T(8,128)(2,1)} %pack.1) | copy-start | bytes 589828
  6.5 19.4 %copy-start.5 = (s32[3]{0:T(128)S(1)}, s32[3]{0:T(128)}, u32[]{:S(2)}) copy-start(s32[3]{0:T(128)} %constant.62.clone) | copy-start | bytes 40
  6.5 23.4 %copy-start = (bf16[384,1024]{1,0:T(8,128)(2,1)S(1)}, bf16[384,1024]{1,0:T(8,128)(2,1)}, u32[]{:S(2)}) copy-start(bf16[384,1024]{1,0:T(8,128)(2,1)} %q_ref.7) | copy-start | bytes 2359300
  6.5 23.4 %copy-start.1 = (s32[48,48]{1,0:T(8,128)S(1)}, s32[48,48]{1,0:T(8,128)}, u32[]{:S(2)}) copy-start(s32[48,48]{1,0:T(8,128)} %mask.7) | copy-start | bytes 27652
  6.5 23.4 %copy-start.2 = (bf16[384,8]{0,1:T(8,128)(2,1)S(1)}, bf16[384,8]{0,1:T(8,128)(2,1)}, u32[]{:S(2)}) copy-start(bf16[384,8]{0,1:T(8,128)(2,1)} %param.14) | copy-start | bytes 18436
  10.1 62.8 %collective-permute-start.11 = (bf16[8,512,512]{2,1,0:T(8,128)(2,1)}, bf16[8,512,512]{2,1,0:T(8,128)(2,1)}, u32[]{:S(2)}, u32[]{:S(2)}) collective-permute-start(bf16[8,512,512]{2,1,0:T(8,128)(2,1)} %cut.1), channel_id=1, source_target_pairs={{0,4},{1,5},{2,6},{3,7},{8,28},{9,29},{10,30},{11,31},{4,16},{5,17... | collective-permute-start | bytes 12582920 | tf_op jit(solution)/shard_map/ppermute | solution.py:455
  11.4 7.6 %collective-permute-start = (bf16[3,128,256]{2,1,0:T(8,128)(2,1)S(1)}, bf16[3,128,256]{2,1,0:T(8,128)(2,1)S(1)}, u32[]{:S(2)}, u32[]{:S(2)}) collective-permute-start(bf16[3,128,256]{2,1,0:T(8,128)(2,1)S(1)} %copy-done.3), channel_id=1, source_target_pairs={{0,32},{8,40},{16,48},{24,56},{32,64},{40,72},{48,80},{56,88},{64,... | collective-permute-start | bytes 589832 | tf_op jit(solution)/shard_map/ppermute | solution.py:289
  12.7 9.2 %collective-permute-start.1 = (bf16[3,128,256]{2,1,0:T(8,128)(2,1)S(1)}, bf16[3,128,256]{2,1,0:T(8,128)(2,1)S(1)}, u32[]{:S(2)}, u32[]{:S(2)}) collective-permute-start(bf16[3,128,256]{2,1,0:T(8,128)(2,1)S(1)} %copy-done.3), channel_id=1, source_target_pairs={{0,64},{8,72},{16,80},{24,88},{32,96},{40,104},{48,112},{56,120},{... | collective-permute-start | bytes 589832 | tf_op jit(solution)/shard_map/ppermute | solution.py:289
  14.0 11.7 %collective-permute-start.2 = (bf16[3,128,256]{2,1,0:T(8,128)(2,1)S(1)}, bf16[3,128,256]{2,1,0:T(8,128)(2,1)S(1)}, u32[]{:S(2)}, u32[]{:S(2)}) collective-permute-start(bf16[3,128,256]{2,1,0:T(8,128)(2,1)S(1)} %copy-done.3), channel_id=1, source_target_pairs={{0,96},{8,104},{16,112},{24,120},{1,97},{9,105},{17,113},{25,121},... | collective-permute-start | bytes 589832 | tf_op jit(solution)/shard_map/ppermute | solution.py:289
  25.8 4.1 %collective-permute-start.7 = (bf16[12,128,256]{2,1,0:T(8,128)(2,1)S(1)}, bf16[12,128,256]{2,1,0:T(8,128)(2,1)S(1)}, u32[]{:S(2)}, u32[]{:S(2)}) collective-permute-start(bf16[12,128,256]{2,1,0:T(8,128)(2,1)S(1)} %constant_dynamic-update-slice_fusion.mine), channel_id=1, source_target_pairs={{0,8},{8,0},{16,24},{24,16},{32,40},{40,32},{48,56},{56,48},{64,72... | collective-permute-start | bytes 2359304 | tf_op jit(solution)/shard_map/ppermute | solution.py:295
  26.0 16.7 %collective-permute-start.4 = (bf16[3,128,256]{2,1,0:T(8,128)(2,1)S(1)}, bf16[3,128,256]{2,1,0:T(8,128)(2,1)S(1)}, u32[]{:S(2)}, u32[]{:S(2)}) collective-permute-start(bf16[3,128,256]{2,1,0:T(8,128)(2,1)S(1)} %collective-permute-done.3), channel_id=1, source_target_pairs={{0,32},{8,40},{16,48},{24,56},{32,64},{40,72},{48,80},{56,88},{64,... | collective-permute-start | bytes 589832 | tf_op jit(solution)/shard_map/ppermute | solution.py:289
  27.3 15.4 %collective-permute-start.5 = (bf16[3,128,256]{2,1,0:T(8,128)(2,1)S(1)}, bf16[3,128,256]{2,1,0:T(8,128)(2,1)S(1)}, u32[]{:S(2)}, u32[]{:S(2)}) collective-permute-start(bf16[3,128,256]{2,1,0:T(8,128)(2,1)S(1)} %collective-permute-done.3), channel_id=1, source_target_pairs={{0,64},{8,72},{16,80},{24,88},{32,96},{40,104},{48,112},{56,120},{... | collective-permute-start | bytes 589832 | tf_op jit(solution)/shard_map/ppermute | solution.py:289
  28.6 14.1 %collective-permute-start.6 = (bf16[3,128,256]{2,1,0:T(8,128)(2,1)S(1)}, bf16[3,128,256]{2,1,0:T(8,128)(2,1)S(1)}, u32[]{:S(2)}, u32[]{:S(2)}) collective-permute-start(bf16[3,128,256]{2,1,0:T(8,128)(2,1)S(1)} %collective-permute-done.3), channel_id=1, source_target_pairs={{0,96},{8,104},{16,112},{24,120},{1,97},{9,105},{17,113},{25,121},... | collective-permute-start | bytes 589832 | tf_op jit(solution)/shard_map/ppermute | solution.py:289
  42.8 15.9 %copy-start.6 = (s32[3]{0:T(128)S(1)}, s32[3]{0:T(128)}, u32[]{:S(2)}) copy-start(s32[3]{0:T(128)} %constant.61.clone) | copy-start | bytes 40
  42.8 7.9 %collective-permute-start.8 = (bf16[12,128,256]{2,1,0:T(8,128)(2,1)S(1)}, bf16[12,128,256]{2,1,0:T(8,128)(2,1)S(1)}, u32[]{:S(2)}, u32[]{:S(2)}) collective-permute-start(bf16[12,128,256]{2,1,0:T(8,128)(2,1)S(1)} %constant_dynamic-update-slice_fusion.4.mine), channel_id=1, source_target_pairs={{0,8},{8,0},{16,24},{24,16},{32,40},{40,32},{48,56},{56,48},{64,72... | collective-permute-start | bytes 2359304 | tf_op jit(solution)/shard_map/ppermute | solution.py:295
  57.7 9.2 %collective-permute-start.9 = (bf16[128,1024]{1,0:T(8,128)(2,1)S(1)}, bf16[128,1024]{1,0:T(8,128)(2,1)S(1)}, u32[]{:S(2)}, u32[]{:S(2)}) collective-permute-start(bf16[128,1024]{1,0:T(8,128)(2,1)S(1)} %attend_second.3.refs_0_), channel_id=1, source_target_pairs={{0,4},{1,5},{2,6},{3,7},{4,0},{5,1},{6,2},{7,3},{8,12},{9,13},{10,... | collective-permute-start | bytes 786440 | tf_op jit(solution)/shard_map/ppermute | solution.py:468
  65.6 7.3 %collective-permute-start.10 = (bf16[128,1024]{1,0:T(8,128)(2,1)S(1)}, bf16[128,1024]{1,0:T(8,128)(2,1)S(1)}, u32[]{:S(2)}, u32[]{:S(2)}) collective-permute-start(bf16[128,1024]{1,0:T(8,128)(2,1)S(1)} %attend_second.4.refs_1_), channel_id=1, source_target_pairs={{0,4},{1,5},{2,6},{3,7},{4,0},{5,1},{6,2},{7,3},{8,12},{9,13},{10,... | collective-permute-start | bytes 786440 | tf_op jit(solution)/shard_map/ppermute | solution.py:468
  73.0 8.8 %collective-permute-start.13 = (bf16[8,512,512]{2,1,0:T(8,128)(2,1)}, bf16[8,512,512]{2,1,0:T(8,128)(2,1)S(1)}, u32[]{:S(2)}, u32[]{:S(2)}) collective-permute-start(bf16[8,512,512]{2,1,0:T(8,128)(2,1)} %collective-permute-done.11.refs_4_), channel_id=1, source_target_pairs={{0,8},{8,0},{16,24},{24,16},{32,40},{40,32},{48,56},{56,48},{64,72... | collective-permute-start | bytes 12582920 | tf_op jit(solution)/shard_map/ppermute | solution.py:473
  73.1 8.7 %collective-permute-start.12 = (bf16[128,1024]{1,0:T(8,128)(2,1)S(1)}, bf16[128,1024]{1,0:T(8,128)(2,1)S(1)}, u32[]{:S(2)}, u32[]{:S(2)}) collective-permute-start(bf16[128,1024]{1,0:T(8,128)(2,1)S(1)} %attend_second.5.refs_2_), channel_id=1, source_target_pairs={{0,4},{1,5},{2,6},{3,7},{4,0},{5,1},{6,2},{7,3},{8,12},{9,13},{10,... | collective-permute-start | bytes 786440 | tf_op jit(solution)/shard_map/ppermute | solution.py:468
  86.3 13.0 %collective-permute-start.15 = (bf16[384,512]{1,0:T(8,128)(2,1)S(1)}, bf16[384,512]{1,0:T(8,128)(2,1)S(1)}, u32[]{:S(2)}, u32[]{:S(2)}) collective-permute-start(bf16[384,512]{1,0:T(8,128)(2,1)S(1)} %get-tuple-element.86), channel_id=1, source_target_pairs={{0,1},{1,2},{2,3},{3,0},{4,5},{5,6},{6,7},{7,4},{8,9},{9,10},{10,1... | collective-permute-start | bytes 1179656 | tf_op jit(solution)/shard_map/ppermute | solution.py:430
  92.8 12.1 %collective-permute-start.18 = (bf16[384,512]{1,0:T(8,128)(2,1)S(1)}, bf16[384,512]{1,0:T(8,128)(2,1)S(1)}, u32[]{:S(2)}, u32[]{:S(2)}) collective-permute-start(bf16[384,512]{1,0:T(8,128)(2,1)S(1)} %get-tuple-element.90), channel_id=1, source_target_pairs={{0,3},{1,0},{2,1},{3,2},{4,7},{5,4},{6,5},{7,6},{8,11},{9,8},{10,9... | collective-permute-start | bytes 1179656 | tf_op jit(solution)/shard_map/ppermute | solution.py:430
  95.0 18.3 %collective-permute-start.14 = (bf16[384,512]{1,0:T(8,128)(2,1)S(1)}, bf16[384,512]{1,0:T(8,128)(2,1)S(1)}, u32[]{:S(2)}, u32[]{:S(2)}) collective-permute-start(bf16[384,512]{1,0:T(8,128)(2,1)S(1)} %get-tuple-element.84), channel_id=1, source_target_pairs={{0,3},{1,0},{2,1},{3,2},{4,7},{5,4},{6,5},{7,6},{8,11},{9,8},{10,9... | collective-permute-start | bytes 1179656 | tf_op jit(solution)/shard_map/ppermute | solution.py:430
  99.5 13.9 %collective-permute-start.16 = (bf16[384,512]{1,0:T(8,128)(2,1)S(1)}, bf16[384,512]{1,0:T(8,128)(2,1)S(1)}, u32[]{:S(2)}, u32[]{:S(2)}) collective-permute-start(bf16[384,512]{1,0:T(8,128)(2,1)S(1)} %add_convert_fusion.1), channel_id=1, source_target_pairs={{0,1},{1,2},{2,3},{3,0},{4,5},{5,6},{6,7},{7,4},{8,9},{9,10},{10,1... | collective-permute-start | bytes 1179656 | tf_op jit(solution)/shard_map/ppermute | solution.py:430
  99.5 19.7 %collective-permute-start.17 = (bf16[384,512]{1,0:T(8,128)(2,1)S(1)}, bf16[384,512]{1,0:T(8,128)(2,1)S(1)}, u32[]{:S(2)}, u32[]{:S(2)}) collective-permute-start(bf16[384,512]{1,0:T(8,128)(2,1)S(1)} %get-tuple-element.88), channel_id=1, source_target_pairs={{0,1},{1,2},{2,3},{3,0},{4,5},{5,6},{6,7},{7,4},{8,9},{9,10},{10,1... | collective-permute-start | bytes 1179656 | tf_op jit(solution)/shard_map/ppermute | solution.py:430
  105.1 15.3 %collective-permute-start.19 = (bf16[384,512]{1,0:T(8,128)(2,1)S(1)}, bf16[384,512]{1,0:T(8,128)(2,1)S(1)}, u32[]{:S(2)}, u32[]{:S(2)}) collective-permute-start(bf16[384,512]{1,0:T(8,128)(2,1)S(1)} %add_convert_fusion), channel_id=1, source_target_pairs={{0,3},{1,0},{2,1},{3,2},{4,7},{5,4},{6,5},{7,6},{8,11},{9,8},{10,9... | collective-permute-start | bytes 1179656 | tf_op jit(solution)/shard_map/ppermute | solution.py:430
  113.4 7.1 %copy-start.4 = (f32[1024]{0:T(1024)S(1)}, f32[1024]{0:T(1024)}, u32[]{:S(2)}) copy-start(f32[1024]{0:T(1024)} %param.21) | copy-start | bytes 12292
